TPU v7x, 32 devices: a whole 2x2x4 slice. The times are simulated.
32 devices in a mesh: grp: 8 (over y, x, core), dir: 4 (over z).
Axes of the slice: x: 2, y: 2, z: 4, core: 2. Of those that a mesh axis runs over, the one named last changes fastest.
Arguments:
- currents: bfloat16 [256, 64, 256], P(('grp', 'dir')), may hold values from -6 to 6
- live_counts: int32 [256], P(('grp', 'dir')), may hold values from 32 to 128, as said below
- radiation: bfloat16 [1024, 2, 128], replicated, may hold values from -0.375 to 0.375
- sources: int32 [256, 189], P('grp'), may hold values from 0 to 255, as said below
- operator_ids: int32 [256, 189], P('grp'), may hold values from 0 to 315
- translators: bfloat16 [316, 2, 1024], P(None, None, 'dir'), may hold values from -0.4375 to 0.4375
- stencil: int32 [1024, 8], P('dir'), may hold values from 0 to 1023, as said below
- stencil_weights: bfloat16 [1024, 8], P('dir'), may hold values from -3 to 3
- receiving: bfloat16 [1024, 2, 128], replicated, may hold values from -0.125 to 0.125
Outputs:
- product: float32 [256, 64, 256], P(('grp', 'dir'))
Inputs may be any that keep to these rules, and one draw needn't show every extreme that they name: `live_counts`: some box holds all 128 basis functions. `sources`: every entry lies within 32 of its own box's index, and that distance is reached; entries of a list may repeat. `stencil`: each row names 8 distinct directions within 8 of the row's own direction, counted cyclically over 1024; the distance 8 is reached.
All inputs are finite; a program needn't handle non-finite values.
Results may differ from a plain program's by a relative error of at most 0.0054.
Values may be sent and summed in bfloat16 or wider, within the bound.
No kernel may reach another device: no remote copies, remote signals or barrier semaphores. Data moves between devices by JAX's collectives and lax.ppermute only.
A program may use at most 64 MiB of HBM per device.

v0:
```python
import jax
import jax.numpy as jnp
from jax import lax
from jax.sharding import PartitionSpec as P

UNK = 128
DIRS = 1024
RIM = 8


def extended_2(cells, sides, width, closed):
    for axis, dim in sides:
        count = lax.axis_size(axis)
        ends = count if closed else count - 1
        head = lax.slice_in_dim(cells, 0, width, axis=dim)
        tail = lax.slice_in_dim(cells, cells.shape[dim] - width, cells.shape[dim], axis=dim)
        cells = jnp.concatenate(
            [
                lax.ppermute(tail, axis, [(i, (i + 1) % count) for i in range(ends)]),
                cells,
                lax.ppermute(head, axis, [((i + 1) % count, i) for i in range(ends)]),
            ],
            axis=dim,
        )
    return cells


def mask_rows(values, live_counts):
    column = jnp.arange(values.shape[-1], dtype=jnp.int32) % UNK
    keep = column[None, None, :] < live_counts[:, None, None]
    return jnp.where(keep, values, jnp.zeros_like(values))


def radiation_block(table):
    real_part = table[:, 0, :]
    imag_part = table[:, 1, :]
    upper = jnp.concatenate([real_part, -imag_part], axis=1)
    lower = jnp.concatenate([imag_part, real_part], axis=1)
    return jnp.stack([upper, lower], axis=1)


def receive_block(table):
    real_part = table[:, 0, :]
    imag_part = table[:, 1, :]
    upper = jnp.concatenate([real_part, imag_part], axis=1)
    lower = jnp.concatenate([-imag_part, real_part], axis=1)
    return jnp.stack([upper, lower], axis=1)


def radiate_rows(table_block, box_rows):
    result = jnp.einsum("kcv,brv->kbcr", table_block, box_rows, preferred_element_type=jnp.float32)
    return result.reshape(table_block.shape[0], box_rows.shape[0], 2 * box_rows.shape[1]).astype(
        jnp.bfloat16
    )


def body(
    currents,
    live_counts,
    radiation,
    sources,
    operator_ids,
    translators,
    stencil,
    stencil_weights,
    receiving,
):
    dir_index = lax.axis_index("dir")
    slice_dirs = translators.shape[2]
    kind_count = translators.shape[0]
    masked = mask_rows(currents, live_counts)
    forward = radiation_block(radiation)
    own_forward = lax.dynamic_slice_in_dim(forward, dir_index * slice_dirs, slice_dirs, 0)
    pattern = radiate_rows(own_forward, lax.all_gather(masked, "dir", axis=0, tiled=True))
    group_boxes = pattern.shape[1]
    window_width = 3 * group_boxes
    incid_count = pattern.shape[2] // 2
    extended = extended_2(pattern, (("grp", 1),), group_boxes, False)
    first_box = (lax.axis_index("grp") - 1) * group_boxes
    local_sources = sources - first_box
    window_ids = jnp.arange(window_width, dtype=jnp.int32)
    kind_ids = jnp.arange(kind_count, dtype=jnp.int32)
    flat_table = translators.reshape(kind_count, 2 * slice_dirs)
    block_boxes = 8
    block_count = group_boxes // block_boxes

    def translate_block(block_id, result):
        offset = block_id * block_boxes
        block_rows = lax.dynamic_slice_in_dim(local_sources, offset, block_boxes, 0)
        block_kinds = lax.dynamic_slice_in_dim(operator_ids, offset, block_boxes, 0)
        kind_hits = (block_kinds[:, :, None] == kind_ids[None, None, :]).astype(jnp.bfloat16)
        picked = jnp.einsum(
            "bjo,om->bjm", kind_hits, flat_table, preferred_element_type=jnp.float32
        ).astype(jnp.bfloat16)
        picked = picked.reshape(block_boxes, block_rows.shape[1], 2, slice_dirs)
        selector = (block_rows[:, :, None] == window_ids[None, None, :]).astype(jnp.bfloat16)
        matrix = jnp.einsum(
            "bjs,bjck->kcbs", selector, picked, preferred_element_type=jnp.float32
        ).astype(jnp.bfloat16)
        matrix = matrix.reshape(slice_dirs, 2 * block_boxes, window_width)
        applied = lax.dot_general(
            matrix, extended, (((2,), (1,)), ((0,), (0,))), preferred_element_type=jnp.float32
        )
        applied = applied.reshape(slice_dirs, 2, block_boxes, 2, incid_count)
        real_part = applied[:, 0, :, 0] - applied[:, 1, :, 1]
        imag_part = applied[:, 0, :, 1] + applied[:, 1, :, 0]
        block_field = jnp.concatenate([real_part, imag_part], axis=-1).astype(jnp.bfloat16)
        return lax.dynamic_update_slice_in_dim(result, block_field, offset, 1)

    translated = lax.fori_loop(
        0, block_count, translate_block, jnp.zeros(pattern.shape, jnp.bfloat16)
    )
    backward = receive_block(receiving)
    near_dirs = extended_2(translated, (("dir", 0),), RIM, True)
    own_dirs = dir_index * slice_dirs + jnp.arange(slice_dirs, dtype=jnp.int32)
    distance = (stencil - own_dirs[:, None]) % DIRS
    distance = jnp.where(distance > DIRS // 2, distance - DIRS, distance)
    position = jnp.arange(slice_dirs, dtype=jnp.int32)[:, None] + RIM + distance
    near_ids = jnp.arange(slice_dirs + 2 * RIM, dtype=jnp.int32)
    matches = position[:, :, None] == near_ids[None, None, :]
    spread_weights = jnp.where(matches, stencil_weights.astype(jnp.float32)[:, :, None], 0.0)
    interpolation = jnp.sum(spread_weights, axis=1).astype(jnp.bfloat16)
    near_flat = near_dirs.reshape(slice_dirs + 2 * RIM, group_boxes * 2 * incid_count)
    filtered = jnp.dot(interpolation, near_flat, preferred_element_type=jnp.float32).astype(
        jnp.bfloat16
    )
    split_field = filtered.reshape(slice_dirs, group_boxes, 2, incid_count)
    own_backward = lax.dynamic_slice_in_dim(backward, dir_index * slice_dirs, slice_dirs, 0)
    summed = lax.psum_scatter(
        jnp.einsum("kbcr,kcv->brv", split_field, own_backward, preferred_element_type=jnp.float32),
        "dir",
        scatter_dimension=0,
        tiled=True,
    )
    return mask_rows(summed, live_counts)


def solution(mesh):
    placed = (
        P(("grp", "dir"), None, None),
        P(("grp", "dir")),
        P(),
        P("grp", None),
        P("grp", None),
        P(None, None, "dir"),
        P("dir", None),
        P("dir", None),
        P(),
    )
    return jax.shard_map(
        body, mesh=mesh, in_specs=placed, out_specs=P(("grp", "dir"), None, None), check_vma=False
    )
```

profile of v0, /device:TPU:2, one launch (start us, length us, event | category | flops | bytes accessed | tf_op | source)
XLA Modules:
  0.0 231.5 jit_solution(17272915505784648923)
XLA Ops:
  9.6 2.2 fusion.42
  12.0 26.9 %all-gather.2.cloned.1.call-done = bf16[32,64,256]{2,1,0:T(8,128)(2,1)} async-done(((bf16[8,64,256]{2,1,0:T(8,128)(2,1)}), bf16[32,64,256]{2,1,0:T(8,128)(2,1)}) %all-gather.2.cloned.1.call-update) | async-done | bytes 1048592 | tf_op jit(solution)/shard_map/all_gather | solution.py:74
  38.9 2.0 convolution_convert_fusion.1
  40.9 3.1 %copy.72 = bf16[256,32,128]{2,1,0:T(8,128)(2,1)} copy(bf16[256,32,128]{0,2,1:T(8,128)(2,1)S(1)} %bitcast.104) | data formatting | bytes 4194304 | tf_op jit(solution)/shard_map/convert_element_type | solution.py:52
  46.0 3.6 %collective-permute-start.1 = (bf16[256,32,128]{2,1,0:T(8,128)(2,1)}, bf16[256,32,128]{2,1,0:T(8,128)(2,1)}, u32[]{:S(2)}, u32[]{:S(2)}) collective-permute-start(bf16[256,32,128]{2,1,0:T(8,128)(2,1)} %copy.72), channel_id=1, source_target_pairs={{4,0},{8,4},{12,8},{16,12},{20,16},{24,20},{28,24},{5,1},{9,5},{13... | collective-permute-start | bytes 6291464 | tf_op jit(solution)/shard_map/ppermute | solution.py:21
  53.4 18.3 %collective-permute-done = bf16[256,32,128]{2,1,0:T(8,128)(2,1)} collective-permute-done((bf16[256,32,128]{2,1,0:T(8,128)(2,1)}, bf16[256,32,128]{2,1,0:T(8,128)(2,1)}, u32[]{:S(2)}, u32[]{:S(2)}) %collective-permute-start) | collective-permute-done | bytes 2097184 | tf_op jit(solution)/shard_map/ppermute | solution.py:19
  71.7 21.5 %collective-permute-done.1 = bf16[256,32,128]{2,1,0:T(8,128)(2,1)} collective-permute-done((bf16[256,32,128]{2,1,0:T(8,128)(2,1)}, bf16[256,32,128]{2,1,0:T(8,128)(2,1)}, u32[]{:S(2)}, u32[]{:S(2)}) %collective-permute-start.1) | collective-permute-done | bytes 2097184 | tf_op jit(solution)/shard_map/ppermute | solution.py:21
  93.2 5.4 %pad_maximum_fusion = bf16[256,96,128]{2,1,0:T(8,128)(2,1)} fusion(bf16[256,32,128]{2,1,0:T(8,128)(2,1)} %collective-permute-done.1, bf16[256,32,128]{2,1,0:T(8,128)(2,1)S(1)} %copy-done, bf16[256,32,128]{2,1,0:T(8,128)(2,1)} %collective-permute-done), kind=kLoop, calls=%fused_computation.25 | loop fusion | flops 18874368 | bytes 12582912 | tf_op jit(solution)/shard_map/concatenate | solution.py:17
  100.2 54.7 %while.14 = (s32[]{:T(128)}, bf16[256,32,128]{0,2,1:T(8,128)(2,1)}, s32[32,189]{1,0:T(8,128)}, bf16[316,512]{1,0:T(8,128)(2,1)}, s32[32,189]{1,0:T(8,128)S(1)}, ...) while((s32[]{:T(128)}, bf16[256,32,128]{0,2,1:T(8,128)(2,1)}, ...), condition=%wide.region_2.3_spmd.clone, body=%wide.region_1.2_spmd.clone.sunk | while | flops 741921152 | bytes 27718292 | solution.py:110
  100.9 2.0 fusion.64
  105.0 5.9 %fusion.66 = f32[256,16,128]{2,1,0:T(8,128)} fusion(bf16[256,16,96]{2,1,0:T(8,128)(2,1)S(1)} %copy.114, bf16[256,96,128]{2,1,0:T(8,128)(2,1)} %get-tuple-element.256), kind=kOutput, calls=%fused_computation.72.clone.1 | convolution fusion | flops 100663296 | bytes 9175040 | tf_op jit(solution)/shard_map/while/body/eval_jaxpr/dot_general | solution.py:101
  114.6 2.0 fusion.64
  118.7 5.9 %fusion.66 = f32[256,16,128]{2,1,0:T(8,128)} fusion(bf16[256,16,96]{2,1,0:T(8,128)(2,1)S(1)} %copy.114, bf16[256,96,128]{2,1,0:T(8,128)(2,1)} %get-tuple-element.256), kind=kOutput, calls=%fused_computation.72.clone.1 | convolution fusion | flops 100663296 | bytes 9175040 | tf_op jit(solution)/shard_map/while/body/eval_jaxpr/dot_general | solution.py:101
  128.2 2.0 fusion.64
  132.3 5.9 %fusion.66 = f32[256,16,128]{2,1,0:T(8,128)} fusion(bf16[256,16,96]{2,1,0:T(8,128)(2,1)S(1)} %copy.114, bf16[256,96,128]{2,1,0:T(8,128)(2,1)} %get-tuple-element.256), kind=kOutput, calls=%fused_computation.72.clone.1 | convolution fusion | flops 100663296 | bytes 9175040 | tf_op jit(solution)/shard_map/while/body/eval_jaxpr/dot_general | solution.py:101
  141.9 2.0 fusion.64
  146.0 5.9 %fusion.66 = f32[256,16,128]{2,1,0:T(8,128)} fusion(bf16[256,16,96]{2,1,0:T(8,128)(2,1)S(1)} %copy.114, bf16[256,96,128]{2,1,0:T(8,128)(2,1)} %get-tuple-element.256), kind=kOutput, calls=%fused_computation.72.clone.1 | convolution fusion | flops 100663296 | bytes 9175040 | tf_op jit(solution)/shard_map/while/body/eval_jaxpr/dot_general | solution.py:101
  154.9 3.4 %copy.75 = bf16[256,32,128]{2,1,0:T(8,128)(2,1)S(1)} copy(bf16[256,32,128]{0,2,1:T(8,128)(2,1)} %get-tuple-element.144) | data formatting | bytes 4194304 | tf_op jit(solution)/shard_map/while | solution.py:110
  160.4 2.4 %collective-permute-start.3 = (bf16[8,32,128]{2,1,0:T(8,128)(2,1)}, bf16[8,32,128]{2,1,0:T(8,128)(2,1)}, u32[]{:S(2)}, u32[]{:S(2)}) collective-permute-start(bf16[8,32,128]{2,1,0:T(8,128)(2,1)} %get-tuple-element.179), channel_id=1, source_target_pairs={{1,0},{2,1},{3,2},{0,3},{5,4},{6,5},{7,6},{4,7},{9,8},{10,9},{11,1... | collective-permute-start | bytes 196616 | tf_op jit(solution)/shard_map/ppermute | solution.py:21
  168.2 3.6 %pad_maximum_fusion.1 = bf16[272,32,128]{0,2,1:T(8,128)(2,1)S(1)} fusion(bf16[8,32,128]{0,2,1:T(8,128)(2,1)S(1)} %copy.78, bf16[256,32,128]{0,2,1:T(8,128)(2,1)} %get-tuple-element.144, bf16[8,32,128]{0,2,1:T(8,128)(2,1)S(1)} %copy.77), kind=kLoop, calls=%fused_computation.27 | loop fusion | flops 6684672 | bytes 4456448 | tf_op jit(solution)/shard_map/concatenate | solution.py:17
  171.8 2.6 %convolution_convert_fusion = bf16[256,4096]{1,0:T(8,128)(2,1)} fusion(bf16[272,4096]{0,1:T(8,128)(2,1)S(1)} %bitcast.102, bf16[256,272]{0,1:T(8,128)(2,1)S(1)} %select_reduce_fusion), kind=kOutput, calls=%fused_computation.26 | convolution fusion | flops 571473920 | bytes 4464640 | tf_op jit(solution)/shard_map/dot_general | solution.py:124
  174.4 3.3 %copy.79 = bf16[256,4096]{0,1:T(8,128)(2,1)S(1)} copy(bf16[256,4096]{1,0:T(8,128)(2,1)} %convolution_convert_fusion) | data formatting | bytes 4194304 | tf_op jit(solution)/shard_map/convert_element_type | solution.py:124
  177.7 2.0 convolution_bitcast_fusion
  179.8 43.0 %reduce-scatter.2.cloned.1.call-done = f32[8,64,256]{2,1,0:T(8,128)} async-done(((f32[32,64,256]{2,1,0:T(8,128)}), f32[8,64,256]{2,1,0:T(8,128)}) %reduce-scatter.2.cloned.1.call-update) | async-done | bytes 524304 | tf_op jit(solution)/shard_map/reduce_scatter | solution.py:129
  (96 shorter events, 42.6 us)
Async XLA Ops:
  6.5 32.4 %all-gather.2.cloned.1.call-start = ((), (), s32[]{:S(2)}) async-start(), calls=%async_computation.1 | async-start | bytes 1310720 | tf_op jit(solution)/shard_map/all_gather | solution.py:74
  7.3 0.6 copy-start.5
  9.6 213.2 %reduce-scatter.2.cloned.1.call-start = ((), (), s32[]{:S(2)}) async-start(), calls=%async_computation.2 | async-start | bytes 2621440 | tf_op jit(solution)/shard_map/reduce_scatter | solution.py:129
  40.9 8.7 %copy-start.2 = (bf16[316,2,256]{2,1,0:T(2,128)(2,1)S(1)}, bf16[316,2,256]{2,1,0:T(2,128)(2,1)}, u32[]{:S(2)}) copy-start(bf16[316,2,256]{2,1,0:T(2,128)(2,1)} %param.16) | copy-start | bytes 970756
  40.9 9.8 %copy-start.8 = (bf16[256,8]{0,1:T(8,128)(2,1)S(1)}, bf16[256,8]{0,1:T(8,128)(2,1)}, u32[]{:S(2)}) copy-start(bf16[256,8]{0,1:T(8,128)(2,1)} %param.18) | copy-start | bytes 12292
  40.9 9.8 %copy-start.1 = (bf16[1024,2,128]{2,1,0:T(2,128)(2,1)S(1)}, bf16[1024,2,128]{2,1,0:T(2,128)(2,1)}, u32[]{:S(2)}) copy-start(bf16[1024,2,128]{2,1,0:T(2,128)(2,1)} %param.19) | copy-start | bytes 1572868
  44.1 27.7 %collective-permute-start = (bf16[256,32,128]{2,1,0:T(8,128)(2,1)}, bf16[256,32,128]{2,1,0:T(8,128)(2,1)}, u32[]{:S(2)}, u32[]{:S(2)}) collective-permute-start(bf16[256,32,128]{2,1,0:T(8,128)(2,1)} %copy.72), channel_id=1, source_target_pairs={{0,4},{4,8},{8,12},{12,16},{16,20},{20,24},{24,28},{1,5},{5,9},{9,... | collective-permute-start | bytes 6291464 | tf_op jit(solution)/shard_map/ppermute | solution.py:19
  46.0 47.2 %collective-permute-start.1 = (bf16[256,32,128]{2,1,0:T(8,128)(2,1)}, bf16[256,32,128]{2,1,0:T(8,128)(2,1)}, u32[]{:S(2)}, u32[]{:S(2)}) collective-permute-start(bf16[256,32,128]{2,1,0:T(8,128)(2,1)} %copy.72), channel_id=1, source_target_pairs={{4,0},{8,4},{12,8},{16,12},{20,16},{24,20},{28,24},{5,1},{9,5},{13... | collective-permute-start | bytes 6291464 | tf_op jit(solution)/shard_map/ppermute | solution.py:21
  49.6 1.9 copy-start.7
  50.7 42.5 %copy-start = (bf16[256,32,128]{2,1,0:T(8,128)(2,1)S(1)}, bf16[256,32,128]{2,1,0:T(8,128)(2,1)}, u32[]{:S(2)}) copy-start(bf16[256,32,128]{2,1,0:T(8,128)(2,1)} %copy.72) | copy-start | bytes 6291460
  100.2 0.7 copy-start.3
  112.9 1.0 copy-start.4
  113.8 0.7 copy-start.3
  126.5 1.0 copy-start.4
  127.5 0.7 copy-start.3
  140.2 1.0 copy-start.4
  141.2 0.7 copy-start.3
  153.9 1.0 copy-start.4
  159.0 6.2 %collective-permute-start.2 = (bf16[8,32,128]{2,1,0:T(8,128)(2,1)S(1)}, bf16[8,32,128]{2,1,0:T(8,128)(2,1)S(1)}, u32[]{:S(2)}, u32[]{:S(2)}) collective-permute-start(bf16[8,32,128]{2,1,0:T(8,128)(2,1)S(1)} %get-tuple-element.178), channel_id=1, source_target_pairs={{0,1},{1,2},{2,3},{3,0},{4,5},{5,6},{6,7},{7,4},{8,9},{9,10},{10,1... | collective-permute-start | bytes 196616 | tf_op jit(solution)/shard_map/ppermute | solution.py:19
  160.4 6.4 %collective-permute-start.3 = (bf16[8,32,128]{2,1,0:T(8,128)(2,1)}, bf16[8,32,128]{2,1,0:T(8,128)(2,1)}, u32[]{:S(2)}, u32[]{:S(2)}) collective-permute-start(bf16[8,32,128]{2,1,0:T(8,128)(2,1)} %get-tuple-element.179), channel_id=1, source_target_pairs={{1,0},{2,1},{3,2},{0,3},{5,4},{6,5},{7,6},{4,7},{9,8},{10,9},{11,1... | collective-permute-start | bytes 196616 | tf_op jit(solution)/shard_map/ppermute | solution.py:21
  179.7 43.0 %copy-start.6 = (pred[8,256]{1,0:T(8,128)(4,1)S(1)}, pred[8,256]{1,0:T(8,128)(4,1)}, u32[]{:S(2)}) copy-start(pred[8,256]{1,0:T(8,128)(4,1)} %copy-done.5) | copy-start | bytes 6148
Sparse Core Ops, SparseCore 0:
  9.7 29.1 all-gather.1
  179.9 42.8 reduce-scatter.1
where the time goes:
time: 234 us; the launch traced here: 231 us
  waiting for transfers between devices  112 us (48%)
  matrix products  40.1 us (17%)
  local copies, waits for them, and re-layouts  35.6 us (15%)
  other arithmetic  20.3 us (9%)
  between operations  13.6 us (6%)
  starting transfers between devices  9.42 us (4%)
    reduce_scatter x1, waiting for transfers between devices, body(): lax.psum_scatter(jnp.einsum('kbcr,kcv->brv', split_field, own_backward, p...  43 us
    all_gather x1, waiting for transfers between devices, body(): lax.all_gather(masked, 'dir', axis=0, tiled=True)  26.9 us
    dot_general x4, matrix products, translate_block(): lax.dot_general(matrix, extended, (((2,), (1,)), ((0,), (0,))), preferred...  23.7 us
    ppermute x2, waiting for transfers between devices, extended_2(): lax.ppermute(head, axis, [((i + 1) % count, i) for i in range(ends)])  22.7 us
    ppermute x2, waiting for transfers between devices, extended_2(): lax.ppermute(tail, axis, [(i, (i + 1) % count) for i in range(ends)])  19.5 us
    concatenate x2, other arithmetic, extended_2(): jnp.concatenate([lax.ppermute(tail, axis, [(i, (i + 1) % count) for i in...  8.97 us
    dot_general x4, matrix products, translate_block(): jnp.einsum('bjo,om->bjm', kind_hits, flat_table, preferred_element_type=j...  7.99 us
    dot_general x4, local copies, waits for them, and re-layouts, translate_block(): lax.dot_general(matrix, extended, (((2,), (1,)), ((0,), (0,))), preferred...  7.72 us
  transfers between devices with their start and end apart: 6, of which 6 were waited for; matrix products, arithmetic and copies ran while one was open for 3% of the time, Pallas kernels for 0%

commit v1 on v0

v1 whole, which is shorter than its diff:
```python
import functools

import jax
import jax.numpy as jnp
from jax import lax
from jax.experimental import pallas as pl
from jax.experimental.pallas import tpu as pltpu
from jax.sharding import PartitionSpec as P

RIM = 8
LANES = 128
BF = jnp.bfloat16
F32 = jnp.float32
NT = (((1,), (1,)), ((), ()))
TN = (((0,), (0,)), ((), ()))
NN = (((1,), (0,)), ((), ()))
VMEM = pl.BlockSpec(memory_space=pltpu.VMEM)


def round_up(value, unit):
    return -(-value // unit) * unit


def dot(a, b, dims):
    return lax.dot_general(a, b, dims, preferred_element_type=F32)


def cost(flops, nbytes):
    return pl.CostEstimate(flops=int(flops), bytes_accessed=int(nbytes), transcendentals=0)


def tables_kernel(
    src_ref, op_ref, table_ref, offset_ref, weight_ref, receive_ref, matrix_ref, folded_ref, wide
):
    boxes, width = src_ref.shape
    dirs, rows, window = matrix_ref.shape
    kinds = table_ref.shape[1]

    def one_box(box, carry):
        src = src_ref[pl.ds(box, 1), :]
        ops = op_ref[pl.ds(box, 1), :]
        hit_kind = (lax.broadcasted_iota(jnp.int32, (kinds, width), 0) == ops).astype(F32).astype(BF)
        hit_src = (lax.broadcasted_iota(jnp.int32, (window, width), 0) == src).astype(F32).astype(BF)
        counts = dot(hit_kind, hit_src, NT).astype(BF)
        entries = dot(table_ref[...], counts, NN)
        for c in range(window // LANES):
            part = entries[:, c * LANES : (c + 1) * LANES]
            wide[c, pl.ds(box, dirs, stride=rows), :] = part[:dirs]
            wide[c, pl.ds(box + boxes, dirs, stride=rows), :] = part[dirs:]
        return carry

    lax.fori_loop(0, boxes, one_box, 0)

    def narrow(step, carry):
        for i in range(4):
            k = step * 4 + i
            for c in range(window // LANES):
                part = wide[c, pl.ds(pl.multiple_of(k * rows, 8), rows), :]
                matrix_ref[k, :, c * LANES : (c + 1) * LANES] = part.astype(BF)
        return carry

    lax.fori_loop(0, dirs // 4, narrow, 0)

    extent = offset_ref.shape[1]
    own = lax.broadcasted_iota(jnp.int32, (dirs, extent), 0)
    spread = jnp.zeros((dirs, extent), F32)
    for p in range(offset_ref.shape[0]):
        spread += jnp.where(own == offset_ref[p : p + 1, :], weight_ref[p : p + 1, :], 0.0)
    folded_ref[...] = dot(spread.astype(BF), receive_ref[...], NN).astype(BF)


def build_tables(src, ops, table, offsets, weights, receive, dirs, window):
    boxes = src.shape[0]
    return pl.pallas_call(
        tables_kernel,
        out_shape=(
            jax.ShapeDtypeStruct((dirs, 2 * boxes, window), BF),
            jax.ShapeDtypeStruct((dirs, receive.shape[1]), BF),
        ),
        in_specs=[VMEM] * 6,
        out_specs=(VMEM, VMEM),
        scratch_shapes=[pltpu.VMEM((window // LANES, dirs * 2 * boxes, LANES), F32)],
        cost_estimate=cost(2 * boxes * 2 * dirs * 320 * window * 4, 8 << 20),
        name="tables",
    )(src, ops, table, offsets, weights, receive)


def rotated(box):
    half = box.shape[1] // 2
    re, im = box[:, :half], box[:, half:]
    return jnp.concatenate(
        [jnp.concatenate([re, -im], axis=1), jnp.concatenate([im, re], axis=1)], axis=0
    )


def radiate(forward_ref, box_refs, out, stride):
    dirs = forward_ref.shape[0]
    first = 0
    for ref in box_refs:
        count = ref.shape[0]
        width = 2 * ref.shape[1]

        def pair(step, carry, ref=ref, first=first, width=width):
            both = jnp.concatenate([rotated(ref[2 * step]), rotated(ref[2 * step + 1])], axis=0)
            field = dot(forward_ref[...], both, NT)
            at = first + 2 * step
            out[pl.ds(at, dirs, stride=stride), :] = field[:, :width]
            out[pl.ds(at + 1, dirs, stride=stride), :] = field[:, width:]
            return carry

        lax.fori_loop(0, count // 2, pair, 0)
        first += count


def pattern_kernel(count, forward_ref, *refs):
    box_refs, pattern_ref, wide = refs[:count], refs[count], refs[count + 1]
    dirs, boxes, _ = pattern_ref.shape
    radiate(forward_ref, box_refs, wide, boxes)

    def narrow(step, carry):
        for i in range(4):
            k = step * 4 + i
            pattern_ref[k] = wide[pl.ds(pl.multiple_of(k * boxes, 8), boxes), :].astype(BF)
        return carry

    lax.fori_loop(0, dirs // 4, narrow, 0)


def own_pattern(forward, shards):
    dirs = forward.shape[0]
    boxes = sum(s.shape[0] for s in shards)
    width = 2 * shards[0].shape[1]
    return pl.pallas_call(
        functools.partial(pattern_kernel, len(shards)),
        out_shape=jax.ShapeDtypeStruct((dirs, boxes, width), BF),
        in_specs=[VMEM] * (1 + len(shards)),
        out_specs=VMEM,
        scratch_shapes=[pltpu.VMEM((dirs * boxes, width), F32)],
        cost_estimate=cost(2 * dirs * boxes * width * 256, 4 << 20),
        name="pattern",
    )(forward, *shards)


def field_kernel(count, forward_ref, matrix_ref, folded_ref, own_ref, *refs):
    box_refs = refs[: 2 * count]
    out_refs = refs[2 * count : 3 * count]
    near, moved = refs[3 * count :]
    dirs, own_boxes, width = own_ref.shape
    near_boxes = 2 * own_boxes
    boxes = matrix_ref.shape[1] // 2
    half = width // 2
    radiate(forward_ref, box_refs, near, near_boxes)
    lane = lax.broadcasted_iota(jnp.int32, (boxes, width), 1)
    sign = jnp.where(lane < half, -1.0, 1.0).astype(F32)

    def translate(step, carry):
        for i in range(4):
            k = step * 4 + i
            around = near[pl.ds(pl.multiple_of(k * near_boxes, 8), near_boxes), :].astype(BF)
            fields = jnp.concatenate([own_ref[k], around], axis=0)
            both = dot(matrix_ref[k][:, : own_boxes + near_boxes], fields, NN)
            turned = pltpu.roll(both[boxes:], half, 1)
            moved[pl.ds(pl.multiple_of(k * boxes, 8), boxes), :] = both[:boxes] + sign * turned
        return carry

    lax.fori_loop(0, dirs // 4, translate, 0)

    per = boxes // count
    unk = folded_ref.shape[1] // 2
    for j, out_ref in enumerate(out_refs):

        def receive(i, carry, j=j, out_ref=out_ref):
            field = moved[pl.ds(j * per + i, dirs, stride=boxes), :].astype(BF)
            full = dot(field, folded_ref[...], TN)
            re = full[:half, :unk] - full[half:, unk:]
            im = full[:half, unk:] + full[half:, :unk]
            out_ref[i] = jnp.concatenate([re, im], axis=1).astype(out_ref.dtype)
            return carry

        lax.fori_loop(0, per, receive, 0)


def receive_field(forward, matrix, folded, own, left, right):
    count = len(left)
    dirs, own_boxes, width = own.shape
    per = matrix.shape[1] // 2 // count
    kinds = [F32] + [BF] * (count - 1)
    return pl.pallas_call(
        functools.partial(field_kernel, count),
        out_shape=tuple(
            jax.ShapeDtypeStruct((per, width // 2, folded.shape[1]), kind) for kind in kinds
        ),
        in_specs=[VMEM] * (4 + 2 * count),
        out_specs=(VMEM,) * count,
        scratch_shapes=[
            pltpu.VMEM((dirs * 2 * own_boxes, width), F32),
            pltpu.VMEM((dirs * matrix.shape[1] // 2, width), F32),
        ],
        cost_estimate=cost(4 << 30, 16 << 20),
        name="field",
    )(forward, matrix, folded, own, *left, *right)


def mask_rows(values, live_counts):
    column = jnp.arange(values.shape[-1], dtype=jnp.int32) % (values.shape[-1] // 2)
    keep = column[None, None, :] < live_counts[:, None, None]
    return jnp.where(keep, values, jnp.zeros_like(values))


def body(
    currents,
    live_counts,
    radiation,
    sources,
    operator_ids,
    translators,
    stencil,
    stencil_weights,
    receiving,
):
    dir_index = lax.axis_index("dir")
    n_dir, n_grp = lax.axis_size("dir"), lax.axis_size("grp")
    kinds, _, dirs = translators.shape
    all_dirs = radiation.shape[0]
    per = currents.shape[0]
    boxes = n_dir * per
    window = round_up(3 * boxes, 128)

    def turn(values, step):
        return lax.ppermute(values, "dir", [(i, (i + step) % n_dir) for i in range(n_dir)])

    def shift(values, step):
        pairs = [(i, i + step) for i in range(n_grp) if 0 <= i + step < n_grp]
        return lax.ppermute(values, "grp", pairs)

    masked = mask_rows(currents, live_counts)
    shards = [masked] + [turn(masked, j) for j in range(1, n_dir)]
    left = [shift(s, 1) for s in shards]
    right = [shift(s, -1) for s in shards]

    local = sources - (lax.axis_index("grp") - 1) * boxes
    group, inside = local // boxes, local % boxes
    slot = (dir_index - inside // per) % n_dir
    place = jnp.where(group == 1, 0, jnp.where(group == 0, 1, 2))
    place = place * boxes + slot * per + inside % per
    pad = round_up(sources.shape[1], 128) - sources.shape[1]
    lists = jnp.stack([place, operator_ids])
    lists = jnp.pad(lists, ((0, 0), (0, 0), (0, pad)), constant_values=-1)
    lists = lax.dynamic_slice_in_dim(
        jnp.concatenate([lists, lists], axis=1), dir_index * per, boxes, 1
    )
    table = translators.transpose(1, 2, 0).reshape(2 * dirs, kinds)
    table = jnp.pad(table, ((0, 0), (0, round_up(kinds, 64) - kinds)))

    own_dirs = dir_index * dirs + jnp.arange(dirs, dtype=jnp.int32)
    distance = (stencil - own_dirs[:, None]) % all_dirs
    distance = jnp.where(distance > all_dirs // 2, distance - all_dirs, distance)
    rows = jnp.concatenate([distance.astype(BF), stencil_weights], axis=1)
    rows = jnp.concatenate([turn(rows[-RIM:], 1), rows, turn(rows[:RIM], -1)], axis=0)
    extent = dirs + 2 * RIM
    fill = round_up(extent, 128) - extent
    points = stencil.shape[1]
    position = jnp.arange(extent, dtype=jnp.int32)[:, None] - RIM
    offsets = jnp.pad((position + rows[:, :points].astype(jnp.int32)).T, ((0, 0), (0, fill)))
    weights = jnp.pad(rows[:, points:].astype(F32).T, ((0, 0), (0, fill)))
    flat = receiving.reshape(all_dirs, -1)
    around = jnp.concatenate([flat[-RIM:], flat, flat[: RIM + fill]], axis=0)
    receive = lax.dynamic_slice_in_dim(around, dir_index * dirs, extent + fill, 0)
    forward = lax.dynamic_slice_in_dim(
        radiation.reshape(all_dirs, -1), dir_index * dirs, dirs, 0
    )

    matrix, folded = build_tables(
        lists[0], lists[1], table, offsets, weights, receive, dirs, window
    )
    own = own_pattern(forward, shards)
    parts = receive_field(forward, matrix, folded, own, left, right)
    total = parts[0]
    for j in range(1, n_dir):
        total = total + turn(parts[j], j).astype(F32)
    return mask_rows(total, live_counts)


def solution(mesh):
    placed = (
        P(("grp", "dir"), None, None),
        P(("grp", "dir")),
        P(),
        P("grp", None),
        P("grp", None),
        P(None, None, "dir"),
        P("dir", None),
        P("dir", None),
        P(),
    )
    return jax.shard_map(
        body, mesh=mesh, in_specs=placed, out_specs=P(("grp", "dir"), None, None), check_vma=False
    )
```

time: 234 us -> 161 us (0.69)
  the two profiles are of different devices: /device:TPU:2 before, /device:TPU:11 now
where the time goes in v1:
time: 161 us; the launch traced here: 160 us
  Pallas kernels  76.6 us (48%)
  starting transfers between devices  43.2 us (27%)
  waiting for transfers between devices  22.8 us (14%)
  other arithmetic  8.51 us (5%)
  local copies, waits for them, and re-layouts  8.29 us (5%)
    pallas_call x1, Pallas kernels, receive_field(): pl.pallas_call(functools.partial(field_kernel, count), out_shape=tuple((j...  42.4 us
    ppermute x8, starting transfers between devices, shift(): return lax.ppermute(values, 'grp', pairs)  25.8 us
    pallas_call x1, Pallas kernels, build_tables(): pl.pallas_call(tables_kernel, out_shape=(jax.ShapeDtypeStruct((dirs, 2 *...  24.7 us
    ppermute x8, waiting for transfers between devices, turn(): lax.ppermute(values, 'dir', [(i, (i + step) % n_dir) for i in range(n_dir)])  22.8 us
    ppermute x8, starting transfers between devices, turn(): lax.ppermute(values, 'dir', [(i, (i + step) % n_dir) for i in range(n_dir)])  17.4 us
    pallas_call x1, Pallas kernels, own_pattern(): pl.pallas_call(functools.partial(pattern_kernel, len(shards)), out_shape=...  9.48 us
    unnamed x33, local copies, waits for them, and re-layouts  4.09 us
  transfers between devices with their start and end apart: 16, of which 4 were waited for; matrix products, arithmetic and copies ran while one was open for 7% of the time, Pallas kernels for 21%

profile of v1, /device:TPU:11, one launch (start us, length us, event | category | flops | bytes accessed | tf_op | source)
XLA Modules:
  0.0 159.7 jit_solution(13718722774605588008)
XLA Ops:
  1.8 2.6 %collective-permute-start.9 = (bf16[8,64,256]{2,1,0:T(8,128)(2,1)S(1)}, bf16[8,64,256]{2,1,0:T(8,128)(2,1)S(1)}, u32[]{:S(2)}, u32[]{:S(2)}) collective-permute-start(bf16[8,64,256]{2,1,0:T(8,128)(2,1)S(1)} %broadcast_select_fusion.refs_0_), channel_id=1, source_target_pairs={{4,0},{8,4},{12,8},{16,12},{20,16},{24,20},{28,24},{5,1},{9,5},{13... | collective-permute-start | bytes 786440 | tf_op jit(solution)/shard_map/ppermute | solution.py:234
  4.4 3.9 %collective-permute-start.5 = (bf16[8,64,256]{2,1,0:T(8,128)(2,1)S(1)}, bf16[8,64,256]{2,1,0:T(8,128)(2,1)S(1)}, u32[]{:S(2)}, u32[]{:S(2)}) collective-permute-start(bf16[8,64,256]{2,1,0:T(8,128)(2,1)S(1)} %broadcast_select_fusion.refs_0_), channel_id=1, source_target_pairs={{0,4},{4,8},{8,12},{12,16},{16,20},{20,24},{24,28},{1,5},{5,9},{9,... | collective-permute-start | bytes 786440 | tf_op jit(solution)/shard_map/ppermute | solution.py:234
  10.0 1.3 collective-permute-start
  11.3 2.0 %collective-permute-start.1 = (bf16[8,16]{0,1:T(8,128)(2,1)S(1)}, bf16[8,16]{0,1:T(8,128)(2,1)S(1)}, u32[]{:S(2)}, u32[]{:S(2)}) collective-permute-start(bf16[8,16]{0,1:T(8,128)(2,1)S(1)} %get-tuple-element.20), channel_id=1, source_target_pairs={{0,3},{1,0},{2,1},{3,2},{4,7},{5,4},{6,5},{7,6},{8,11},{9,8},{10,9... | collective-permute-start | bytes 776 | tf_op jit(solution)/shard_map/ppermute | solution.py:230
  17.2 1.1 copy.20
  18.3 1.1 copy.19
  22.5 2.1 %collective-permute-start.3 = (bf16[8,64,256]{2,1,0:T(8,128)(2,1)S(1)}, bf16[8,64,256]{2,1,0:T(8,128)(2,1)S(1)}, u32[]{:S(2)}, u32[]{:S(2)}) collective-permute-start(bf16[8,64,256]{2,1,0:T(8,128)(2,1)S(1)} %broadcast_select_fusion.refs_0_), channel_id=1, source_target_pairs={{0,2},{1,3},{2,0},{3,1},{4,6},{5,7},{6,4},{7,5},{8,10},{9,11},{10,... | collective-permute-start | bytes 786440 | tf_op jit(solution)/shard_map/ppermute | solution.py:230
  24.6 2.4 %collective-permute-start.2 = (bf16[8,64,256]{2,1,0:T(8,128)(2,1)S(1)}, bf16[8,64,256]{2,1,0:T(8,128)(2,1)S(1)}, u32[]{:S(2)}, u32[]{:S(2)}) collective-permute-start(bf16[8,64,256]{2,1,0:T(8,128)(2,1)S(1)} %broadcast_select_fusion.refs_0_), channel_id=1, source_target_pairs={{0,1},{1,2},{2,3},{3,0},{4,5},{5,6},{6,7},{7,4},{8,9},{9,10},{10,1... | collective-permute-start | bytes 786440 | tf_op jit(solution)/shard_map/ppermute | solution.py:230
  27.7 1.9 %collective-permute-start.12 = (bf16[8,64,256]{2,1,0:T(8,128)(2,1)S(1)}, bf16[8,64,256]{2,1,0:T(8,128)(2,1)S(1)}, u32[]{:S(2)}, u32[]{:S(2)}) collective-permute-start(bf16[8,64,256]{2,1,0:T(8,128)(2,1)S(1)} %collective-permute-done.4.refs_3_), channel_id=1, source_target_pairs={{4,0},{8,4},{12,8},{16,12},{20,16},{24,20},{28,24},{5,1},{9,5},{13... | collective-permute-start | bytes 786440 | tf_op jit(solution)/shard_map/ppermute | solution.py:234
  30.2 4.5 %collective-permute-start.8 = (bf16[8,64,256]{2,1,0:T(8,128)(2,1)S(1)}, bf16[8,64,256]{2,1,0:T(8,128)(2,1)S(1)}, u32[]{:S(2)}, u32[]{:S(2)}) collective-permute-start(bf16[8,64,256]{2,1,0:T(8,128)(2,1)S(1)} %collective-permute-done.4.refs_3_), channel_id=1, source_target_pairs={{0,4},{4,8},{8,12},{12,16},{16,20},{20,24},{24,28},{1,5},{5,9},{9,... | collective-permute-start | bytes 786440 | tf_op jit(solution)/shard_map/ppermute | solution.py:234
  34.7 1.6 %collective-permute-done.3.refs_2_ = bf16[8,64,256]{2,1,0:T(8,128)(2,1)S(1)} collective-permute-done((bf16[8,64,256]{2,1,0:T(8,128)(2,1)S(1)}, bf16[8,64,256]{2,1,0:T(8,128)(2,1)S(1)}, u32[]{:S(2)}, u32[]{:S(2)}) %collective-permute-start.3) | collective-permute-done | bytes 262176 | tf_op jit(solution)/shard_map/ppermute | solution.py:230
  36.4 1.9 %collective-permute-start.11 = (bf16[8,64,256]{2,1,0:T(8,128)(2,1)S(1)}, bf16[8,64,256]{2,1,0:T(8,128)(2,1)S(1)}, u32[]{:S(2)}, u32[]{:S(2)}) collective-permute-start(bf16[8,64,256]{2,1,0:T(8,128)(2,1)S(1)} %collective-permute-done.3.refs_2_), channel_id=1, source_target_pairs={{4,0},{8,4},{12,8},{16,12},{20,16},{24,20},{28,24},{5,1},{9,5},{13... | collective-permute-start | bytes 786440 | tf_op jit(solution)/shard_map/ppermute | solution.py:234
  38.3 4.5 %collective-permute-start.7 = (bf16[8,64,256]{2,1,0:T(8,128)(2,1)S(1)}, bf16[8,64,256]{2,1,0:T(8,128)(2,1)S(1)}, u32[]{:S(2)}, u32[]{:S(2)}) collective-permute-start(bf16[8,64,256]{2,1,0:T(8,128)(2,1)S(1)} %collective-permute-done.3.refs_2_), channel_id=1, source_target_pairs={{0,4},{4,8},{8,12},{12,16},{16,20},{20,24},{24,28},{1,5},{5,9},{9,... | collective-permute-start | bytes 786440 | tf_op jit(solution)/shard_map/ppermute | solution.py:234
  42.9 1.9 %collective-permute-start.10 = (bf16[8,64,256]{2,1,0:T(8,128)(2,1)S(1)}, bf16[8,64,256]{2,1,0:T(8,128)(2,1)S(1)}, u32[]{:S(2)}, u32[]{:S(2)}) collective-permute-start(bf16[8,64,256]{2,1,0:T(8,128)(2,1)S(1)} %collective-permute-done.2.refs_1_), channel_id=1, source_target_pairs={{4,0},{8,4},{12,8},{16,12},{20,16},{24,20},{28,24},{5,1},{9,5},{13... | collective-permute-start | bytes 786440 | tf_op jit(solution)/shard_map/ppermute | solution.py:234
  44.8 4.5 %collective-permute-start.6 = (bf16[8,64,256]{2,1,0:T(8,128)(2,1)S(1)}, bf16[8,64,256]{2,1,0:T(8,128)(2,1)S(1)}, u32[]{:S(2)}, u32[]{:S(2)}) collective-permute-start(bf16[8,64,256]{2,1,0:T(8,128)(2,1)S(1)} %collective-permute-done.2.refs_1_), channel_id=1, source_target_pairs={{0,4},{4,8},{8,12},{12,16},{16,20},{20,24},{24,28},{1,5},{5,9},{9,... | collective-permute-start | bytes 786440 | tf_op jit(solution)/shard_map/ppermute | solution.py:234
  49.4 24.7 %tables.1 = (bf16[256,64,128]{2,1,0:T(8,128)(2,1)}, bf16[256,256]{1,0:T(8,128)(2,1)}) custom-call(s32[32,256]{1,0:T(8,128)} %get-tuple-element.18.src_ref, s32[32,256]{1,0:T(8,128)} %get-tuple-element.17.op_ref, bf16[512,320]{1,0:T(8,128)(2,1)} %pad.19.table_ref, s32[8,384]{1,0:T(8,128)} %pad.20.offset_ref, f32[8,384]{1,0:T(8,128)} %pad_convert_fusion.weight_ref, ...), custom_call_target="tpu_custom_call" | custom-call | flops 5368709120 | bytes 8388608 | tf_op jit(solution)/shard_map/tables/pallas_call | solution.py:74
  74.2 9.5 %pattern.1.own_ref = bf16[256,32,128]{2,1,0:T(8,128)(2,1)} custom-call(bf16[256,256]{1,0:T(8,128)(2,1)} %constant_dynamic-slice_fusion.forward_ref, bf16[8,64,256]{2,1,0:T(8,128)(2,1)} %copy-done, bf16[8,64,256]{2,1,0:T(8,128)(2,1)} %copy-done.4, bf16[8,64,256]{2,1,0:T(8,128)(2,1)} %copy-done.3, bf16[8,64,256]{2,1,0:T(8,128)(2,1)} %copy-done.2), custom_call_target="tpu_custom_call" | custom-call | flops 536870912 | bytes 4194304 | tf_op jit(solution)/shard_map/pattern/pallas_call | solution.py:133
  84.8 42.4 %field.1 = (f32[8,64,256]{2,1,0:T(8,128)}, bf16[8,64,256]{2,1,0:T(8,128)(2,1)}, bf16[8,64,256]{2,1,0:T(8,128)(2,1)}, bf16[8,64,256]{2,1,0:T(8,128)(2,1)}) custom-call(bf16[256,256]{1,0:T(8,128)(2,1)} %constant_dynamic-slice_fusion.forward_ref, bf16[256,64,128]{2,1,0:T(8,128)(2,1)} %get-tuple-element.11.matrix_ref, ...), custom_call_target="tpu_custom_call" | custom-call | flops 4294967296 | bytes 16777216 | tf_op jit(solution)/shard_map/field/pallas_call | solution.py:188
  127.2 5.4 %collective-permute-start.13 = (bf16[8,64,256]{2,1,0:T(8,128)(2,1)}, bf16[8,64,256]{2,1,0:T(8,128)(2,1)S(1)}, u32[]{:S(2)}, u32[]{:S(2)}) collective-permute-start(bf16[8,64,256]{2,1,0:T(8,128)(2,1)} %get-tuple-element.14), channel_id=1, source_target_pairs={{0,1},{1,2},{2,3},{3,0},{4,5},{5,6},{6,7},{7,4},{8,9},{9,10},{10,1... | collective-permute-start | bytes 786440 | tf_op jit(solution)/shard_map/ppermute | solution.py:230
  132.6 4.0 %collective-permute-start.14 = (bf16[8,64,256]{2,1,0:T(8,128)(2,1)}, bf16[8,64,256]{2,1,0:T(8,128)(2,1)S(1)}, u32[]{:S(2)}, u32[]{:S(2)}) collective-permute-start(bf16[8,64,256]{2,1,0:T(8,128)(2,1)} %get-tuple-element.15), channel_id=1, source_target_pairs={{0,2},{1,3},{2,0},{3,1},{4,6},{5,7},{6,4},{7,5},{8,10},{9,11},{10,... | collective-permute-start | bytes 786440 | tf_op jit(solution)/shard_map/ppermute | solution.py:230
  136.6 5.0 %collective-permute-done.13 = bf16[8,64,256]{2,1,0:T(8,128)(2,1)S(1)} collective-permute-done((bf16[8,64,256]{2,1,0:T(8,128)(2,1)}, bf16[8,64,256]{2,1,0:T(8,128)(2,1)S(1)}, u32[]{:S(2)}, u32[]{:S(2)}) %collective-permute-start.13) | collective-permute-done | bytes 262176 | tf_op jit(solution)/shard_map/ppermute | solution.py:230
  141.6 12.7 %collective-permute-done.14 = bf16[8,64,256]{2,1,0:T(8,128)(2,1)S(1)} collective-permute-done((bf16[8,64,256]{2,1,0:T(8,128)(2,1)}, bf16[8,64,256]{2,1,0:T(8,128)(2,1)S(1)}, u32[]{:S(2)}, u32[]{:S(2)}) %collective-permute-start.14) | collective-permute-done | bytes 262176 | tf_op jit(solution)/shard_map/ppermute | solution.py:230
  154.2 3.5 %collective-permute-done.15 = bf16[8,64,256]{2,1,0:T(8,128)(2,1)S(1)} collective-permute-done((bf16[8,64,256]{2,1,0:T(8,128)(2,1)}, bf16[8,64,256]{2,1,0:T(8,128)(2,1)S(1)}, u32[]{:S(2)}, u32[]{:S(2)}) %collective-permute-start.15) | collective-permute-done | bytes 262176 | tf_op jit(solution)/shard_map/ppermute | solution.py:230
  157.8 2.0 %add_select_fusion = f32[8,64,256]{2,1,0:T(8,128)} fusion(bf16[8,64,256]{2,1,0:T(8,128)(2,1)S(1)} %collective-permute-done.15, bf16[8,64,256]{2,1,0:T(8,128)(2,1)S(1)} %collective-permute-done.14, f32[8,64,256]{2,1,0:T(8,128)} %get-tuple-element.13, bf16[8,64,256]{2,1,0:T(8,128)(2,1)S(1)} %collective-permute-done.13, pred[8,256]{1,0:T(8,128)(4,1)S(1)} %broadcast_compare_fusion), kind=kLoop, calls=%fused_computation.5 | loop fusion | flops 917504 | bytes 1837056 | tf_op jit(solution)/shard_map/jit(_where)/select_n | solution.py:207
  (67 shorter events, 12.8 us)
Async XLA Ops:
  0.0 27.0 %copy-start.5 = (bf16[256,8]{0,1:T(8,128)(2,1)S(1)}, bf16[256,8]{0,1:T(8,128)(2,1)}, u32[]{:S(2)}) copy-start(bf16[256,8]{0,1:T(8,128)(2,1)} %param.16) | copy-start | bytes 12292
  1.8 72.4 %copy-start = (bf16[8,64,256]{2,1,0:T(8,128)(2,1)}, bf16[8,64,256]{2,1,0:T(8,128)(2,1)S(1)}, u32[]{:S(2)}) copy-start(bf16[8,64,256]{2,1,0:T(8,128)(2,1)S(1)} %broadcast_select_fusion.refs_0_) | copy-start | bytes 786436
  1.8 28.4 %collective-permute-start.9 = (bf16[8,64,256]{2,1,0:T(8,128)(2,1)S(1)}, bf16[8,64,256]{2,1,0:T(8,128)(2,1)S(1)}, u32[]{:S(2)}, u32[]{:S(2)}) collective-permute-start(bf16[8,64,256]{2,1,0:T(8,128)(2,1)S(1)} %broadcast_select_fusion.refs_0_), channel_id=1, source_target_pairs={{4,0},{8,4},{12,8},{16,12},{20,16},{24,20},{28,24},{5,1},{9,5},{13... | collective-permute-start | bytes 786440 | tf_op jit(solution)/shard_map/ppermute | solution.py:234
  4.4 33.9 %collective-permute-start.5 = (bf16[8,64,256]{2,1,0:T(8,128)(2,1)S(1)}, bf16[8,64,256]{2,1,0:T(8,128)(2,1)S(1)}, u32[]{:S(2)}, u32[]{:S(2)}) collective-permute-start(bf16[8,64,256]{2,1,0:T(8,128)(2,1)S(1)} %broadcast_select_fusion.refs_0_), channel_id=1, source_target_pairs={{0,4},{4,8},{8,12},{12,16},{16,20},{20,24},{24,28},{1,5},{5,9},{9,... | collective-permute-start | bytes 786440 | tf_op jit(solution)/shard_map/ppermute | solution.py:234
  8.3 19.4 %collective-permute-start.4 = (bf16[8,64,256]{2,1,0:T(8,128)(2,1)S(1)}, bf16[8,64,256]{2,1,0:T(8,128)(2,1)S(1)}, u32[]{:S(2)}, u32[]{:S(2)}) collective-permute-start(bf16[8,64,256]{2,1,0:T(8,128)(2,1)S(1)} %broadcast_select_fusion.refs_0_), channel_id=1, source_target_pairs={{0,3},{1,0},{2,1},{3,2},{4,7},{5,4},{6,5},{7,6},{8,11},{9,8},{10,9... | collective-permute-start | bytes 786440 | tf_op jit(solution)/shard_map/ppermute | solution.py:230
  10.0 12.6 %collective-permute-start = (bf16[8,16]{0,1:T(8,128)(2,1)S(1)}, bf16[8,16]{0,1:T(8,128)(2,1)S(1)}, u32[]{:S(2)}, u32[]{:S(2)}) collective-permute-start(bf16[8,16]{0,1:T(8,128)(2,1)S(1)} %get-tuple-element.19), channel_id=1, source_target_pairs={{0,1},{1,2},{2,3},{3,0},{4,5},{5,6},{6,7},{7,4},{8,9},{9,10},{10,1... | collective-permute-start | bytes 776 | tf_op jit(solution)/shard_map/ppermute | solution.py:230
  11.3 13.3 %collective-permute-start.1 = (bf16[8,16]{0,1:T(8,128)(2,1)S(1)}, bf16[8,16]{0,1:T(8,128)(2,1)S(1)}, u32[]{:S(2)}, u32[]{:S(2)}) collective-permute-start(bf16[8,16]{0,1:T(8,128)(2,1)S(1)} %get-tuple-element.20), channel_id=1, source_target_pairs={{0,3},{1,0},{2,1},{3,2},{4,7},{5,4},{6,5},{7,6},{8,11},{9,8},{10,9... | collective-permute-start | bytes 776 | tf_op jit(solution)/shard_map/ppermute | solution.py:230
  22.5 13.9 %collective-permute-start.3 = (bf16[8,64,256]{2,1,0:T(8,128)(2,1)S(1)}, bf16[8,64,256]{2,1,0:T(8,128)(2,1)S(1)}, u32[]{:S(2)}, u32[]{:S(2)}) collective-permute-start(bf16[8,64,256]{2,1,0:T(8,128)(2,1)S(1)} %broadcast_select_fusion.refs_0_), channel_id=1, source_target_pairs={{0,2},{1,3},{2,0},{3,1},{4,6},{5,7},{6,4},{7,5},{8,10},{9,11},{10,... | collective-permute-start | bytes 786440 | tf_op jit(solution)/shard_map/ppermute | solution.py:230
  24.6 18.3 %collective-permute-start.2 = (bf16[8,64,256]{2,1,0:T(8,128)(2,1)S(1)}, bf16[8,64,256]{2,1,0:T(8,128)(2,1)S(1)}, u32[]{:S(2)}, u32[]{:S(2)}) collective-permute-start(bf16[8,64,256]{2,1,0:T(8,128)(2,1)S(1)} %broadcast_select_fusion.refs_0_), channel_id=1, source_target_pairs={{0,1},{1,2},{2,3},{3,0},{4,5},{5,6},{6,7},{7,4},{8,9},{9,10},{10,1... | collective-permute-start | bytes 786440 | tf_op jit(solution)/shard_map/ppermute | solution.py:230
  27.7 46.5 %copy-start.2 = (bf16[8,64,256]{2,1,0:T(8,128)(2,1)}, bf16[8,64,256]{2,1,0:T(8,128)(2,1)S(1)}, u32[]{:S(2)}) copy-start(bf16[8,64,256]{2,1,0:T(8,128)(2,1)S(1)} %collective-permute-done.4.refs_3_) | copy-start | bytes 786436
  27.7 17.2 %collective-permute-start.12 = (bf16[8,64,256]{2,1,0:T(8,128)(2,1)S(1)}, bf16[8,64,256]{2,1,0:T(8,128)(2,1)S(1)}, u32[]{:S(2)}, u32[]{:S(2)}) collective-permute-start(bf16[8,64,256]{2,1,0:T(8,128)(2,1)S(1)} %collective-permute-done.4.refs_3_), channel_id=1, source_target_pairs={{4,0},{8,4},{12,8},{16,12},{20,16},{24,20},{28,24},{5,1},{9,5},{13... | collective-permute-start | bytes 786440 | tf_op jit(solution)/shard_map/ppermute | solution.py:234
  30.2 43.9 %copy-start.6 = (bf16[8,64,256]{2,1,0:T(8,128)(2,1)}, bf16[8,64,256]{2,1,0:T(8,128)(2,1)S(1)}, u32[]{:S(2)}) copy-start(bf16[8,64,256]{2,1,0:T(8,128)(2,1)S(1)} %collective-permute-done.9.refs_4_) | copy-start | bytes 786436
  30.2 53.5 %collective-permute-start.8 = (bf16[8,64,256]{2,1,0:T(8,128)(2,1)S(1)}, bf16[8,64,256]{2,1,0:T(8,128)(2,1)S(1)}, u32[]{:S(2)}, u32[]{:S(2)}) collective-permute-start(bf16[8,64,256]{2,1,0:T(8,128)(2,1)S(1)} %collective-permute-done.4.refs_3_), channel_id=1, source_target_pairs={{0,4},{4,8},{8,12},{12,16},{16,20},{20,24},{24,28},{1,5},{5,9},{9,... | collective-permute-start | bytes 786440 | tf_op jit(solution)/shard_map/ppermute | solution.py:234
  36.4 37.8 %copy-start.3 = (bf16[8,64,256]{2,1,0:T(8,128)(2,1)}, bf16[8,64,256]{2,1,0:T(8,128)(2,1)S(1)}, u32[]{:S(2)}) copy-start(bf16[8,64,256]{2,1,0:T(8,128)(2,1)S(1)} %collective-permute-done.3.refs_2_) | copy-start | bytes 786436
  36.4 47.3 %collective-permute-start.11 = (bf16[8,64,256]{2,1,0:T(8,128)(2,1)S(1)}, bf16[8,64,256]{2,1,0:T(8,128)(2,1)S(1)}, u32[]{:S(2)}, u32[]{:S(2)}) collective-permute-start(bf16[8,64,256]{2,1,0:T(8,128)(2,1)S(1)} %collective-permute-done.3.refs_2_), channel_id=1, source_target_pairs={{4,0},{8,4},{12,8},{16,12},{20,16},{24,20},{28,24},{5,1},{9,5},{13... | collective-permute-start | bytes 786440 | tf_op jit(solution)/shard_map/ppermute | solution.py:234
  38.3 35.8 %copy-start.7 = (bf16[8,64,256]{2,1,0:T(8,128)(2,1)}, bf16[8,64,256]{2,1,0:T(8,128)(2,1)S(1)}, u32[]{:S(2)}) copy-start(bf16[8,64,256]{2,1,0:T(8,128)(2,1)S(1)} %collective-permute-done.5.refs_0_) | copy-start | bytes 786436
  38.3 45.4 %collective-permute-start.7 = (bf16[8,64,256]{2,1,0:T(8,128)(2,1)S(1)}, bf16[8,64,256]{2,1,0:T(8,128)(2,1)S(1)}, u32[]{:S(2)}, u32[]{:S(2)}) collective-permute-start(bf16[8,64,256]{2,1,0:T(8,128)(2,1)S(1)} %collective-permute-done.3.refs_2_), channel_id=1, source_target_pairs={{0,4},{4,8},{8,12},{12,16},{16,20},{20,24},{24,28},{1,5},{5,9},{9,... | collective-permute-start | bytes 786440 | tf_op jit(solution)/shard_map/ppermute | solution.py:234
  42.9 31.3 %copy-start.4 = (bf16[8,64,256]{2,1,0:T(8,128)(2,1)}, bf16[8,64,256]{2,1,0:T(8,128)(2,1)S(1)}, u32[]{:S(2)}) copy-start(bf16[8,64,256]{2,1,0:T(8,128)(2,1)S(1)} %collective-permute-done.2.refs_1_) | copy-start | bytes 786436
  42.9 40.8 %collective-permute-start.10 = (bf16[8,64,256]{2,1,0:T(8,128)(2,1)S(1)}, bf16[8,64,256]{2,1,0:T(8,128)(2,1)S(1)}, u32[]{:S(2)}, u32[]{:S(2)}) collective-permute-start(bf16[8,64,256]{2,1,0:T(8,128)(2,1)S(1)} %collective-permute-done.2.refs_1_), channel_id=1, source_target_pairs={{4,0},{8,4},{12,8},{16,12},{20,16},{24,20},{28,24},{5,1},{9,5},{13... | collective-permute-start | bytes 786440 | tf_op jit(solution)/shard_map/ppermute | solution.py:234
  44.8 29.3 %copy-start.8 = (bf16[8,64,256]{2,1,0:T(8,128)(2,1)}, bf16[8,64,256]{2,1,0:T(8,128)(2,1)S(1)}, u32[]{:S(2)}) copy-start(bf16[8,64,256]{2,1,0:T(8,128)(2,1)S(1)} %collective-permute-done.12.refs_7_) | copy-start | bytes 786436
  44.8 38.9 %collective-permute-start.6 = (bf16[8,64,256]{2,1,0:T(8,128)(2,1)S(1)}, bf16[8,64,256]{2,1,0:T(8,128)(2,1)S(1)}, u32[]{:S(2)}, u32[]{:S(2)}) collective-permute-start(bf16[8,64,256]{2,1,0:T(8,128)(2,1)S(1)} %collective-permute-done.2.refs_1_), channel_id=1, source_target_pairs={{0,4},{4,8},{8,12},{12,16},{16,20},{20,24},{24,28},{1,5},{5,9},{9,... | collective-permute-start | bytes 786440 | tf_op jit(solution)/shard_map/ppermute | solution.py:234
  127.2 14.4 %collective-permute-start.13 = (bf16[8,64,256]{2,1,0:T(8,128)(2,1)}, bf16[8,64,256]{2,1,0:T(8,128)(2,1)S(1)}, u32[]{:S(2)}, u32[]{:S(2)}) collective-permute-start(bf16[8,64,256]{2,1,0:T(8,128)(2,1)} %get-tuple-element.14), channel_id=1, source_target_pairs={{0,1},{1,2},{2,3},{3,0},{4,5},{5,6},{6,7},{7,4},{8,9},{9,10},{10,1... | collective-permute-start | bytes 786440 | tf_op jit(solution)/shard_map/ppermute | solution.py:230
  132.6 21.6 %collective-permute-start.14 = (bf16[8,64,256]{2,1,0:T(8,128)(2,1)}, bf16[8,64,256]{2,1,0:T(8,128)(2,1)S(1)}, u32[]{:S(2)}, u32[]{:S(2)}) collective-permute-start(bf16[8,64,256]{2,1,0:T(8,128)(2,1)} %get-tuple-element.15), channel_id=1, source_target_pairs={{0,2},{1,3},{2,0},{3,1},{4,6},{5,7},{6,4},{7,5},{8,10},{9,11},{10,... | collective-permute-start | bytes 786440 | tf_op jit(solution)/shard_map/ppermute | solution.py:230
  136.6 21.2 %collective-permute-start.15 = (bf16[8,64,256]{2,1,0:T(8,128)(2,1)}, bf16[8,64,256]{2,1,0:T(8,128)(2,1)S(1)}, u32[]{:S(2)}, u32[]{:S(2)}) collective-permute-start(bf16[8,64,256]{2,1,0:T(8,128)(2,1)} %get-tuple-element.16), channel_id=1, source_target_pairs={{0,3},{1,0},{2,1},{3,2},{4,7},{5,4},{6,5},{7,6},{8,11},{9,8},{10,9... | collective-permute-start | bytes 786440 | tf_op jit(solution)/shard_map/ppermute | solution.py:230
  (6 other events, 25.6 us)

commit v2 on v1

--- a/solution.py
+++ b/solution.py
@@ -29,6 +29,17 @@
     return pl.CostEstimate(flops=int(flops), bytes_accessed=int(nbytes), transcendentals=0)
 
 
+def unrolled(trips, most, step):
+    size = next(n for n in range(min(most, trips), 0, -1) if trips % n == 0)
+
+    def block(i, carry):
+        for j in range(size):
+            step(i * size + j)
+        return carry
+
+    lax.fori_loop(0, trips // size, block, 0)
+
+
 def tables_kernel(
     src_ref, op_ref, table_ref, offset_ref, weight_ref, receive_ref, matrix_ref, folded_ref, wide
 ):
@@ -36,30 +47,31 @@
     dirs, rows, window = matrix_ref.shape
     kinds = table_ref.shape[1]
 
-    def one_box(box, carry):
-        src = src_ref[pl.ds(box, 1), :]
-        ops = op_ref[pl.ds(box, 1), :]
-        hit_kind = (lax.broadcasted_iota(jnp.int32, (kinds, width), 0) == ops).astype(F32).astype(BF)
-        hit_src = (lax.broadcasted_iota(jnp.int32, (window, width), 0) == src).astype(F32).astype(BF)
-        counts = dot(hit_kind, hit_src, NT).astype(BF)
+    def two_boxes(step):
+        counts = []
+        for box in (2 * step, 2 * step + 1):
+            src = src_ref[pl.ds(box, 1), :]
+            ops = op_ref[pl.ds(box, 1), :]
+            hit_kind = lax.broadcasted_iota(jnp.int32, (kinds, width), 0) == ops
+            hit_src = lax.broadcasted_iota(jnp.int32, (window, width), 0) == src
+            counts.append(dot(hit_kind.astype(F32).astype(BF), hit_src.astype(F32).astype(BF), NT))
+        counts = jnp.concatenate(counts, axis=1).astype(BF)
         entries = dot(table_ref[...], counts, NN)
+        for i in range(2):
+            for c in range(window // LANES):
+                part = entries[:, i * window + c * LANES : i * window + (c + 1) * LANES]
+                at = 2 * step + i
+                wide[c, pl.ds(at, dirs, stride=rows + 1), :] = part[:dirs]
+                wide[c, pl.ds(at + boxes, dirs, stride=rows + 1), :] = part[dirs:]
+
+    unrolled(boxes // 2, 2, two_boxes)
+
+    def narrow(k):
         for c in range(window // LANES):
-            part = entries[:, c * LANES : (c + 1) * LANES]
-            wide[c, pl.ds(box, dirs, stride=rows), :] = part[:dirs]
-            wide[c, pl.ds(box + boxes, dirs, stride=rows), :] = part[dirs:]
-        return carry
-
-    lax.fori_loop(0, boxes, one_box, 0)
-
-    def narrow(step, carry):
-        for i in range(4):
-            k = step * 4 + i
-            for c in range(window // LANES):
-                part = wide[c, pl.ds(pl.multiple_of(k * rows, 8), rows), :]
-                matrix_ref[k, :, c * LANES : (c + 1) * LANES] = part.astype(BF)
-        return carry
-
-    lax.fori_loop(0, dirs // 4, narrow, 0)
+            part = wide[c, pl.ds(k * (rows + 1), rows), :]
+            matrix_ref[k, :, c * LANES : (c + 1) * LANES] = part.astype(BF)
+
+    unrolled(dirs, 8, narrow)
 
     extent = offset_ref.shape[1]
     own = lax.broadcasted_iota(jnp.int32, (dirs, extent), 0)
@@ -79,7 +91,7 @@
         ),
         in_specs=[VMEM] * 6,
         out_specs=(VMEM, VMEM),
-        scratch_shapes=[pltpu.VMEM((window // LANES, dirs * 2 * boxes, LANES), F32)],
+        scratch_shapes=[pltpu.VMEM((window // LANES, dirs * (2 * boxes + 1), LANES), F32)],
         cost_estimate=cost(2 * boxes * 2 * dirs * 320 * window * 4, 8 << 20),
         name="tables",
     )(src, ops, table, offsets, weights, receive)
@@ -97,33 +109,29 @@
     dirs = forward_ref.shape[0]
     first = 0
     for ref in box_refs:
-        count = ref.shape[0]
         width = 2 * ref.shape[1]
 
-        def pair(step, carry, ref=ref, first=first, width=width):
+        def pair(step, ref=ref, first=first, width=width):
             both = jnp.concatenate([rotated(ref[2 * step]), rotated(ref[2 * step + 1])], axis=0)
             field = dot(forward_ref[...], both, NT)
             at = first + 2 * step
             out[pl.ds(at, dirs, stride=stride), :] = field[:, :width]
             out[pl.ds(at + 1, dirs, stride=stride), :] = field[:, width:]
-            return carry
-
-        lax.fori_loop(0, count // 2, pair, 0)
-        first += count
+
+        for step in range(ref.shape[0] // 2):
+            pair(step)
+        first += ref.shape[0]
 
 
 def pattern_kernel(count, forward_ref, *refs):
     box_refs, pattern_ref, wide = refs[:count], refs[count], refs[count + 1]
     dirs, boxes, _ = pattern_ref.shape
-    radiate(forward_ref, box_refs, wide, boxes)
-
-    def narrow(step, carry):
-        for i in range(4):
-            k = step * 4 + i
-            pattern_ref[k] = wide[pl.ds(pl.multiple_of(k * boxes, 8), boxes), :].astype(BF)
-        return carry
-
-    lax.fori_loop(0, dirs // 4, narrow, 0)
+    radiate(forward_ref, box_refs, wide, boxes + 1)
+
+    def narrow(k):
+        pattern_ref[k] = wide[pl.ds(k * (boxes + 1), boxes), :].astype(BF)
+
+    unrolled(dirs, 16, narrow)
 
 
 def own_pattern(forward, shards):
@@ -135,7 +143,7 @@
         out_shape=jax.ShapeDtypeStruct((dirs, boxes, width), BF),
         in_specs=[VMEM] * (1 + len(shards)),
         out_specs=VMEM,
-        scratch_shapes=[pltpu.VMEM((dirs * boxes, width), F32)],
+        scratch_shapes=[pltpu.VMEM((dirs * (boxes + 1), width), F32)],
         cost_estimate=cost(2 * dirs * boxes * width * 256, 4 << 20),
         name="pattern",
     )(forward, *shards)
@@ -149,35 +157,28 @@
     near_boxes = 2 * own_boxes
     boxes = matrix_ref.shape[1] // 2
     half = width // 2
-    radiate(forward_ref, box_refs, near, near_boxes)
+    radiate(forward_ref, box_refs, near, near_boxes + 1)
     lane = lax.broadcasted_iota(jnp.int32, (boxes, width), 1)
     sign = jnp.where(lane < half, -1.0, 1.0).astype(F32)
 
-    def translate(step, carry):
-        for i in range(4):
-            k = step * 4 + i
-            around = near[pl.ds(pl.multiple_of(k * near_boxes, 8), near_boxes), :].astype(BF)
-            fields = jnp.concatenate([own_ref[k], around], axis=0)
-            both = dot(matrix_ref[k][:, : own_boxes + near_boxes], fields, NN)
-            turned = pltpu.roll(both[boxes:], half, 1)
-            moved[pl.ds(pl.multiple_of(k * boxes, 8), boxes), :] = both[:boxes] + sign * turned
-        return carry
-
-    lax.fori_loop(0, dirs // 4, translate, 0)
+    def translate(k):
+        around = near[pl.ds(k * (near_boxes + 1), near_boxes), :].astype(BF)
+        fields = jnp.concatenate([own_ref[k], around], axis=0)
+        both = dot(matrix_ref[k][:, : own_boxes + near_boxes], fields, NN)
+        turned = pltpu.roll(both[boxes:], half, 1)
+        moved[pl.ds(k * (boxes + 1), boxes), :] = both[:boxes] + sign * turned
+
+    unrolled(dirs, 64 * 32 // boxes, translate)
 
     per = boxes // count
     unk = folded_ref.shape[1] // 2
     for j, out_ref in enumerate(out_refs):
-
-        def receive(i, carry, j=j, out_ref=out_ref):
-            field = moved[pl.ds(j * per + i, dirs, stride=boxes), :].astype(BF)
+        for i in range(per):
+            field = moved[pl.ds(j * per + i, dirs, stride=boxes + 1), :].astype(BF)
             full = dot(field, folded_ref[...], TN)
             re = full[:half, :unk] - full[half:, unk:]
             im = full[:half, unk:] + full[half:, :unk]
             out_ref[i] = jnp.concatenate([re, im], axis=1).astype(out_ref.dtype)
-            return carry
-
-        lax.fori_loop(0, per, receive, 0)
 
 
 def receive_field(forward, matrix, folded, own, left, right):
@@ -193,8 +194,8 @@
         in_specs=[VMEM] * (4 + 2 * count),
         out_specs=(VMEM,) * count,
         scratch_shapes=[
-            pltpu.VMEM((dirs * 2 * own_boxes, width), F32),
-            pltpu.VMEM((dirs * matrix.shape[1] // 2, width), F32),
+            pltpu.VMEM((dirs * (2 * own_boxes + 1), width), F32),
+            pltpu.VMEM((dirs * (matrix.shape[1] // 2 + 1), width), F32),
         ],
         cost_estimate=cost(4 << 30, 16 << 20),
         name="field",
@@ -250,7 +251,7 @@
         jnp.concatenate([lists, lists], axis=1), dir_index * per, boxes, 1
     )
     table = translators.transpose(1, 2, 0).reshape(2 * dirs, kinds)
-    table = jnp.pad(table, ((0, 0), (0, round_up(kinds, 64) - kinds)))
+    table = jnp.pad(table, ((0, 0), (0, round_up(kinds, LANES) - kinds)))
 
     own_dirs = dir_index * dirs + jnp.arange(dirs, dtype=jnp.int32)
     distance = (stencil - own_dirs[:, None]) % all_dirs

time: 161 us -> 106 us (0.66)
  Pallas kernels: 76.6 us -> 22 us
    pallas_call x1, Pallas kernels: 42.4 us -> 8.69 us  [receive_field(): pl.pallas_call(functools.partial(field_kernel, count), out_shape=tuple((j...]
    pallas_call x1, Pallas kernels: 24.7 us -> 9.72 us  [build_tables(): pl.pallas_call(tables_kernel, out_shape=(jax.ShapeDtypeStruct((dirs, 2 *...]
    pallas_call x1, Pallas kernels: 9.48 us -> 3.63 us  [own_pattern(): pl.pallas_call(functools.partial(pattern_kernel, len(shards)), out_shape=...]
  transfers between devices with their start and end apart: 16 -> 16, of which waited for: 4 -> 4; matrix products, arithmetic and copies ran while one was open for 7% -> 11% of each run, Pallas kernels for 21% -> 13%
where the time goes in v2:
time: 106 us; the launch traced here: 105 us
  starting transfers between devices  43.2 us (41%)
  waiting for transfers between devices  22.8 us (22%)
  Pallas kernels  22 us (21%)
  other arithmetic  8.51 us (8%)
  local copies, waits for them, and re-layouts  8.29 us (8%)
    ppermute x8, starting transfers between devices, shift(): return lax.ppermute(values, 'grp', pairs)  25.8 us
    ppermute x8, waiting for transfers between devices, turn(): lax.ppermute(values, 'dir', [(i, (i + step) % n_dir) for i in range(n_dir)])  22.8 us
    ppermute x8, starting transfers between devices, turn(): lax.ppermute(values, 'dir', [(i, (i + step) % n_dir) for i in range(n_dir)])  17.4 us
    pallas_call x1, Pallas kernels, build_tables(): pl.pallas_call(tables_kernel, out_shape=(jax.ShapeDtypeStruct((dirs, 2 *...  9.72 us
    pallas_call x1, Pallas kernels, receive_field(): pl.pallas_call(functools.partial(field_kernel, count), out_shape=tuple((j...  8.69 us
    unnamed x33, local copies, waits for them, and re-layouts  4.09 us
    pallas_call x1, Pallas kernels, own_pattern(): pl.pallas_call(functools.partial(pattern_kernel, len(shards)), out_shape=...  3.63 us
    select_n x2, other arithmetic, mask_rows(): return jnp.where(keep, values, jnp.zeros_like(values))  2.94 us
  transfers between devices with their start and end apart: 16, of which 4 were waited for; matrix products, arithmetic and copies ran while one was open for 11% of the time, Pallas kernels for 13%

profile of v2, /device:TPU:11, one launch (start us, length us, event | category | flops | bytes accessed | tf_op | source)
XLA Modules:
  0.0 105.2 jit_solution(16568064132221478233)
XLA Ops:
  1.8 2.6 %collective-permute-start.9 = (bf16[8,64,256]{2,1,0:T(8,128)(2,1)S(1)}, bf16[8,64,256]{2,1,0:T(8,128)(2,1)S(1)}, u32[]{:S(2)}, u32[]{:S(2)}) collective-permute-start(bf16[8,64,256]{2,1,0:T(8,128)(2,1)S(1)} %broadcast_select_fusion.refs_0_), channel_id=1, source_target_pairs={{4,0},{8,4},{12,8},{16,12},{20,16},{24,20},{28,24},{5,1},{9,5},{13... | collective-permute-start | bytes 786440 | tf_op jit(solution)/shard_map/ppermute | solution.py:235
  4.4 3.9 %collective-permute-start.5 = (bf16[8,64,256]{2,1,0:T(8,128)(2,1)S(1)}, bf16[8,64,256]{2,1,0:T(8,128)(2,1)S(1)}, u32[]{:S(2)}, u32[]{:S(2)}) collective-permute-start(bf16[8,64,256]{2,1,0:T(8,128)(2,1)S(1)} %broadcast_select_fusion.refs_0_), channel_id=1, source_target_pairs={{0,4},{4,8},{8,12},{12,16},{16,20},{20,24},{24,28},{1,5},{5,9},{9,... | collective-permute-start | bytes 786440 | tf_op jit(solution)/shard_map/ppermute | solution.py:235
  10.0 1.3 %collective-permute-start = (bf16[8,16]{0,1:T(8,128)(2,1)S(1)}, bf16[8,16]{0,1:T(8,128)(2,1)S(1)}, u32[]{:S(2)}, u32[]{:S(2)}) collective-permute-start(bf16[8,16]{0,1:T(8,128)(2,1)S(1)} %get-tuple-element.19), channel_id=1, source_target_pairs={{0,1},{1,2},{2,3},{3,0},{4,5},{5,6},{6,7},{7,4},{8,9},{9,10},{10,1... | collective-permute-start | bytes 776 | tf_op jit(solution)/shard_map/ppermute | solution.py:231
  11.3 2.0 %collective-permute-start.1 = (bf16[8,16]{0,1:T(8,128)(2,1)S(1)}, bf16[8,16]{0,1:T(8,128)(2,1)S(1)}, u32[]{:S(2)}, u32[]{:S(2)}) collective-permute-start(bf16[8,16]{0,1:T(8,128)(2,1)S(1)} %get-tuple-element.20), channel_id=1, source_target_pairs={{0,3},{1,0},{2,1},{3,2},{4,7},{5,4},{6,5},{7,6},{8,11},{9,8},{10,9... | collective-permute-start | bytes 776 | tf_op jit(solution)/shard_map/ppermute | solution.py:231
  17.2 1.1 %copy.20 = bf16[128,8,2,128]{3,1,2,0:T(8,128)(2,1)S(1)} copy(bf16[128,8,2,128]{3,2,1,0:T(2,128)(2,1)} %bitcast.34) | data formatting | bytes 1048576
  18.3 1.1 %copy.19 = bf16[128,8,2,128]{3,1,2,0:T(8,128)(2,1)S(1)} copy(bf16[128,8,2,128]{3,2,1,0:T(2,128)(2,1)} %bitcast.33) | data formatting | bytes 1048576
  22.5 2.1 %collective-permute-start.3 = (bf16[8,64,256]{2,1,0:T(8,128)(2,1)S(1)}, bf16[8,64,256]{2,1,0:T(8,128)(2,1)S(1)}, u32[]{:S(2)}, u32[]{:S(2)}) collective-permute-start(bf16[8,64,256]{2,1,0:T(8,128)(2,1)S(1)} %broadcast_select_fusion.refs_0_), channel_id=1, source_target_pairs={{0,2},{1,3},{2,0},{3,1},{4,6},{5,7},{6,4},{7,5},{8,10},{9,11},{10,... | collective-permute-start | bytes 786440 | tf_op jit(solution)/shard_map/ppermute | solution.py:231
  24.6 2.4 %collective-permute-start.2 = (bf16[8,64,256]{2,1,0:T(8,128)(2,1)S(1)}, bf16[8,64,256]{2,1,0:T(8,128)(2,1)S(1)}, u32[]{:S(2)}, u32[]{:S(2)}) collective-permute-start(bf16[8,64,256]{2,1,0:T(8,128)(2,1)S(1)} %broadcast_select_fusion.refs_0_), channel_id=1, source_target_pairs={{0,1},{1,2},{2,3},{3,0},{4,5},{5,6},{6,7},{7,4},{8,9},{9,10},{10,1... | collective-permute-start | bytes 786440 | tf_op jit(solution)/shard_map/ppermute | solution.py:231
  27.7 1.9 %collective-permute-start.12 = (bf16[8,64,256]{2,1,0:T(8,128)(2,1)S(1)}, bf16[8,64,256]{2,1,0:T(8,128)(2,1)S(1)}, u32[]{:S(2)}, u32[]{:S(2)}) collective-permute-start(bf16[8,64,256]{2,1,0:T(8,128)(2,1)S(1)} %collective-permute-done.4.refs_3_), channel_id=1, source_target_pairs={{4,0},{8,4},{12,8},{16,12},{20,16},{24,20},{28,24},{5,1},{9,5},{13... | collective-permute-start | bytes 786440 | tf_op jit(solution)/shard_map/ppermute | solution.py:235
  30.2 4.5 %collective-permute-start.8 = (bf16[8,64,256]{2,1,0:T(8,128)(2,1)S(1)}, bf16[8,64,256]{2,1,0:T(8,128)(2,1)S(1)}, u32[]{:S(2)}, u32[]{:S(2)}) collective-permute-start(bf16[8,64,256]{2,1,0:T(8,128)(2,1)S(1)} %collective-permute-done.4.refs_3_), channel_id=1, source_target_pairs={{0,4},{4,8},{8,12},{12,16},{16,20},{20,24},{24,28},{1,5},{5,9},{9,... | collective-permute-start | bytes 786440 | tf_op jit(solution)/shard_map/ppermute | solution.py:235
  34.7 1.6 %collective-permute-done.3.refs_2_ = bf16[8,64,256]{2,1,0:T(8,128)(2,1)S(1)} collective-permute-done((bf16[8,64,256]{2,1,0:T(8,128)(2,1)S(1)}, bf16[8,64,256]{2,1,0:T(8,128)(2,1)S(1)}, u32[]{:S(2)}, u32[]{:S(2)}) %collective-permute-start.3) | collective-permute-done | bytes 262176 | tf_op jit(solution)/shard_map/ppermute | solution.py:231
  36.4 1.9 %collective-permute-start.11 = (bf16[8,64,256]{2,1,0:T(8,128)(2,1)S(1)}, bf16[8,64,256]{2,1,0:T(8,128)(2,1)S(1)}, u32[]{:S(2)}, u32[]{:S(2)}) collective-permute-start(bf16[8,64,256]{2,1,0:T(8,128)(2,1)S(1)} %collective-permute-done.3.refs_2_), channel_id=1, source_target_pairs={{4,0},{8,4},{12,8},{16,12},{20,16},{24,20},{28,24},{5,1},{9,5},{13... | collective-permute-start | bytes 786440 | tf_op jit(solution)/shard_map/ppermute | solution.py:235
  38.3 4.5 %collective-permute-start.7 = (bf16[8,64,256]{2,1,0:T(8,128)(2,1)S(1)}, bf16[8,64,256]{2,1,0:T(8,128)(2,1)S(1)}, u32[]{:S(2)}, u32[]{:S(2)}) collective-permute-start(bf16[8,64,256]{2,1,0:T(8,128)(2,1)S(1)} %collective-permute-done.3.refs_2_), channel_id=1, source_target_pairs={{0,4},{4,8},{8,12},{12,16},{16,20},{20,24},{24,28},{1,5},{5,9},{9,... | collective-permute-start | bytes 786440 | tf_op jit(solution)/shard_map/ppermute | solution.py:235
  42.9 1.9 %collective-permute-start.10 = (bf16[8,64,256]{2,1,0:T(8,128)(2,1)S(1)}, bf16[8,64,256]{2,1,0:T(8,128)(2,1)S(1)}, u32[]{:S(2)}, u32[]{:S(2)}) collective-permute-start(bf16[8,64,256]{2,1,0:T(8,128)(2,1)S(1)} %collective-permute-done.2.refs_1_), channel_id=1, source_target_pairs={{4,0},{8,4},{12,8},{16,12},{20,16},{24,20},{28,24},{5,1},{9,5},{13... | collective-permute-start | bytes 786440 | tf_op jit(solution)/shard_map/ppermute | solution.py:235
  44.8 4.5 %collective-permute-start.6 = (bf16[8,64,256]{2,1,0:T(8,128)(2,1)S(1)}, bf16[8,64,256]{2,1,0:T(8,128)(2,1)S(1)}, u32[]{:S(2)}, u32[]{:S(2)}) collective-permute-start(bf16[8,64,256]{2,1,0:T(8,128)(2,1)S(1)} %collective-permute-done.2.refs_1_), channel_id=1, source_target_pairs={{0,4},{4,8},{8,12},{12,16},{16,20},{20,24},{24,28},{1,5},{5,9},{9,... | collective-permute-start | bytes 786440 | tf_op jit(solution)/shard_map/ppermute | solution.py:235
  49.4 9.7 %tables.1 = (bf16[256,64,128]{2,1,0:T(8,128)(2,1)}, bf16[256,256]{1,0:T(8,128)(2,1)}) custom-call(s32[32,256]{1,0:T(8,128)} %get-tuple-element.18.src_ref, s32[32,256]{1,0:T(8,128)} %get-tuple-element.17.op_ref, bf16[512,384]{1,0:T(8,128)(2,1)} %pad.19.table_ref, s32[8,384]{1,0:T(8,128)} %pad.20.offset_ref, f32[8,384]{1,0:T(8,128)} %pad_convert_fusion.weight_ref, ...), custom_call_target="tpu_custom_call" | custom-call | flops 5368709120 | bytes 8388608 | tf_op jit(solution)/shard_map/tables/pallas_call | solution.py:86
  59.2 3.6 %pattern.1.own_ref = bf16[256,32,128]{2,1,0:T(8,128)(2,1)} custom-call(bf16[256,256]{1,0:T(8,128)(2,1)} %constant_dynamic-slice_fusion.forward_ref, bf16[8,64,256]{2,1,0:T(8,128)(2,1)} %copy-done, bf16[8,64,256]{2,1,0:T(8,128)(2,1)} %copy-done.4, bf16[8,64,256]{2,1,0:T(8,128)(2,1)} %copy-done.3, bf16[8,64,256]{2,1,0:T(8,128)(2,1)} %copy-done.2), custom_call_target="tpu_custom_call" | custom-call | flops 536870912 | bytes 4194304 | tf_op jit(solution)/shard_map/pattern/pallas_call | solution.py:141
  64.0 8.7 %field.1 = (f32[8,64,256]{2,1,0:T(8,128)}, bf16[8,64,256]{2,1,0:T(8,128)(2,1)}, bf16[8,64,256]{2,1,0:T(8,128)(2,1)}, bf16[8,64,256]{2,1,0:T(8,128)(2,1)}) custom-call(bf16[256,256]{1,0:T(8,128)(2,1)} %constant_dynamic-slice_fusion.forward_ref, bf16[256,64,128]{2,1,0:T(8,128)(2,1)} %get-tuple-element.11.matrix_ref, ...), custom_call_target="tpu_custom_call" | custom-call | flops 4294967296 | bytes 16777216 | tf_op jit(solution)/shard_map/field/pallas_call | solution.py:189
  72.6 5.4 %collective-permute-start.13 = (bf16[8,64,256]{2,1,0:T(8,128)(2,1)}, bf16[8,64,256]{2,1,0:T(8,128)(2,1)S(1)}, u32[]{:S(2)}, u32[]{:S(2)}) collective-permute-start(bf16[8,64,256]{2,1,0:T(8,128)(2,1)} %get-tuple-element.14), channel_id=1, source_target_pairs={{0,1},{1,2},{2,3},{3,0},{4,5},{5,6},{6,7},{7,4},{8,9},{9,10},{10,1... | collective-permute-start | bytes 786440 | tf_op jit(solution)/shard_map/ppermute | solution.py:231
  78.1 4.0 %collective-permute-start.14 = (bf16[8,64,256]{2,1,0:T(8,128)(2,1)}, bf16[8,64,256]{2,1,0:T(8,128)(2,1)S(1)}, u32[]{:S(2)}, u32[]{:S(2)}) collective-permute-start(bf16[8,64,256]{2,1,0:T(8,128)(2,1)} %get-tuple-element.15), channel_id=1, source_target_pairs={{0,2},{1,3},{2,0},{3,1},{4,6},{5,7},{6,4},{7,5},{8,10},{9,11},{10,... | collective-permute-start | bytes 786440 | tf_op jit(solution)/shard_map/ppermute | solution.py:231
  82.1 5.0 %collective-permute-done.13 = bf16[8,64,256]{2,1,0:T(8,128)(2,1)S(1)} collective-permute-done((bf16[8,64,256]{2,1,0:T(8,128)(2,1)}, bf16[8,64,256]{2,1,0:T(8,128)(2,1)S(1)}, u32[]{:S(2)}, u32[]{:S(2)}) %collective-permute-start.13) | collective-permute-done | bytes 262176 | tf_op jit(solution)/shard_map/ppermute | solution.py:231
  87.0 12.7 %collective-permute-done.14 = bf16[8,64,256]{2,1,0:T(8,128)(2,1)S(1)} collective-permute-done((bf16[8,64,256]{2,1,0:T(8,128)(2,1)}, bf16[8,64,256]{2,1,0:T(8,128)(2,1)S(1)}, u32[]{:S(2)}, u32[]{:S(2)}) %collective-permute-start.14) | collective-permute-done | bytes 262176 | tf_op jit(solution)/shard_map/ppermute | solution.py:231
  99.7 3.5 %collective-permute-done.15 = bf16[8,64,256]{2,1,0:T(8,128)(2,1)S(1)} collective-permute-done((bf16[8,64,256]{2,1,0:T(8,128)(2,1)}, bf16[8,64,256]{2,1,0:T(8,128)(2,1)S(1)}, u32[]{:S(2)}, u32[]{:S(2)}) %collective-permute-start.15) | collective-permute-done | bytes 262176 | tf_op jit(solution)/shard_map/ppermute | solution.py:231
  103.2 2.0 %add_select_fusion = f32[8,64,256]{2,1,0:T(8,128)} fusion(bf16[8,64,256]{2,1,0:T(8,128)(2,1)S(1)} %collective-permute-done.15, bf16[8,64,256]{2,1,0:T(8,128)(2,1)S(1)} %collective-permute-done.14, f32[8,64,256]{2,1,0:T(8,128)} %get-tuple-element.13, bf16[8,64,256]{2,1,0:T(8,128)(2,1)S(1)} %collective-permute-done.13, pred[8,256]{1,0:T(8,128)(4,1)S(1)} %broadcast_compare_fusion), kind=kLoop, calls=%fused_computation.5 | loop fusion | flops 917504 | bytes 1837056 | tf_op jit(solution)/shard_map/jit(_where)/select_n | solution.py:208
  (67 shorter events, 12.8 us)
Async XLA Ops:
  0.0 27.0 %copy-start.5 = (bf16[256,8]{0,1:T(8,128)(2,1)S(1)}, bf16[256,8]{0,1:T(8,128)(2,1)}, u32[]{:S(2)}) copy-start(bf16[256,8]{0,1:T(8,128)(2,1)} %param.16) | copy-start | bytes 12292
  0.0 21.1 %copy-start.1 = (bf16[316,2,256]{2,1,0:T(2,128)(2,1)S(1)}, bf16[316,2,256]{2,1,0:T(2,128)(2,1)}, u32[]{:S(2)}) copy-start(bf16[316,2,256]{2,1,0:T(2,128)(2,1)} %param.14) | copy-start | bytes 970756
  1.8 57.4 %copy-start = (bf16[8,64,256]{2,1,0:T(8,128)(2,1)}, bf16[8,64,256]{2,1,0:T(8,128)(2,1)S(1)}, u32[]{:S(2)}) copy-start(bf16[8,64,256]{2,1,0:T(8,128)(2,1)S(1)} %broadcast_select_fusion.refs_0_) | copy-start | bytes 786436
  1.8 28.4 %collective-permute-start.9 = (bf16[8,64,256]{2,1,0:T(8,128)(2,1)S(1)}, bf16[8,64,256]{2,1,0:T(8,128)(2,1)S(1)}, u32[]{:S(2)}, u32[]{:S(2)}) collective-permute-start(bf16[8,64,256]{2,1,0:T(8,128)(2,1)S(1)} %broadcast_select_fusion.refs_0_), channel_id=1, source_target_pairs={{4,0},{8,4},{12,8},{16,12},{20,16},{24,20},{28,24},{5,1},{9,5},{13... | collective-permute-start | bytes 786440 | tf_op jit(solution)/shard_map/ppermute | solution.py:235
  4.4 33.9 %collective-permute-start.5 = (bf16[8,64,256]{2,1,0:T(8,128)(2,1)S(1)}, bf16[8,64,256]{2,1,0:T(8,128)(2,1)S(1)}, u32[]{:S(2)}, u32[]{:S(2)}) collective-permute-start(bf16[8,64,256]{2,1,0:T(8,128)(2,1)S(1)} %broadcast_select_fusion.refs_0_), channel_id=1, source_target_pairs={{0,4},{4,8},{8,12},{12,16},{16,20},{20,24},{24,28},{1,5},{5,9},{9,... | collective-permute-start | bytes 786440 | tf_op jit(solution)/shard_map/ppermute | solution.py:235
  8.3 19.4 %collective-permute-start.4 = (bf16[8,64,256]{2,1,0:T(8,128)(2,1)S(1)}, bf16[8,64,256]{2,1,0:T(8,128)(2,1)S(1)}, u32[]{:S(2)}, u32[]{:S(2)}) collective-permute-start(bf16[8,64,256]{2,1,0:T(8,128)(2,1)S(1)} %broadcast_select_fusion.refs_0_), channel_id=1, source_target_pairs={{0,3},{1,0},{2,1},{3,2},{4,7},{5,4},{6,5},{7,6},{8,11},{9,8},{10,9... | collective-permute-start | bytes 786440 | tf_op jit(solution)/shard_map/ppermute | solution.py:231
  10.0 12.6 %collective-permute-start = (bf16[8,16]{0,1:T(8,128)(2,1)S(1)}, bf16[8,16]{0,1:T(8,128)(2,1)S(1)}, u32[]{:S(2)}, u32[]{:S(2)}) collective-permute-start(bf16[8,16]{0,1:T(8,128)(2,1)S(1)} %get-tuple-element.19), channel_id=1, source_target_pairs={{0,1},{1,2},{2,3},{3,0},{4,5},{5,6},{6,7},{7,4},{8,9},{9,10},{10,1... | collective-permute-start | bytes 776 | tf_op jit(solution)/shard_map/ppermute | solution.py:231
  11.3 13.3 %collective-permute-start.1 = (bf16[8,16]{0,1:T(8,128)(2,1)S(1)}, bf16[8,16]{0,1:T(8,128)(2,1)S(1)}, u32[]{:S(2)}, u32[]{:S(2)}) collective-permute-start(bf16[8,16]{0,1:T(8,128)(2,1)S(1)} %get-tuple-element.20), channel_id=1, source_target_pairs={{0,3},{1,0},{2,1},{3,2},{4,7},{5,4},{6,5},{7,6},{8,11},{9,8},{10,9... | collective-permute-start | bytes 776 | tf_op jit(solution)/shard_map/ppermute | solution.py:231
  22.5 13.9 %collective-permute-start.3 = (bf16[8,64,256]{2,1,0:T(8,128)(2,1)S(1)}, bf16[8,64,256]{2,1,0:T(8,128)(2,1)S(1)}, u32[]{:S(2)}, u32[]{:S(2)}) collective-permute-start(bf16[8,64,256]{2,1,0:T(8,128)(2,1)S(1)} %broadcast_select_fusion.refs_0_), channel_id=1, source_target_pairs={{0,2},{1,3},{2,0},{3,1},{4,6},{5,7},{6,4},{7,5},{8,10},{9,11},{10,... | collective-permute-start | bytes 786440 | tf_op jit(solution)/shard_map/ppermute | solution.py:231
  24.6 18.3 %collective-permute-start.2 = (bf16[8,64,256]{2,1,0:T(8,128)(2,1)S(1)}, bf16[8,64,256]{2,1,0:T(8,128)(2,1)S(1)}, u32[]{:S(2)}, u32[]{:S(2)}) collective-permute-start(bf16[8,64,256]{2,1,0:T(8,128)(2,1)S(1)} %broadcast_select_fusion.refs_0_), channel_id=1, source_target_pairs={{0,1},{1,2},{2,3},{3,0},{4,5},{5,6},{6,7},{7,4},{8,9},{9,10},{10,1... | collective-permute-start | bytes 786440 | tf_op jit(solution)/shard_map/ppermute | solution.py:231
  27.7 31.5 %copy-start.2 = (bf16[8,64,256]{2,1,0:T(8,128)(2,1)}, bf16[8,64,256]{2,1,0:T(8,128)(2,1)S(1)}, u32[]{:S(2)}) copy-start(bf16[8,64,256]{2,1,0:T(8,128)(2,1)S(1)} %collective-permute-done.4.refs_3_) | copy-start | bytes 786436
  27.7 17.2 %collective-permute-start.12 = (bf16[8,64,256]{2,1,0:T(8,128)(2,1)S(1)}, bf16[8,64,256]{2,1,0:T(8,128)(2,1)S(1)}, u32[]{:S(2)}, u32[]{:S(2)}) collective-permute-start(bf16[8,64,256]{2,1,0:T(8,128)(2,1)S(1)} %collective-permute-done.4.refs_3_), channel_id=1, source_target_pairs={{4,0},{8,4},{12,8},{16,12},{20,16},{24,20},{28,24},{5,1},{9,5},{13... | collective-permute-start | bytes 786440 | tf_op jit(solution)/shard_map/ppermute | solution.py:235
  30.2 28.9 %copy-start.6 = (bf16[8,64,256]{2,1,0:T(8,128)(2,1)}, bf16[8,64,256]{2,1,0:T(8,128)(2,1)S(1)}, u32[]{:S(2)}) copy-start(bf16[8,64,256]{2,1,0:T(8,128)(2,1)S(1)} %collective-permute-done.9.refs_4_) | copy-start | bytes 786436
  30.2 32.6 %collective-permute-start.8 = (bf16[8,64,256]{2,1,0:T(8,128)(2,1)S(1)}, bf16[8,64,256]{2,1,0:T(8,128)(2,1)S(1)}, u32[]{:S(2)}, u32[]{:S(2)}) collective-permute-start(bf16[8,64,256]{2,1,0:T(8,128)(2,1)S(1)} %collective-permute-done.4.refs_3_), channel_id=1, source_target_pairs={{0,4},{4,8},{8,12},{12,16},{16,20},{20,24},{24,28},{1,5},{5,9},{9,... | collective-permute-start | bytes 786440 | tf_op jit(solution)/shard_map/ppermute | solution.py:235
  36.4 22.7 %copy-start.3 = (bf16[8,64,256]{2,1,0:T(8,128)(2,1)}, bf16[8,64,256]{2,1,0:T(8,128)(2,1)S(1)}, u32[]{:S(2)}) copy-start(bf16[8,64,256]{2,1,0:T(8,128)(2,1)S(1)} %collective-permute-done.3.refs_2_) | copy-start | bytes 786436
  36.4 26.4 %collective-permute-start.11 = (bf16[8,64,256]{2,1,0:T(8,128)(2,1)S(1)}, bf16[8,64,256]{2,1,0:T(8,128)(2,1)S(1)}, u32[]{:S(2)}, u32[]{:S(2)}) collective-permute-start(bf16[8,64,256]{2,1,0:T(8,128)(2,1)S(1)} %collective-permute-done.3.refs_2_), channel_id=1, source_target_pairs={{4,0},{8,4},{12,8},{16,12},{20,16},{24,20},{28,24},{5,1},{9,5},{13... | collective-permute-start | bytes 786440 | tf_op jit(solution)/shard_map/ppermute | solution.py:235
  38.3 20.8 %copy-start.7 = (bf16[8,64,256]{2,1,0:T(8,128)(2,1)}, bf16[8,64,256]{2,1,0:T(8,128)(2,1)S(1)}, u32[]{:S(2)}) copy-start(bf16[8,64,256]{2,1,0:T(8,128)(2,1)S(1)} %collective-permute-done.5.refs_0_) | copy-start | bytes 786436
  38.3 24.5 %collective-permute-start.7 = (bf16[8,64,256]{2,1,0:T(8,128)(2,1)S(1)}, bf16[8,64,256]{2,1,0:T(8,128)(2,1)S(1)}, u32[]{:S(2)}, u32[]{:S(2)}) collective-permute-start(bf16[8,64,256]{2,1,0:T(8,128)(2,1)S(1)} %collective-permute-done.3.refs_2_), channel_id=1, source_target_pairs={{0,4},{4,8},{8,12},{12,16},{16,20},{20,24},{24,28},{1,5},{5,9},{9,... | collective-permute-start | bytes 786440 | tf_op jit(solution)/shard_map/ppermute | solution.py:235
  42.9 16.3 %copy-start.4 = (bf16[8,64,256]{2,1,0:T(8,128)(2,1)}, bf16[8,64,256]{2,1,0:T(8,128)(2,1)S(1)}, u32[]{:S(2)}) copy-start(bf16[8,64,256]{2,1,0:T(8,128)(2,1)S(1)} %collective-permute-done.2.refs_1_) | copy-start | bytes 786436
  42.9 19.9 %collective-permute-start.10 = (bf16[8,64,256]{2,1,0:T(8,128)(2,1)S(1)}, bf16[8,64,256]{2,1,0:T(8,128)(2,1)S(1)}, u32[]{:S(2)}, u32[]{:S(2)}) collective-permute-start(bf16[8,64,256]{2,1,0:T(8,128)(2,1)S(1)} %collective-permute-done.2.refs_1_), channel_id=1, source_target_pairs={{4,0},{8,4},{12,8},{16,12},{20,16},{24,20},{28,24},{5,1},{9,5},{13... | collective-permute-start | bytes 786440 | tf_op jit(solution)/shard_map/ppermute | solution.py:235
  44.8 18.0 %collective-permute-start.6 = (bf16[8,64,256]{2,1,0:T(8,128)(2,1)S(1)}, bf16[8,64,256]{2,1,0:T(8,128)(2,1)S(1)}, u32[]{:S(2)}, u32[]{:S(2)}) collective-permute-start(bf16[8,64,256]{2,1,0:T(8,128)(2,1)S(1)} %collective-permute-done.2.refs_1_), channel_id=1, source_target_pairs={{0,4},{4,8},{8,12},{12,16},{16,20},{20,24},{24,28},{1,5},{5,9},{9,... | collective-permute-start | bytes 786440 | tf_op jit(solution)/shard_map/ppermute | solution.py:235
  72.6 14.4 %collective-permute-start.13 = (bf16[8,64,256]{2,1,0:T(8,128)(2,1)}, bf16[8,64,256]{2,1,0:T(8,128)(2,1)S(1)}, u32[]{:S(2)}, u32[]{:S(2)}) collective-permute-start(bf16[8,64,256]{2,1,0:T(8,128)(2,1)} %get-tuple-element.14), channel_id=1, source_target_pairs={{0,1},{1,2},{2,3},{3,0},{4,5},{5,6},{6,7},{7,4},{8,9},{9,10},{10,1... | collective-permute-start | bytes 786440 | tf_op jit(solution)/shard_map/ppermute | solution.py:231
  78.1 21.6 %collective-permute-start.14 = (bf16[8,64,256]{2,1,0:T(8,128)(2,1)}, bf16[8,64,256]{2,1,0:T(8,128)(2,1)S(1)}, u32[]{:S(2)}, u32[]{:S(2)}) collective-permute-start(bf16[8,64,256]{2,1,0:T(8,128)(2,1)} %get-tuple-element.15), channel_id=1, source_target_pairs={{0,2},{1,3},{2,0},{3,1},{4,6},{5,7},{6,4},{7,5},{8,10},{9,11},{10,... | collective-permute-start | bytes 786440 | tf_op jit(solution)/shard_map/ppermute | solution.py:231
  82.1 21.2 %collective-permute-start.15 = (bf16[8,64,256]{2,1,0:T(8,128)(2,1)}, bf16[8,64,256]{2,1,0:T(8,128)(2,1)S(1)}, u32[]{:S(2)}, u32[]{:S(2)}) collective-permute-start(bf16[8,64,256]{2,1,0:T(8,128)(2,1)} %get-tuple-element.16), channel_id=1, source_target_pairs={{0,3},{1,0},{2,1},{3,2},{4,7},{5,4},{6,5},{7,6},{8,11},{9,8},{10,9... | collective-permute-start | bytes 786440 | tf_op jit(solution)/shard_map/ppermute | solution.py:231
  (6 other events, 18.9 us)

commit v3 on v2

v3 whole, which is shorter than its diff:
```python
import functools

import jax
import jax.numpy as jnp
from jax import lax
from jax.experimental import pallas as pl
from jax.experimental.pallas import tpu as pltpu
from jax.sharding import PartitionSpec as P

RIM = 8
LANES = 128
BF = jnp.bfloat16
F32 = jnp.float32
I32 = jnp.int32
NT = (((1,), (1,)), ((), ()))
TN = (((0,), (0,)), ((), ()))
NN = (((1,), (0,)), ((), ()))
VMEM = pl.BlockSpec(memory_space=pltpu.VMEM)
SMEM = pl.BlockSpec(memory_space=pltpu.SMEM)


def round_up(value, unit):
    return -(-value // unit) * unit


def dot(a, b, dims):
    return lax.dot_general(a, b, dims, preferred_element_type=F32)


def cost(flops, nbytes):
    return pl.CostEstimate(flops=int(flops), bytes_accessed=int(nbytes), transcendentals=0)


def count_of(shape, axis):
    return lax.broadcasted_iota(I32, shape, axis)


def as_bf16(mask):
    return mask.astype(F32).astype(BF)


def unrolled(trips, most, step):
    size = next(n for n in range(min(most, trips), 0, -1) if trips % n == 0)

    def block(i, carry):
        for j in range(size):
            step(i * size + j)
        return carry

    lax.fori_loop(0, trips // size, block, 0)


def prepare_kernel(rim, all_dirs, place_ref, live_ref, stencil_ref, weight_ref, box_ref, out_ref, point_ref):
    boxes, incid, width = box_ref.shape
    points, dirs = stencil_ref.shape
    unk = count_of((incid, width), 1)
    unk = jnp.where(unk < width // 2, unk, unk - width // 2)
    for b in range(boxes):
        kept = jnp.where(unk < live_ref[b], box_ref[b].astype(F32), 0.0)
        out_ref[b * incid : (b + 1) * incid, :] = kept.astype(BF)
    away = stencil_ref[...] - (count_of((points, dirs), 1) + place_ref[0] * dirs)
    away = jnp.where(away > all_dirs // 2, away - all_dirs, away)
    away = jnp.where(away < -(all_dirs // 2), away + all_dirs, away)
    rows = jnp.concatenate([away.astype(F32), weight_ref[...].astype(F32)], axis=0)
    point_ref[...] = rows
    source, target = count_of((dirs, width), 0), count_of((dirs, width), 1)
    head = (target < rim) & (source == target)
    tail = (target >= rim) & (target < 2 * rim) & (source == target + dirs - 2 * rim)
    out_ref[boxes * incid :, :] = dot(rows.astype(BF), as_bf16(head | tail), NN).astype(BF)


def prepare(place, live_counts, stencil, weights, currents, all_dirs):
    boxes, incid, width = currents.shape
    points, dirs = stencil.shape
    return pl.pallas_call(
        functools.partial(prepare_kernel, RIM, all_dirs),
        out_shape=(
            jax.ShapeDtypeStruct((boxes * incid + 2 * points, width), BF),
            jax.ShapeDtypeStruct((2 * points, dirs), F32),
        ),
        in_specs=[SMEM, SMEM, VMEM, VMEM, VMEM],
        out_specs=(VMEM, VMEM),
        cost_estimate=cost(1 << 20, 1 << 20),
        name="prepare",
    )(place, live_counts, stencil, weights, currents)


def transfer_kernel(first, per, slots, place_ref, source_ref, kind_ref, table_ref, matrix_ref, lists, table, wide):
    all_boxes, width = source_ref.shape
    dirs, rows, window = matrix_ref.shape
    boxes = rows // 2
    kinds = table_ref.shape[0]
    padded = table.shape[1]
    own_dir, own_group = place_ref[0], place_ref[1]

    local = source_ref[...] - (own_group - 1) * all_boxes
    group = (local >= all_boxes).astype(I32) + (local >= 2 * all_boxes).astype(I32)
    inside = local - group * all_boxes
    holder = jnp.zeros_like(inside)
    for j in range(1, slots):
        holder += (inside >= j * per).astype(I32)
    paired = jnp.where(own_group % 2 == 0, 2, 0)
    turn = jnp.where(group == 1, 0, jnp.where(group == paired, 2, 1))
    spot = turn * all_boxes + (own_dir ^ holder) * per + inside - holder * per
    lists[...] = jnp.full(lists.shape, -1, I32)
    lists[:all_boxes, :width] = spot
    lists[all_boxes:, :width] = kind_ref[...]

    fill = jnp.zeros((padded - kinds, dirs), BF)
    for c in range(2):
        part = jnp.concatenate([table_ref[:, c, :], fill], axis=0)
        table[c * dirs : (c + 1) * dirs, :] = part.T

    lanes = lists.shape[1]

    def two_boxes(step):
        counts = []
        for i in range(2):
            at = first + 2 * step + i
            row = (own_dir ^ (at // per)) * per + at % per
            hit_kind = count_of((padded, lanes), 0) == lists[pl.ds(all_boxes + row, 1), :]
            hit_source = count_of((window, lanes), 0) == lists[pl.ds(row, 1), :]
            counts.append(dot(as_bf16(hit_kind), as_bf16(hit_source), NT))
        counts = jnp.concatenate(counts, axis=1).astype(BF)
        entries = dot(table[...], counts, NN)
        for i in range(2):
            for c in range(window // LANES):
                part = entries[:, i * window + c * LANES : i * window + (c + 1) * LANES]
                at = 2 * step + i
                wide[c, pl.ds(at, dirs, stride=rows + 1), :] = part[:dirs]
                wide[c, pl.ds(at + boxes, dirs, stride=rows + 1), :] = part[dirs:]

    unrolled(boxes // 2, 4, two_boxes)

    def narrow(k):
        for c in range(window // LANES):
            part = wide[c, pl.ds(k * (rows + 1), rows), :]
            matrix_ref[k, :, c * LANES : (c + 1) * LANES] = part.astype(BF)

    unrolled(dirs, 16, narrow)


def transfer(place, sources, operator_ids, translators, first, boxes, per, window):
    kinds, _, dirs = translators.shape
    all_boxes, width = sources.shape
    padded = round_up(kinds, LANES)
    return pl.pallas_call(
        functools.partial(transfer_kernel, first, per, all_boxes // per),
        out_shape=jax.ShapeDtypeStruct((dirs, 2 * boxes, window), BF),
        in_specs=[SMEM, VMEM, VMEM, VMEM],
        out_specs=VMEM,
        scratch_shapes=[
            pltpu.VMEM((2 * all_boxes, round_up(width, LANES)), I32),
            pltpu.VMEM((2 * dirs, padded), BF),
            pltpu.VMEM((window // LANES, dirs * (2 * boxes + 1), LANES), F32),
        ],
        cost_estimate=cost(8 << 30, 4 << 20),
        name="transfer",
    )(place, sources, operator_ids, translators)


def rotated(box):
    half = box.shape[1] // 2
    re, im = box[:, :half], box[:, half:]
    return jnp.concatenate(
        [jnp.concatenate([re, -im], axis=1), jnp.concatenate([im, re], axis=1)], axis=0
    )


def radiate(forward, box_refs, incid, out, stride):
    dirs = forward.shape[0]
    at = 0
    for ref in box_refs:
        for row in range(0, ref.shape[0] // incid * incid, 2 * incid):
            both = [rotated(ref[i : i + incid, :]) for i in (row, row + incid)]
            field = dot(forward[...], jnp.concatenate(both, axis=0), NT)
            out[pl.ds(at, dirs, stride=stride), :] = field[:, : 2 * incid]
            out[pl.ds(at + 1, dirs, stride=stride), :] = field[:, 2 * incid :]
            at += 2


def pattern_kernel(
    count, incid, rim, place_ref, forward_ref, receive_ref, after_ref, before_ref, point_ref, *refs
):
    box_refs, (pattern_ref, turned_ref, folded_ref, wide) = refs[:count], refs[count:]
    dirs, boxes, _ = pattern_ref.shape
    turned_ref[...] = jnp.concatenate([forward_ref[:, 0, :], forward_ref[:, 1, :]], axis=1)
    radiate(turned_ref, box_refs, incid, wide, boxes + 1)

    def narrow(k):
        pattern_ref[k] = wide[pl.ds(k * (boxes + 1), boxes), :].astype(BF)

    unrolled(dirs, 16, narrow)

    own_dir = place_ref[0]
    points = point_ref.shape[0] // 2
    lane = count_of((2 * points, LANES), 1)
    ends = jnp.zeros((2 * points, LANES), F32)
    for j, ref in enumerate(box_refs):
        tail = ref[ref.shape[0] - 2 * points :, :LANES].astype(F32)
        holder = own_dir ^ j
        follows = holder == lax.rem(own_dir + 1, count)
        leads = holder == lax.rem(own_dir + count - 1, count)
        here = ((lane < rim) & follows) | ((lane >= rim) & (lane < 2 * rim) & leads)
        ends = jnp.where(here, tail, ends)
    spot = count_of((points, LANES), 1)
    spot = jnp.where(spot < rim, spot + dirs, spot - 2 * rim)
    spots = [point_ref[:points, :].astype(I32) + count_of((points, dirs), 1)]
    spots.append(ends[:points].astype(I32) + spot)
    gains = [point_ref[points:, :], ends[points:]]
    tables = [receive_ref[...], jnp.concatenate([after_ref[...], before_ref[...]], axis=0)]
    folded = None
    for spot, gain, table in zip(spots, gains, tables):
        extent = spot.shape[1]
        own = count_of((dirs, extent), 0)
        spread = jnp.zeros((dirs, extent), F32)
        for p in range(points):
            spread += jnp.where(own == spot[p : p + 1, :], gain[p : p + 1, :], 0.0)
        flat = jnp.concatenate([table[:, 0, :], table[:, 1, :]], axis=1)
        if flat.shape[0] < extent:
            blank = jnp.zeros((extent - flat.shape[0], flat.shape[1]), BF)
            flat = jnp.concatenate([flat, blank], axis=0)
        part = dot(spread.astype(BF), flat, NN)
        folded = part if folded is None else folded + part
    folded_ref[...] = folded.astype(BF)


def own_pattern(place, radiation, receiving, rows, shards, incid, dirs):
    count = len(shards)
    boxes = sum(s.shape[0] // incid for s in shards)
    all_dirs, parts, unk = receiving.shape
    own = pl.BlockSpec((dirs, parts, unk), lambda i, at: (at[0], 0, 0))
    rims, total = dirs // RIM, all_dirs // RIM
    after = pl.BlockSpec((RIM, parts, unk), lambda i, at: (lax.rem((at[0] + 1) * rims, total), 0, 0))
    before = pl.BlockSpec(
        (RIM, parts, unk), lambda i, at: (lax.rem(at[0] * rims + total - 1, total), 0, 0)
    )
    return pl.pallas_call(
        functools.partial(pattern_kernel, count, incid, RIM),
        out_shape=(
            jax.ShapeDtypeStruct((dirs, boxes, 2 * incid), BF),
            jax.ShapeDtypeStruct((dirs, parts * unk), BF),
            jax.ShapeDtypeStruct((dirs, parts * unk), BF),
        ),
        grid_spec=pltpu.PrefetchScalarGridSpec(
            num_scalar_prefetch=1,
            grid=(1,),
            in_specs=[own, own, after, before] + [VMEM] * (1 + count),
            out_specs=(VMEM, VMEM, VMEM),
            scratch_shapes=[pltpu.VMEM((dirs * (boxes + 1), 2 * incid), F32)],
        ),
        cost_estimate=cost(1 << 30, 4 << 20),
        name="pattern",
    )(place, radiation, receiving, receiving, receiving, rows, *shards)


def field_kernel(count, halves, forward_ref, folded_ref, own_ref, *refs):
    matrix_refs, refs = refs[:halves], refs[halves:]
    box_refs, out_refs, (near, moved) = refs[: -count - 2], refs[-count - 2 : -2], refs[-2:]
    dirs, own_boxes, width = own_ref.shape
    near_boxes = 2 * own_boxes
    boxes = matrix_refs[0].shape[1] // 2
    half = width // 2
    radiate(forward_ref, box_refs, half, near, near_boxes + 1)
    sign = jnp.where(count_of((boxes, width), 1) < half, -1.0, 1.0).astype(F32)
    stride = own_boxes + 1

    def translate(k):
        around = near[pl.ds(k * (near_boxes + 1), near_boxes), :].astype(BF)
        fields = jnp.concatenate([own_ref[k], around], axis=0)
        weights = [ref[k][:, : own_boxes + near_boxes] for ref in matrix_refs]
        both = dot(jnp.concatenate(weights, axis=0), fields, NN)
        for h in range(halves):
            part = both[2 * boxes * h : 2 * boxes * (h + 1)]
            turned = pltpu.roll(part[boxes:], half, 1)
            moved[pl.ds(k * stride + h * boxes, boxes), :] = part[:boxes] + sign * turned

    unrolled(dirs, 64 * 32 // own_boxes, translate)

    unk = folded_ref.shape[1] // 2
    per = own_boxes // count
    for j, out_ref in enumerate(out_refs):
        for i in range(per):
            field = moved[pl.ds(j * per + i, dirs, stride=stride), :].astype(BF)
            full = dot(field, folded_ref[...], TN)
            re = full[:half, :unk] - full[half:, unk:]
            im = full[:half, unk:] + full[half:, :unk]
            out_ref[i] = jnp.concatenate([re, im], axis=1).astype(out_ref.dtype)


def receive_field(forward, folded, own, matrices, near, kinds):
    count = len(kinds)
    dirs, boxes, width = own.shape
    return pl.pallas_call(
        functools.partial(field_kernel, count, len(matrices)),
        out_shape=tuple(
            jax.ShapeDtypeStruct((boxes // count, width // 2, folded.shape[1]), kind)
            for kind in kinds
        ),
        in_specs=[VMEM] * (3 + len(matrices) + len(near)),
        out_specs=(VMEM,) * count,
        scratch_shapes=[
            pltpu.VMEM((dirs * (2 * boxes + 1), width), F32),
            pltpu.VMEM((dirs * (boxes + 1), width), F32),
        ],
        cost_estimate=cost(4 << 30, 16 << 20),
        name="field",
    )(forward, folded, own, *matrices, *near)


def mask_rows(values, live_counts):
    column = jnp.arange(values.shape[-1], dtype=I32) % (values.shape[-1] // 2)
    keep = column[None, None, :] < live_counts[:, None, None]
    return jnp.where(keep, values, jnp.zeros_like(values))


def body(
    currents,
    live_counts,
    radiation,
    sources,
    operator_ids,
    translators,
    stencil,
    stencil_weights,
    receiving,
):
    n_dir, n_grp = lax.axis_size("dir"), lax.axis_size("grp")
    dirs = translators.shape[2]
    per, incid, _ = currents.shape
    boxes = n_dir * per
    window = round_up(3 * boxes, LANES)
    place = jnp.stack([lax.axis_index("dir"), lax.axis_index("grp")]).astype(I32)

    def swap(values, bit):
        return lax.ppermute(values, "dir", [(i, i ^ bit) for i in range(n_dir)])

    def pair(values, odd):
        pairs = [(i, i + 1) for i in range(odd, n_grp - 1, 2)]
        return lax.ppermute(values, "grp", pairs + [(b, a) for a, b in pairs])

    shard, points = prepare(
        place, live_counts, stencil.T, stencil_weights.T, currents, radiation.shape[0]
    )
    slots = {0: shard}
    bit = n_dir // 2
    while bit:
        for j in sorted(slots):
            slots[j + bit] = swap(slots[j], bit)
        bit //= 2
    shards = [slots[j] for j in range(n_dir)]
    far = [pair(s, 1) for s in shards]
    near = [pair(s, 0) for s in shards]

    half = boxes // 2
    matrices = [
        transfer(place, sources, operator_ids, translators, first, half, per, window)
        for first in (0, half)
    ]
    own, forward, folded = own_pattern(place, radiation, receiving, points, shards, incid, dirs)
    kinds = [BF if j & 1 else F32 for j in range(n_dir)]
    parts = receive_field(forward, folded, own, matrices, far + near, kinds)
    sums = dict(enumerate(parts))
    bit = 1
    while bit < n_dir:
        for j in sorted((j for j in sums if j & bit), reverse=True):
            sums[j ^ bit] = sums[j ^ bit] + swap(sums.pop(j).astype(BF), bit).astype(F32)
        bit *= 2
    return mask_rows(sums[0], live_counts)


def solution(mesh):
    placed = (
        P(("grp", "dir"), None, None),
        P(("grp", "dir")),
        P(),
        P("grp", None),
        P("grp", None),
        P(None, None, "dir"),
        P("dir", None),
        P("dir", None),
        P(),
    )
    return jax.shard_map(
        body,
        mesh=mesh,
        in_specs=placed,
        out_specs=P(("grp", "dir"), None, None),
        check_vma=False,
    )
```

time: 106 us -> 83.3 us (0.79)
  the two profiles are of different devices: /device:TPU:11 before, /device:TPU:2 now
where the time goes in v3:
time: 83.3 us; the launch traced here: 82.9 us
  Pallas kernels  27.5 us (33%)
  waiting for transfers between devices  27 us (32%)
  starting transfers between devices  23.5 us (28%)
  other arithmetic  3.78 us (5%)
  local copies, waits for them, and re-layouts  1.05 us (1%)
    ppermute x6, waiting for transfers between devices, swap(): return lax.ppermute(values, 'dir', [(i, i ^ bit) for i in range(n_dir)])  27 us
    ppermute x8, starting transfers between devices, pair(): return lax.ppermute(values, 'grp', pairs + [(b, a) for a, b in pairs])  13.3 us
    pallas_call x2, Pallas kernels, transfer(): pl.pallas_call(functools.partial(transfer_kernel, first, per, all_boxes /...  12.1 us
    ppermute x6, starting transfers between devices, swap(): return lax.ppermute(values, 'dir', [(i, i ^ bit) for i in range(n_dir)])  10.2 us
    pallas_call x1, Pallas kernels, receive_field(): pl.pallas_call(functools.partial(field_kernel, count, len(matrices)), out...  8.76 us
    pallas_call x1, Pallas kernels, own_pattern(): pl.pallas_call(functools.partial(pattern_kernel, count, incid, RIM), out_...  4.71 us
    select_n x1, other arithmetic, mask_rows(): return jnp.where(keep, values, jnp.zeros_like(values))  1.93 us
    pallas_call x1, Pallas kernels, prepare(): pl.pallas_call(functools.partial(prepare_kernel, RIM, all_dirs), out_shap...  1.88 us
  transfers between devices with their start and end apart: 14, of which 4 were waited for; matrix products, arithmetic and copies ran while one was open for 1% of the time, Pallas kernels for 20%

profile of v3, /device:TPU:2, one launch (start us, length us, event | category | flops | bytes accessed | tf_op | source)
XLA Modules:
  0.0 82.9 jit_solution(12993044204450672827)
XLA Ops:
  0.7 1.9 %prepare.1 = (bf16[528,256]{1,0:T(8,128)(2,1)}, f32[16,256]{1,0:T(8,128)}) custom-call(s32[2]{0:T(128)} %pad_add_fusion.place_ref, s32[8]{0:T(128)} %live_ref.1, s32[8,256]{1,0:T(8,128)} %bitcast.4, bf16[8,256]{1,0:T(8,128)(2,1)} %bitcast.5, bf16[8,64,256]{2,1,0:T(8,128)(2,1)} %box_ref.1), custom_call_target="tpu_custom_call" | custom-call | flops 1048576 | bytes 1048576 | tf_op jit(solution)/shard_map/prepare/pallas_call | solution.py:75
  2.5 2.6 %collective-permute-start.1 = (bf16[528,256]{1,0:T(8,128)(2,1)}, bf16[528,256]{1,0:T(8,128)(2,1)S(1)}, u32[]{:S(2)}, u32[]{:S(2)}) collective-permute-start(bf16[528,256]{1,0:T(8,128)(2,1)} %get-tuple-element.15.refs_0_), channel_id=1, source_target_pairs={{0,2},{1,3},{2,0},{3,1},{4,6},{5,7},{6,4},{7,5},{8,10},{9,11},{10,... | collective-permute-start | bytes 811016 | tf_op jit(solution)/shard_map/ppermute | solution.py:336
  5.1 1.6 %collective-permute-start = (bf16[528,256]{1,0:T(8,128)(2,1)}, bf16[528,256]{1,0:T(8,128)(2,1)S(1)}, u32[]{:S(2)}, u32[]{:S(2)}) collective-permute-start(bf16[528,256]{1,0:T(8,128)(2,1)} %get-tuple-element.15.refs_0_), channel_id=1, source_target_pairs={{0,1},{1,0},{2,3},{3,2},{4,5},{5,4},{6,7},{7,6},{8,9},{9,8},{10,11... | collective-permute-start | bytes 811016 | tf_op jit(solution)/shard_map/ppermute | solution.py:336
  6.7 1.9 %collective-permute-start.3 = (bf16[528,256]{1,0:T(8,128)(2,1)}, bf16[528,256]{1,0:T(8,128)(2,1)S(1)}, u32[]{:S(2)}, u32[]{:S(2)}) collective-permute-start(bf16[528,256]{1,0:T(8,128)(2,1)} %get-tuple-element.15.refs_0_), channel_id=1, source_target_pairs={{4,8},{12,16},{20,24},{8,4},{16,12},{24,20},{5,9},{13,17},{21,25},... | collective-permute-start | bytes 811016 | tf_op jit(solution)/shard_map/ppermute | solution.py:340
  8.6 1.7 %collective-permute-start.7 = (bf16[528,256]{1,0:T(8,128)(2,1)}, bf16[528,256]{1,0:T(8,128)(2,1)S(1)}, u32[]{:S(2)}, u32[]{:S(2)}) collective-permute-start(bf16[528,256]{1,0:T(8,128)(2,1)} %get-tuple-element.15.refs_0_), channel_id=1, source_target_pairs={{0,4},{8,12},{16,20},{24,28},{4,0},{12,8},{20,16},{28,24},{1,5},{9... | collective-permute-start | bytes 811016 | tf_op jit(solution)/shard_map/ppermute | solution.py:340
  10.3 7.5 %collective-permute-done.1.refs_2_ = bf16[528,256]{1,0:T(8,128)(2,1)S(1)} collective-permute-done((bf16[528,256]{1,0:T(8,128)(2,1)}, bf16[528,256]{1,0:T(8,128)(2,1)S(1)}, u32[]{:S(2)}, u32[]{:S(2)}) %collective-permute-start.1) | collective-permute-done | bytes 270368 | tf_op jit(solution)/shard_map/ppermute | solution.py:336
  17.8 0.7 collective-permute-start.2
  18.4 1.9 %collective-permute-start.5 = (bf16[528,256]{1,0:T(8,128)(2,1)S(1)}, bf16[528,256]{1,0:T(8,128)(2,1)S(1)}, u32[]{:S(2)}, u32[]{:S(2)}) collective-permute-start(bf16[528,256]{1,0:T(8,128)(2,1)S(1)} %collective-permute-done.1.refs_2_), channel_id=1, source_target_pairs={{4,8},{12,16},{20,24},{8,4},{16,12},{24,20},{5,9},{13,17},{21,25},... | collective-permute-start | bytes 811016 | tf_op jit(solution)/shard_map/ppermute | solution.py:340
  20.4 6.1 %transfer.2.refs_0_ = bf16[256,32,128]{2,1,0:T(8,128)(2,1)} custom-call(s32[2]{0:T(128)} %pad_add_fusion.place_ref, s32[32,189]{1,0:T(8,128)} %source_ref.3, s32[32,189]{1,0:T(8,128)} %kind_ref.3, bf16[316,2,256]{2,1,0:T(2,128)(2,1)} %table_ref.3), custom_call_target="tpu_custom_call" | custom-call | flops 8589934592 | bytes 4194304 | tf_op jit(solution)/shard_map/transfer/pallas_call | solution.py:147
  26.4 1.7 %collective-permute-start.9 = (bf16[528,256]{1,0:T(8,128)(2,1)S(1)}, bf16[528,256]{1,0:T(8,128)(2,1)S(1)}, u32[]{:S(2)}, u32[]{:S(2)}) collective-permute-start(bf16[528,256]{1,0:T(8,128)(2,1)S(1)} %collective-permute-done.1.refs_2_), channel_id=1, source_target_pairs={{0,4},{8,12},{16,20},{24,28},{4,0},{12,8},{20,16},{28,24},{1,5},{9... | collective-permute-start | bytes 811016 | tf_op jit(solution)/shard_map/ppermute | solution.py:340
  28.1 2.1 %collective-permute-start.4 = (bf16[528,256]{1,0:T(8,128)(2,1)S(1)}, bf16[528,256]{1,0:T(8,128)(2,1)S(1)}, u32[]{:S(2)}, u32[]{:S(2)}) collective-permute-start(bf16[528,256]{1,0:T(8,128)(2,1)S(1)} %collective-permute-done.refs_1_), channel_id=1, source_target_pairs={{4,8},{12,16},{20,24},{8,4},{16,12},{24,20},{5,9},{13,17},{21,25},... | collective-permute-start | bytes 811016 | tf_op jit(solution)/shard_map/ppermute | solution.py:340
  30.2 1.5 %collective-permute-start.8 = (bf16[528,256]{1,0:T(8,128)(2,1)S(1)}, bf16[528,256]{1,0:T(8,128)(2,1)S(1)}, u32[]{:S(2)}, u32[]{:S(2)}) collective-permute-start(bf16[528,256]{1,0:T(8,128)(2,1)S(1)} %collective-permute-done.refs_1_), channel_id=1, source_target_pairs={{0,4},{8,12},{16,20},{24,28},{4,0},{12,8},{20,16},{28,24},{1,5},{9... | collective-permute-start | bytes 811016 | tf_op jit(solution)/shard_map/ppermute | solution.py:340
  31.8 2.5 %collective-permute-start.6 = (bf16[528,256]{1,0:T(8,128)(2,1)S(1)}, bf16[528,256]{1,0:T(8,128)(2,1)S(1)}, u32[]{:S(2)}, u32[]{:S(2)}) collective-permute-start(bf16[528,256]{1,0:T(8,128)(2,1)S(1)} %collective-permute-done.2.refs_3_), channel_id=1, source_target_pairs={{4,8},{12,16},{20,24},{8,4},{16,12},{24,20},{5,9},{13,17},{21,25},... | collective-permute-start | bytes 811016 | tf_op jit(solution)/shard_map/ppermute | solution.py:340
  34.3 6.1 %transfer.3.refs_1_ = bf16[256,32,128]{2,1,0:T(8,128)(2,1)} custom-call(s32[2]{0:T(128)} %pad_add_fusion.place_ref, s32[32,189]{1,0:T(8,128)} %source_ref.3, s32[32,189]{1,0:T(8,128)} %kind_ref.3, bf16[316,2,256]{2,1,0:T(2,128)(2,1)} %table_ref.3), custom_call_target="tpu_custom_call" | custom-call | flops 8589934592 | bytes 4194304 | tf_op jit(solution)/shard_map/transfer/pallas_call | solution.py:147
  40.4 4.7 %pattern.1 = (bf16[256,32,128]{2,1,0:T(8,128)(2,1)}, bf16[256,256]{1,0:T(8,128)(2,1)}, bf16[256,256]{1,0:T(8,128)(2,1)}) custom-call(s32[2]{0:T(128)} %pad_add_fusion.place_ref, bf16[1024,2,128]{2,1,0:T(2,128)(2,1)} %forward_ref.1, bf16[1024,2,128]{2,1,0:T(2,128)(2,1)} %before_ref.1, bf16[1024,2,128]{2,1,0:T(2,128)(2,1)} %before_ref.1, ...), custom_call_target="tpu_custom_call" | custom-call | flops 1073741824 | bytes 4194304 | tf_op jit(solution)/shard_map/pattern/pallas_call | solution.py:238
  46.2 8.8 %field.1 = (f32[8,64,256]{2,1,0:T(8,128)}, bf16[8,64,256]{2,1,0:T(8,128)(2,1)}, f32[8,64,256]{2,1,0:T(8,128)}, bf16[8,64,256]{2,1,0:T(8,128)(2,1)}) custom-call(bf16[256,256]{1,0:T(8,128)(2,1)} %get-tuple-element.16.forward_ref, bf16[256,256]{1,0:T(8,128)(2,1)} %get-tuple-element.17.folded_ref, bf16[256,32,128]{2,1,0:T(8,128)(2,1)} %get-tuple-element.18.own_ref, ...), custom_call_target="tpu_custom_call" | custom-call | flops 4294967296 | bytes 16777216 | tf_op jit(solution)/shard_map/field/pallas_call | solution.py:294
  55.0 1.3 %collective-permute-start.12 = (bf16[8,64,256]{2,1,0:T(8,128)(2,1)}, bf16[8,64,256]{2,1,0:T(8,128)(2,1)S(1)}, u32[]{:S(2)}, u32[]{:S(2)}) collective-permute-start(bf16[8,64,256]{2,1,0:T(8,128)(2,1)} %get-tuple-element.22), channel_id=1, source_target_pairs={{0,1},{1,0},{2,3},{3,2},{4,5},{5,4},{6,7},{7,6},{8,9},{9,8},{10,11... | collective-permute-start | bytes 786440 | tf_op jit(solution)/shard_map/ppermute | solution.py:336
  56.3 0.7 collective-permute-start.11
  57.0 7.4 %collective-permute-done.12 = bf16[8,64,256]{2,1,0:T(8,128)(2,1)S(1)} collective-permute-done((bf16[8,64,256]{2,1,0:T(8,128)(2,1)}, bf16[8,64,256]{2,1,0:T(8,128)(2,1)S(1)}, u32[]{:S(2)}, u32[]{:S(2)}) %collective-permute-start.12) | collective-permute-done | bytes 262176 | tf_op jit(solution)/shard_map/ppermute | solution.py:336
  64.4 1.1 %add_convert_fusion = bf16[8,64,256]{2,1,0:T(8,128)(2,1)S(1)} fusion(f32[8,64,256]{2,1,0:T(8,128)} %get-tuple-element.21, bf16[8,64,256]{2,1,0:T(8,128)(2,1)S(1)} %collective-permute-done.12), kind=kLoop, calls=%fused_computation.1 | loop fusion | flops 393216 | bytes 1048576 | tf_op jit(solution)/shard_map/convert_element_type | solution.py:367
  65.5 3.3 %collective-permute-start.13 = (bf16[8,64,256]{2,1,0:T(8,128)(2,1)S(1)}, bf16[8,64,256]{2,1,0:T(8,128)(2,1)S(1)}, u32[]{:S(2)}, u32[]{:S(2)}) collective-permute-start(bf16[8,64,256]{2,1,0:T(8,128)(2,1)S(1)} %add_convert_fusion), channel_id=1, source_target_pairs={{0,2},{1,3},{2,0},{3,1},{4,6},{5,7},{6,4},{7,5},{8,10},{9,11},{10,... | collective-permute-start | bytes 786440 | tf_op jit(solution)/shard_map/ppermute | solution.py:336
  68.9 4.1 %collective-permute-done.11 = bf16[8,64,256]{2,1,0:T(8,128)(2,1)S(1)} collective-permute-done((bf16[8,64,256]{2,1,0:T(8,128)(2,1)}, bf16[8,64,256]{2,1,0:T(8,128)(2,1)S(1)}, u32[]{:S(2)}, u32[]{:S(2)}) %collective-permute-start.11) | collective-permute-done | bytes 262176 | tf_op jit(solution)/shard_map/ppermute | solution.py:336
  72.9 8.1 %collective-permute-done.13 = bf16[8,64,256]{2,1,0:T(8,128)(2,1)S(1)} collective-permute-done((bf16[8,64,256]{2,1,0:T(8,128)(2,1)S(1)}, bf16[8,64,256]{2,1,0:T(8,128)(2,1)S(1)}, u32[]{:S(2)}, u32[]{:S(2)}) %collective-permute-start.13) | collective-permute-done | bytes 262176 | tf_op jit(solution)/shard_map/ppermute | solution.py:336
  81.0 1.9 %add_select_fusion = f32[8,64,256]{2,1,0:T(8,128)} fusion(bf16[8,64,256]{2,1,0:T(8,128)(2,1)S(1)} %collective-permute-done.13, f32[8,64,256]{2,1,0:T(8,128)} %get-tuple-element.19, bf16[8,64,256]{2,1,0:T(8,128)(2,1)S(1)} %collective-permute-done.11, pred[8,256]{1,0:T(8,128)(4,1)S(1)} %broadcast_compare_fusion), kind=kLoop, calls=%fused_computation | loop fusion | flops 655360 | bytes 1574912 | tf_op jit(solution)/shard_map/jit(_where)/select_n | solution.py:314
  (38 shorter events, 1.9 us)
Async XLA Ops:
  2.5 15.2 %collective-permute-start.1 = (bf16[528,256]{1,0:T(8,128)(2,1)}, bf16[528,256]{1,0:T(8,128)(2,1)S(1)}, u32[]{:S(2)}, u32[]{:S(2)}) collective-permute-start(bf16[528,256]{1,0:T(8,128)(2,1)} %get-tuple-element.15.refs_0_), channel_id=1, source_target_pairs={{0,2},{1,3},{2,0},{3,1},{4,6},{5,7},{6,4},{7,5},{8,10},{9,11},{10,... | collective-permute-start | bytes 811016 | tf_op jit(solution)/shard_map/ppermute | solution.py:336
  5.1 21.3 %collective-permute-start = (bf16[528,256]{1,0:T(8,128)(2,1)}, bf16[528,256]{1,0:T(8,128)(2,1)S(1)}, u32[]{:S(2)}, u32[]{:S(2)}) collective-permute-start(bf16[528,256]{1,0:T(8,128)(2,1)} %get-tuple-element.15.refs_0_), channel_id=1, source_target_pairs={{0,1},{1,0},{2,3},{3,2},{4,5},{5,4},{6,7},{7,6},{8,9},{9,8},{10,11... | collective-permute-start | bytes 811016 | tf_op jit(solution)/shard_map/ppermute | solution.py:336
  6.7 21.4 %collective-permute-start.3 = (bf16[528,256]{1,0:T(8,128)(2,1)}, bf16[528,256]{1,0:T(8,128)(2,1)S(1)}, u32[]{:S(2)}, u32[]{:S(2)}) collective-permute-start(bf16[528,256]{1,0:T(8,128)(2,1)} %get-tuple-element.15.refs_0_), channel_id=1, source_target_pairs={{4,8},{12,16},{20,24},{8,4},{16,12},{24,20},{5,9},{13,17},{21,25},... | collective-permute-start | bytes 811016 | tf_op jit(solution)/shard_map/ppermute | solution.py:340
  8.6 21.6 %collective-permute-start.7 = (bf16[528,256]{1,0:T(8,128)(2,1)}, bf16[528,256]{1,0:T(8,128)(2,1)S(1)}, u32[]{:S(2)}, u32[]{:S(2)}) collective-permute-start(bf16[528,256]{1,0:T(8,128)(2,1)} %get-tuple-element.15.refs_0_), channel_id=1, source_target_pairs={{0,4},{8,12},{16,20},{24,28},{4,0},{12,8},{20,16},{28,24},{1,5},{9... | collective-permute-start | bytes 811016 | tf_op jit(solution)/shard_map/ppermute | solution.py:340
  17.8 8.7 %copy-start.5 = (bf16[528,256]{1,0:T(8,128)(2,1)}, bf16[528,256]{1,0:T(8,128)(2,1)S(1)}, u32[]{:S(2)}) copy-start(bf16[528,256]{1,0:T(8,128)(2,1)S(1)} %collective-permute-done.1.refs_2_) | copy-start | bytes 811012
  17.8 13.9 %collective-permute-start.2 = (bf16[528,256]{1,0:T(8,128)(2,1)S(1)}, bf16[528,256]{1,0:T(8,128)(2,1)S(1)}, u32[]{:S(2)}, u32[]{:S(2)}) collective-permute-start(bf16[528,256]{1,0:T(8,128)(2,1)S(1)} %collective-permute-done.1.refs_2_), channel_id=1, source_target_pairs={{0,1},{1,0},{2,3},{3,2},{4,5},{5,4},{6,7},{7,6},{8,9},{9,8},{10,11... | collective-permute-start | bytes 811016 | tf_op jit(solution)/shard_map/ppermute | solution.py:336
  18.4 13.4 %collective-permute-start.5 = (bf16[528,256]{1,0:T(8,128)(2,1)S(1)}, bf16[528,256]{1,0:T(8,128)(2,1)S(1)}, u32[]{:S(2)}, u32[]{:S(2)}) collective-permute-start(bf16[528,256]{1,0:T(8,128)(2,1)S(1)} %collective-permute-done.1.refs_2_), channel_id=1, source_target_pairs={{4,8},{12,16},{20,24},{8,4},{16,12},{24,20},{5,9},{13,17},{21,25},... | collective-permute-start | bytes 811016 | tf_op jit(solution)/shard_map/ppermute | solution.py:340
  26.4 13.9 %copy-start.3 = (bf16[528,256]{1,0:T(8,128)(2,1)}, bf16[528,256]{1,0:T(8,128)(2,1)S(1)}, u32[]{:S(2)}) copy-start(bf16[528,256]{1,0:T(8,128)(2,1)S(1)} %collective-permute-done.refs_1_) | copy-start | bytes 811012
  26.4 18.7 %collective-permute-start.9 = (bf16[528,256]{1,0:T(8,128)(2,1)S(1)}, bf16[528,256]{1,0:T(8,128)(2,1)S(1)}, u32[]{:S(2)}, u32[]{:S(2)}) collective-permute-start(bf16[528,256]{1,0:T(8,128)(2,1)S(1)} %collective-permute-done.1.refs_2_), channel_id=1, source_target_pairs={{0,4},{8,12},{16,20},{24,28},{4,0},{12,8},{20,16},{28,24},{1,5},{9... | collective-permute-start | bytes 811016 | tf_op jit(solution)/shard_map/ppermute | solution.py:340
  28.1 12.2 %copy-start.1 = (bf16[528,256]{1,0:T(8,128)(2,1)}, bf16[528,256]{1,0:T(8,128)(2,1)S(1)}, u32[]{:S(2)}) copy-start(bf16[528,256]{1,0:T(8,128)(2,1)S(1)} %collective-permute-done.3.refs_2_) | copy-start | bytes 811012
  28.1 17.0 %collective-permute-start.4 = (bf16[528,256]{1,0:T(8,128)(2,1)S(1)}, bf16[528,256]{1,0:T(8,128)(2,1)S(1)}, u32[]{:S(2)}, u32[]{:S(2)}) collective-permute-start(bf16[528,256]{1,0:T(8,128)(2,1)S(1)} %collective-permute-done.refs_1_), channel_id=1, source_target_pairs={{4,8},{12,16},{20,24},{8,4},{16,12},{24,20},{5,9},{13,17},{21,25},... | collective-permute-start | bytes 811016 | tf_op jit(solution)/shard_map/ppermute | solution.py:340
  30.2 10.2 %copy-start.2 = (bf16[528,256]{1,0:T(8,128)(2,1)}, bf16[528,256]{1,0:T(8,128)(2,1)S(1)}, u32[]{:S(2)}) copy-start(bf16[528,256]{1,0:T(8,128)(2,1)S(1)} %collective-permute-done.7.refs_6_) | copy-start | bytes 811012
  30.2 14.9 %collective-permute-start.8 = (bf16[528,256]{1,0:T(8,128)(2,1)S(1)}, bf16[528,256]{1,0:T(8,128)(2,1)S(1)}, u32[]{:S(2)}, u32[]{:S(2)}) collective-permute-start(bf16[528,256]{1,0:T(8,128)(2,1)S(1)} %collective-permute-done.refs_1_), channel_id=1, source_target_pairs={{0,4},{8,12},{16,20},{24,28},{4,0},{12,8},{20,16},{28,24},{1,5},{9... | collective-permute-start | bytes 811016 | tf_op jit(solution)/shard_map/ppermute | solution.py:340
  31.7 8.6 %copy-start.7 = (bf16[528,256]{1,0:T(8,128)(2,1)}, bf16[528,256]{1,0:T(8,128)(2,1)S(1)}, u32[]{:S(2)}) copy-start(bf16[528,256]{1,0:T(8,128)(2,1)S(1)} %collective-permute-done.2.refs_3_) | copy-start | bytes 811012
  31.7 13.4 %collective-permute-start.10 = (bf16[528,256]{1,0:T(8,128)(2,1)S(1)}, bf16[528,256]{1,0:T(8,128)(2,1)S(1)}, u32[]{:S(2)}, u32[]{:S(2)}) collective-permute-start(bf16[528,256]{1,0:T(8,128)(2,1)S(1)} %collective-permute-done.2.refs_3_), channel_id=1, source_target_pairs={{0,4},{8,12},{16,20},{24,28},{4,0},{12,8},{20,16},{28,24},{1,5},{9... | collective-permute-start | bytes 811016 | tf_op jit(solution)/shard_map/ppermute | solution.py:340
  31.8 8.6 %copy-start.4 = (bf16[528,256]{1,0:T(8,128)(2,1)}, bf16[528,256]{1,0:T(8,128)(2,1)S(1)}, u32[]{:S(2)}) copy-start(bf16[528,256]{1,0:T(8,128)(2,1)S(1)} %collective-permute-done.5.refs_4_) | copy-start | bytes 811012
  31.8 13.4 %collective-permute-start.6 = (bf16[528,256]{1,0:T(8,128)(2,1)S(1)}, bf16[528,256]{1,0:T(8,128)(2,1)S(1)}, u32[]{:S(2)}, u32[]{:S(2)}) collective-permute-start(bf16[528,256]{1,0:T(8,128)(2,1)S(1)} %collective-permute-done.2.refs_3_), channel_id=1, source_target_pairs={{4,8},{12,16},{20,24},{8,4},{16,12},{24,20},{5,9},{13,17},{21,25},... | collective-permute-start | bytes 811016 | tf_op jit(solution)/shard_map/ppermute | solution.py:340
  45.1 0.9 %copy-start.9 = (bf16[528,256]{1,0:T(8,128)(2,1)}, bf16[528,256]{1,0:T(8,128)(2,1)S(1)}, u32[]{:S(2)}) copy-start(bf16[528,256]{1,0:T(8,128)(2,1)S(1)} %collective-permute-done.8.refs_7_) | copy-start | bytes 811012
  45.2 0.9 %copy-start.10 = (bf16[528,256]{1,0:T(8,128)(2,1)}, bf16[528,256]{1,0:T(8,128)(2,1)S(1)}, u32[]{:S(2)}) copy-start(bf16[528,256]{1,0:T(8,128)(2,1)S(1)} %collective-permute-done.10.refs_9_) | copy-start | bytes 811012
  45.2 1.0 %copy-start.11 = (bf16[528,256]{1,0:T(8,128)(2,1)}, bf16[528,256]{1,0:T(8,128)(2,1)S(1)}, u32[]{:S(2)}) copy-start(bf16[528,256]{1,0:T(8,128)(2,1)S(1)} %collective-permute-done.6.refs_5_) | copy-start | bytes 811012
  46.2 22.6 %copy-start = (s32[8]{0:T(128)S(1)}, s32[8]{0:T(128)}, u32[]{:S(2)}) copy-start(s32[8]{0:T(128)} %live_ref.1) | copy-start | bytes 100
  55.0 9.4 %collective-permute-start.12 = (bf16[8,64,256]{2,1,0:T(8,128)(2,1)}, bf16[8,64,256]{2,1,0:T(8,128)(2,1)S(1)}, u32[]{:S(2)}, u32[]{:S(2)}) collective-permute-start(bf16[8,64,256]{2,1,0:T(8,128)(2,1)} %get-tuple-element.22), channel_id=1, source_target_pairs={{0,1},{1,0},{2,3},{3,2},{4,5},{5,4},{6,7},{7,6},{8,9},{9,8},{10,11... | collective-permute-start | bytes 786440 | tf_op jit(solution)/shard_map/ppermute | solution.py:336
  56.3 16.6 %collective-permute-start.11 = (bf16[8,64,256]{2,1,0:T(8,128)(2,1)}, bf16[8,64,256]{2,1,0:T(8,128)(2,1)S(1)}, u32[]{:S(2)}, u32[]{:S(2)}) collective-permute-start(bf16[8,64,256]{2,1,0:T(8,128)(2,1)} %get-tuple-element.20), channel_id=1, source_target_pairs={{0,1},{1,0},{2,3},{3,2},{4,5},{5,4},{6,7},{7,6},{8,9},{9,8},{10,11... | collective-permute-start | bytes 786440 | tf_op jit(solution)/shard_map/ppermute | solution.py:336
  65.5 15.5 %collective-permute-start.13 = (bf16[8,64,256]{2,1,0:T(8,128)(2,1)S(1)}, bf16[8,64,256]{2,1,0:T(8,128)(2,1)S(1)}, u32[]{:S(2)}, u32[]{:S(2)}) collective-permute-start(bf16[8,64,256]{2,1,0:T(8,128)(2,1)S(1)} %add_convert_fusion), channel_id=1, source_target_pairs={{0,2},{1,3},{2,0},{3,1},{4,6},{5,7},{6,4},{7,5},{8,10},{9,11},{10,... | collective-permute-start | bytes 786440 | tf_op jit(solution)/shard_map/ppermute | solution.py:336
  (2 other events, 1.5 us)

commit v4 on v3

--- a/solution.py
+++ b/solution.py
@@ -1,4 +1,5 @@
 import functools
+import math
 
 import jax
 import jax.numpy as jnp
@@ -29,6 +30,14 @@
 
 def cost(flops, nbytes):
     return pl.CostEstimate(flops=int(flops), bytes_accessed=int(nbytes), transcendentals=0)
+
+
+def grant(*groups):
+    size = 4 << 20
+    for group in groups:
+        for item in group:
+            size += math.prod(item.shape) * jnp.dtype(item.dtype).itemsize
+    return pltpu.CompilerParams(vmem_limit_bytes=min(size, 60 * 1024 * 1024))
 
 
 def count_of(shape, axis):
@@ -144,16 +153,19 @@
     kinds, _, dirs = translators.shape
     all_boxes, width = sources.shape
     padded = round_up(kinds, LANES)
+    out_shape = jax.ShapeDtypeStruct((dirs, 2 * boxes, window), BF)
+    scratch = [
+        pltpu.VMEM((2 * all_boxes, round_up(width, LANES)), I32),
+        pltpu.VMEM((2 * dirs, padded), BF),
+        pltpu.VMEM((window // LANES, dirs * (2 * boxes + 1), LANES), F32),
+    ]
     return pl.pallas_call(
         functools.partial(transfer_kernel, first, per, all_boxes // per),
-        out_shape=jax.ShapeDtypeStruct((dirs, 2 * boxes, window), BF),
+        out_shape=out_shape,
         in_specs=[SMEM, VMEM, VMEM, VMEM],
         out_specs=VMEM,
-        scratch_shapes=[
-            pltpu.VMEM((2 * all_boxes, round_up(width, LANES)), I32),
-            pltpu.VMEM((2 * dirs, padded), BF),
-            pltpu.VMEM((window // LANES, dirs * (2 * boxes + 1), LANES), F32),
-        ],
+        scratch_shapes=scratch,
+        compiler_params=grant(scratch, [out_shape, translators, translators]),
         cost_estimate=cost(8 << 30, 4 << 20),
         name="transfer",
     )(place, sources, operator_ids, translators)
@@ -235,20 +247,23 @@
     before = pl.BlockSpec(
         (RIM, parts, unk), lambda i, at: (lax.rem(at[0] * rims + total - 1, total), 0, 0)
     )
+    out_shape = (
+        jax.ShapeDtypeStruct((dirs, boxes, 2 * incid), BF),
+        jax.ShapeDtypeStruct((dirs, parts * unk), BF),
+        jax.ShapeDtypeStruct((dirs, parts * unk), BF),
+    )
+    scratch = [pltpu.VMEM((dirs * (boxes + 1), 2 * incid), F32)]
     return pl.pallas_call(
         functools.partial(pattern_kernel, count, incid, RIM),
-        out_shape=(
-            jax.ShapeDtypeStruct((dirs, boxes, 2 * incid), BF),
-            jax.ShapeDtypeStruct((dirs, parts * unk), BF),
-            jax.ShapeDtypeStruct((dirs, parts * unk), BF),
-        ),
+        out_shape=out_shape,
         grid_spec=pltpu.PrefetchScalarGridSpec(
             num_scalar_prefetch=1,
             grid=(1,),
             in_specs=[own, own, after, before] + [VMEM] * (1 + count),
             out_specs=(VMEM, VMEM, VMEM),
-            scratch_shapes=[pltpu.VMEM((dirs * (boxes + 1), 2 * incid), F32)],
+            scratch_shapes=scratch,
         ),
+        compiler_params=grant(scratch, out_shape, out_shape, shards, shards),
         cost_estimate=cost(1 << 30, 4 << 20),
         name="pattern",
     )(place, radiation, receiving, receiving, receiving, rows, *shards)
@@ -291,18 +306,20 @@
 def receive_field(forward, folded, own, matrices, near, kinds):
     count = len(kinds)
     dirs, boxes, width = own.shape
+    out_shape = tuple(
+        jax.ShapeDtypeStruct((boxes // count, width // 2, folded.shape[1]), kind) for kind in kinds
+    )
+    scratch = [
+        pltpu.VMEM((dirs * (2 * boxes + 1), width), F32),
+        pltpu.VMEM((dirs * (boxes + 1), width), F32),
+    ]
     return pl.pallas_call(
         functools.partial(field_kernel, count, len(matrices)),
-        out_shape=tuple(
-            jax.ShapeDtypeStruct((boxes // count, width // 2, folded.shape[1]), kind)
-            for kind in kinds
-        ),
+        out_shape=out_shape,
         in_specs=[VMEM] * (3 + len(matrices) + len(near)),
         out_specs=(VMEM,) * count,
-        scratch_shapes=[
-            pltpu.VMEM((dirs * (2 * boxes + 1), width), F32),
-            pltpu.VMEM((dirs * (boxes + 1), width), F32),
-        ],
+        scratch_shapes=scratch,
+        compiler_params=grant(scratch, out_shape, [forward, folded, own], matrices, near),
         cost_estimate=cost(4 << 30, 16 << 20),
         name="field",
     )(forward, folded, own, *matrices, *near)

time: 83.3 us -> 74.4 us (0.89)
  Pallas kernels: 27.5 us -> 17.4 us
  local copies, waits for them, and re-layouts: 1.05 us -> 3.17 us
  other arithmetic: 3.78 us -> 1.68 us
    pallas_call x1, Pallas kernels: 8.76 us -> 4.55 us  [receive_field(): pl.pallas_call(functools.partial(field_kernel, count, len(matrices)), out...]
    pallas_call x2, Pallas kernels: 12.1 us -> 8.45 us  [transfer(): pl.pallas_call(functools.partial(transfer_kernel, first, per, all_boxes /...]
    pallas_call x1, Pallas kernels: 4.71 us -> 2.57 us  [own_pattern(): pl.pallas_call(functools.partial(pattern_kernel, count, incid, RIM), out_...]
    unnamed x24 -> x20, local copies, waits for them, and re-layouts: 1.05 us -> 3.17 us
    ppermute x8, waiting for transfers between devices: 0.02 us -> 1.21 us  [pair(): return lax.ppermute(values, 'grp', pairs + [(b, a) for a, b in pairs])]
    select_n x1, other arithmetic: 1.93 us -> 0.89 us  [mask_rows(): return jnp.where(keep, values, jnp.zeros_like(values))]
    convert_element_type x1, other arithmetic: 1.11 us -> 0.07 us  [body(): sums.pop(j).astype(BF)]
  transfers between devices with their start and end apart: 14 -> 14, of which waited for: 4 -> 5; matrix products, arithmetic and copies ran while one was open for 1% -> 0% of each run, Pallas kernels for 20% -> 15%
where the time goes in v4:
time: 74.4 us; the launch traced here: 73.4 us
  waiting for transfers between devices  27.4 us (37%)
  starting transfers between devices  23.5 us (32%)
  Pallas kernels  17.4 us (23%)
  local copies, waits for them, and re-layouts  3.17 us (4%)
  other arithmetic  1.68 us (2%)
    ppermute x6, waiting for transfers between devices, swap(): return lax.ppermute(values, 'dir', [(i, i ^ bit) for i in range(n_dir)])  26.2 us
    ppermute x8, starting transfers between devices, pair(): return lax.ppermute(values, 'grp', pairs + [(b, a) for a, b in pairs])  13.3 us
    ppermute x6, starting transfers between devices, swap(): return lax.ppermute(values, 'dir', [(i, i ^ bit) for i in range(n_dir)])  10.3 us
    pallas_call x2, Pallas kernels, transfer(): pl.pallas_call(functools.partial(transfer_kernel, first, per, all_boxes /...  8.45 us
    pallas_call x1, Pallas kernels, receive_field(): pl.pallas_call(functools.partial(field_kernel, count, len(matrices)), out...  4.55 us
    unnamed x20, local copies, waits for them, and re-layouts  3.17 us
    pallas_call x1, Pallas kernels, own_pattern(): pl.pallas_call(functools.partial(pattern_kernel, count, incid, RIM), out_...  2.57 us
    pallas_call x1, Pallas kernels, prepare(): pl.pallas_call(functools.partial(prepare_kernel, RIM, all_dirs), out_shap...  1.88 us
  transfers between devices with their start and end apart: 14, of which 5 were waited for; matrix products, arithmetic and copies ran while one was open for 0% of the time, Pallas kernels for 15%

profile of v4, /device:TPU:2, one launch (start us, length us, event | category | flops | bytes accessed | tf_op | source)
XLA Modules:
  0.0 73.4 jit_solution(14707425355662119725)
XLA Ops:
  0.6 1.9 %prepare.1 = (bf16[528,256]{1,0:T(8,128)(2,1)}, f32[16,256]{1,0:T(8,128)}) custom-call(s32[2]{0:T(128)} %pad_add_fusion.place_ref, s32[8]{0:T(128)} %live_ref.1, s32[8,256]{1,0:T(8,128)} %bitcast.4, bf16[8,256]{1,0:T(8,128)(2,1)} %bitcast.5, bf16[8,64,256]{2,1,0:T(8,128)(2,1)} %box_ref.1), custom_call_target="tpu_custom_call" | custom-call | flops 1048576 | bytes 1048576 | tf_op jit(solution)/shard_map/prepare/pallas_call | solution.py:84
  2.5 2.6 %collective-permute-start.1 = (bf16[528,256]{1,0:T(8,128)(2,1)}, bf16[528,256]{1,0:T(8,128)(2,1)S(1)}, u32[]{:S(2)}, u32[]{:S(2)}) collective-permute-start(bf16[528,256]{1,0:T(8,128)(2,1)} %get-tuple-element.15.refs_0_), channel_id=1, source_target_pairs={{0,2},{1,3},{2,0},{3,1},{4,6},{5,7},{6,4},{7,5},{8,10},{9,11},{10,... | collective-permute-start | bytes 811016 | tf_op jit(solution)/shard_map/ppermute | solution.py:353
  5.1 1.6 %collective-permute-start = (bf16[528,256]{1,0:T(8,128)(2,1)}, bf16[528,256]{1,0:T(8,128)(2,1)S(1)}, u32[]{:S(2)}, u32[]{:S(2)}) collective-permute-start(bf16[528,256]{1,0:T(8,128)(2,1)} %get-tuple-element.15.refs_0_), channel_id=1, source_target_pairs={{0,1},{1,0},{2,3},{3,2},{4,5},{5,4},{6,7},{7,6},{8,9},{9,8},{10,11... | collective-permute-start | bytes 811016 | tf_op jit(solution)/shard_map/ppermute | solution.py:353
  6.7 1.9 %collective-permute-start.3 = (bf16[528,256]{1,0:T(8,128)(2,1)}, bf16[528,256]{1,0:T(8,128)(2,1)S(1)}, u32[]{:S(2)}, u32[]{:S(2)}) collective-permute-start(bf16[528,256]{1,0:T(8,128)(2,1)} %get-tuple-element.15.refs_0_), channel_id=1, source_target_pairs={{4,8},{12,16},{20,24},{8,4},{16,12},{24,20},{5,9},{13,17},{21,25},... | collective-permute-start | bytes 811016 | tf_op jit(solution)/shard_map/ppermute | solution.py:357
  8.6 1.7 %collective-permute-start.7 = (bf16[528,256]{1,0:T(8,128)(2,1)}, bf16[528,256]{1,0:T(8,128)(2,1)S(1)}, u32[]{:S(2)}, u32[]{:S(2)}) collective-permute-start(bf16[528,256]{1,0:T(8,128)(2,1)} %get-tuple-element.15.refs_0_), channel_id=1, source_target_pairs={{0,4},{8,12},{16,20},{24,28},{4,0},{12,8},{20,16},{28,24},{1,5},{9... | collective-permute-start | bytes 811016 | tf_op jit(solution)/shard_map/ppermute | solution.py:357
  10.3 7.5 %collective-permute-done.1.refs_2_ = bf16[528,256]{1,0:T(8,128)(2,1)S(1)} collective-permute-done((bf16[528,256]{1,0:T(8,128)(2,1)}, bf16[528,256]{1,0:T(8,128)(2,1)S(1)}, u32[]{:S(2)}, u32[]{:S(2)}) %collective-permute-start.1) | collective-permute-done | bytes 270368 | tf_op jit(solution)/shard_map/ppermute | solution.py:353
  18.4 1.9 %collective-permute-start.5 = (bf16[528,256]{1,0:T(8,128)(2,1)S(1)}, bf16[528,256]{1,0:T(8,128)(2,1)S(1)}, u32[]{:S(2)}, u32[]{:S(2)}) collective-permute-start(bf16[528,256]{1,0:T(8,128)(2,1)S(1)} %collective-permute-done.1.refs_2_), channel_id=1, source_target_pairs={{4,8},{12,16},{20,24},{8,4},{16,12},{24,20},{5,9},{13,17},{21,25},... | collective-permute-start | bytes 811016 | tf_op jit(solution)/shard_map/ppermute | solution.py:357
  21.0 1.0 %copy-done.4 = bf16[316,2,256]{2,1,0:T(2,128)(2,1)S(1)} copy-done((bf16[316,2,256]{2,1,0:T(2,128)(2,1)S(1)}, bf16[316,2,256]{2,1,0:T(2,128)(2,1)}, u32[]{:S(2)}) %copy-start.4) | copy-done | bytes 323608
  22.0 0.8 %copy-done.6 = s32[32,189]{1,0:T(8,128)S(1)} copy-done((s32[32,189]{1,0:T(8,128)S(1)}, s32[32,189]{1,0:T(8,128)}, u32[]{:S(2)}) %copy-start.6) | copy-done | bytes 24216
  23.5 4.2 %transfer.2.refs_0_ = bf16[256,32,128]{2,1,0:T(8,128)(2,1)S(1)} custom-call(s32[2]{0:T(128)S(1)} %copy-done, s32[32,189]{1,0:T(8,128)S(1)} %copy-done.6, s32[32,189]{1,0:T(8,128)S(1)} %copy-done.7, bf16[316,2,256]{2,1,0:T(2,128)(2,1)S(1)} %copy-done.4), custom_call_target="tpu_custom_call" | custom-call | flops 8589934592 | bytes 4194304 | tf_op jit(solution)/shard_map/transfer/pallas_call | solution.py:162
  27.8 1.7 %collective-permute-start.9 = (bf16[528,256]{1,0:T(8,128)(2,1)S(1)}, bf16[528,256]{1,0:T(8,128)(2,1)S(1)}, u32[]{:S(2)}, u32[]{:S(2)}) collective-permute-start(bf16[528,256]{1,0:T(8,128)(2,1)S(1)} %collective-permute-done.1.refs_2_), channel_id=1, source_target_pairs={{0,4},{8,12},{16,20},{24,28},{4,0},{12,8},{20,16},{28,24},{1,5},{9... | collective-permute-start | bytes 811016 | tf_op jit(solution)/shard_map/ppermute | solution.py:357
  29.5 2.2 %collective-permute-start.4 = (bf16[528,256]{1,0:T(8,128)(2,1)S(1)}, bf16[528,256]{1,0:T(8,128)(2,1)S(1)}, u32[]{:S(2)}, u32[]{:S(2)}) collective-permute-start(bf16[528,256]{1,0:T(8,128)(2,1)S(1)} %collective-permute-done.refs_1_), channel_id=1, source_target_pairs={{4,8},{12,16},{20,24},{8,4},{16,12},{24,20},{5,9},{13,17},{21,25},... | collective-permute-start | bytes 811016 | tf_op jit(solution)/shard_map/ppermute | solution.py:357
  31.7 1.4 %collective-permute-start.8 = (bf16[528,256]{1,0:T(8,128)(2,1)S(1)}, bf16[528,256]{1,0:T(8,128)(2,1)S(1)}, u32[]{:S(2)}, u32[]{:S(2)}) collective-permute-start(bf16[528,256]{1,0:T(8,128)(2,1)S(1)} %collective-permute-done.refs_1_), channel_id=1, source_target_pairs={{0,4},{8,12},{16,20},{24,28},{4,0},{12,8},{20,16},{28,24},{1,5},{9... | collective-permute-start | bytes 811016 | tf_op jit(solution)/shard_map/ppermute | solution.py:357
  33.1 2.5 %collective-permute-start.6 = (bf16[528,256]{1,0:T(8,128)(2,1)S(1)}, bf16[528,256]{1,0:T(8,128)(2,1)S(1)}, u32[]{:S(2)}, u32[]{:S(2)}) collective-permute-start(bf16[528,256]{1,0:T(8,128)(2,1)S(1)} %collective-permute-done.2.refs_3_), channel_id=1, source_target_pairs={{4,8},{12,16},{20,24},{8,4},{16,12},{24,20},{5,9},{13,17},{21,25},... | collective-permute-start | bytes 811016 | tf_op jit(solution)/shard_map/ppermute | solution.py:357
  35.6 4.2 %transfer.3.refs_1_ = bf16[256,32,128]{2,1,0:T(8,128)(2,1)S(1)} custom-call(s32[2]{0:T(128)S(1)} %copy-done, s32[32,189]{1,0:T(8,128)S(1)} %copy-done.6, s32[32,189]{1,0:T(8,128)S(1)} %copy-done.7, bf16[316,2,256]{2,1,0:T(2,128)(2,1)S(1)} %copy-done.4), custom_call_target="tpu_custom_call" | custom-call | flops 8589934592 | bytes 4194304 | tf_op jit(solution)/shard_map/transfer/pallas_call | solution.py:162
  39.9 2.6 %pattern.1 = (bf16[256,32,128]{2,1,0:T(8,128)(2,1)S(1)}, bf16[256,256]{1,0:T(8,128)(2,1)S(1)}, bf16[256,256]{1,0:T(8,128)(2,1)S(1)}) custom-call(s32[2]{0:T(128)S(1)} %copy-done.1, bf16[1024,2,128]{2,1,0:T(2,128)(2,1)S(1)} %copy-done.2, bf16[1024,2,128]{2,1,0:T(2,128)(2,1)S(1)} %copy-done.3, bf16[1024,2,128]{2,1,0:T(2,128)(2,1)S(1)} %copy-done.3, ...), custom_call_target="tpu_custom_call" | custom-call | flops 1073741824 | bytes 4194304 | tf_op jit(solution)/shard_map/pattern/pallas_call | solution.py:256
  42.5 1.2 %collective-permute-done.6.refs_5_ = bf16[528,256]{1,0:T(8,128)(2,1)S(1)} collective-permute-done((bf16[528,256]{1,0:T(8,128)(2,1)S(1)}, bf16[528,256]{1,0:T(8,128)(2,1)S(1)}, u32[]{:S(2)}, u32[]{:S(2)}) %collective-permute-start.6) | collective-permute-done | bytes 270368 | tf_op jit(solution)/shard_map/ppermute | solution.py:357
  43.7 4.5 %field.1 = (f32[8,64,256]{2,1,0:T(8,128)S(1)}, bf16[8,64,256]{2,1,0:T(8,128)(2,1)S(1)}, f32[8,64,256]{2,1,0:T(8,128)S(1)}, bf16[8,64,256]{2,1,0:T(8,128)(2,1)S(1)}) custom-call(bf16[256,256]{1,0:T(8,128)(2,1)S(1)} %get-tuple-element.16.forward_ref, bf16[256,256]{1,0:T(8,128)(2,1)S(1)} %get-tuple-element.17.folded_ref, ...), custom_call_target="tpu_custom_call" | custom-call | flops 4294967296 | bytes 16777216 | tf_op jit(solution)/shard_map/field/pallas_call | solution.py:316
  48.3 1.4 %collective-permute-start.12 = (bf16[8,64,256]{2,1,0:T(8,128)(2,1)S(1)}, bf16[8,64,256]{2,1,0:T(8,128)(2,1)S(1)}, u32[]{:S(2)}, u32[]{:S(2)}) collective-permute-start(bf16[8,64,256]{2,1,0:T(8,128)(2,1)S(1)} %get-tuple-element.22), channel_id=1, source_target_pairs={{0,1},{1,0},{2,3},{3,2},{4,5},{5,4},{6,7},{7,6},{8,9},{9,8},{10,11... | collective-permute-start | bytes 786440 | tf_op jit(solution)/shard_map/ppermute | solution.py:353
  50.4 6.6 %collective-permute-done.12 = bf16[8,64,256]{2,1,0:T(8,128)(2,1)S(1)} collective-permute-done((bf16[8,64,256]{2,1,0:T(8,128)(2,1)S(1)}, bf16[8,64,256]{2,1,0:T(8,128)(2,1)S(1)}, u32[]{:S(2)}, u32[]{:S(2)}) %collective-permute-start.12) | collective-permute-done | bytes 262176 | tf_op jit(solution)/shard_map/ppermute | solution.py:353
  57.0 3.3 %collective-permute-start.13 = (bf16[8,64,256]{2,1,0:T(8,128)(2,1)S(1)}, bf16[8,64,256]{2,1,0:T(8,128)(2,1)S(1)}, u32[]{:S(2)}, u32[]{:S(2)}) collective-permute-start(bf16[8,64,256]{2,1,0:T(8,128)(2,1)S(1)} %add_convert_fusion), channel_id=1, source_target_pairs={{0,2},{1,3},{2,0},{3,1},{4,6},{5,7},{6,4},{7,5},{8,10},{9,11},{10,... | collective-permute-start | bytes 786440 | tf_op jit(solution)/shard_map/ppermute | solution.py:353
  60.4 6.0 %collective-permute-done.11 = bf16[8,64,256]{2,1,0:T(8,128)(2,1)S(1)} collective-permute-done((bf16[8,64,256]{2,1,0:T(8,128)(2,1)S(1)}, bf16[8,64,256]{2,1,0:T(8,128)(2,1)S(1)}, u32[]{:S(2)}, u32[]{:S(2)}) %collective-permute-start.11) | collective-permute-done | bytes 262176 | tf_op jit(solution)/shard_map/ppermute | solution.py:353
  66.5 6.1 %collective-permute-done.13 = bf16[8,64,256]{2,1,0:T(8,128)(2,1)S(1)} collective-permute-done((bf16[8,64,256]{2,1,0:T(8,128)(2,1)S(1)}, bf16[8,64,256]{2,1,0:T(8,128)(2,1)S(1)}, u32[]{:S(2)}, u32[]{:S(2)}) %collective-permute-start.13) | collective-permute-done | bytes 262176 | tf_op jit(solution)/shard_map/ppermute | solution.py:353
  72.5 0.9 %add_select_fusion = f32[8,64,256]{2,1,0:T(8,128)} fusion(bf16[8,64,256]{2,1,0:T(8,128)(2,1)S(1)} %collective-permute-done.13, f32[8,64,256]{2,1,0:T(8,128)S(1)} %get-tuple-element.19, bf16[8,64,256]{2,1,0:T(8,128)(2,1)S(1)} %collective-permute-done.11, pred[8,256]{1,0:T(8,128)(4,1)S(1)} %broadcast_compare_fusion), kind=kLoop, calls=%fused_computation | loop fusion | flops 655360 | bytes 1574912 | tf_op jit(solution)/shard_map/jit(_where)/select_n | solution.py:331
  (34 shorter events, 3.7 us)
Async XLA Ops:
  2.5 15.2 %collective-permute-start.1 = (bf16[528,256]{1,0:T(8,128)(2,1)}, bf16[528,256]{1,0:T(8,128)(2,1)S(1)}, u32[]{:S(2)}, u32[]{:S(2)}) collective-permute-start(bf16[528,256]{1,0:T(8,128)(2,1)} %get-tuple-element.15.refs_0_), channel_id=1, source_target_pairs={{0,2},{1,3},{2,0},{3,1},{4,6},{5,7},{6,4},{7,5},{8,10},{9,11},{10,... | collective-permute-start | bytes 811016 | tf_op jit(solution)/shard_map/ppermute | solution.py:353
  5.1 22.7 %collective-permute-start = (bf16[528,256]{1,0:T(8,128)(2,1)}, bf16[528,256]{1,0:T(8,128)(2,1)S(1)}, u32[]{:S(2)}, u32[]{:S(2)}) collective-permute-start(bf16[528,256]{1,0:T(8,128)(2,1)} %get-tuple-element.15.refs_0_), channel_id=1, source_target_pairs={{0,1},{1,0},{2,3},{3,2},{4,5},{5,4},{6,7},{7,6},{8,9},{9,8},{10,11... | collective-permute-start | bytes 811016 | tf_op jit(solution)/shard_map/ppermute | solution.py:353
  6.7 22.8 %collective-permute-start.3 = (bf16[528,256]{1,0:T(8,128)(2,1)}, bf16[528,256]{1,0:T(8,128)(2,1)S(1)}, u32[]{:S(2)}, u32[]{:S(2)}) collective-permute-start(bf16[528,256]{1,0:T(8,128)(2,1)} %get-tuple-element.15.refs_0_), channel_id=1, source_target_pairs={{4,8},{12,16},{20,24},{8,4},{16,12},{24,20},{5,9},{13,17},{21,25},... | collective-permute-start | bytes 811016 | tf_op jit(solution)/shard_map/ppermute | solution.py:357
  8.6 23.1 %collective-permute-start.7 = (bf16[528,256]{1,0:T(8,128)(2,1)}, bf16[528,256]{1,0:T(8,128)(2,1)S(1)}, u32[]{:S(2)}, u32[]{:S(2)}) collective-permute-start(bf16[528,256]{1,0:T(8,128)(2,1)} %get-tuple-element.15.refs_0_), channel_id=1, source_target_pairs={{0,4},{8,12},{16,20},{24,28},{4,0},{12,8},{20,16},{28,24},{1,5},{9... | collective-permute-start | bytes 811016 | tf_op jit(solution)/shard_map/ppermute | solution.py:357
  17.8 15.3 %collective-permute-start.2 = (bf16[528,256]{1,0:T(8,128)(2,1)S(1)}, bf16[528,256]{1,0:T(8,128)(2,1)S(1)}, u32[]{:S(2)}, u32[]{:S(2)}) collective-permute-start(bf16[528,256]{1,0:T(8,128)(2,1)S(1)} %collective-permute-done.1.refs_2_), channel_id=1, source_target_pairs={{0,1},{1,0},{2,3},{3,2},{4,5},{5,4},{6,7},{7,6},{8,9},{9,8},{10,11... | collective-permute-start | bytes 811016 | tf_op jit(solution)/shard_map/ppermute | solution.py:353
  18.4 14.7 %collective-permute-start.5 = (bf16[528,256]{1,0:T(8,128)(2,1)S(1)}, bf16[528,256]{1,0:T(8,128)(2,1)S(1)}, u32[]{:S(2)}, u32[]{:S(2)}) collective-permute-start(bf16[528,256]{1,0:T(8,128)(2,1)S(1)} %collective-permute-done.1.refs_2_), channel_id=1, source_target_pairs={{4,8},{12,16},{20,24},{8,4},{16,12},{24,20},{5,9},{13,17},{21,25},... | collective-permute-start | bytes 811016 | tf_op jit(solution)/shard_map/ppermute | solution.py:357
  20.3 0.7 copy-start
  21.0 1.0 %copy-start.4 = (bf16[316,2,256]{2,1,0:T(2,128)(2,1)S(1)}, bf16[316,2,256]{2,1,0:T(2,128)(2,1)}, u32[]{:S(2)}) copy-start(bf16[316,2,256]{2,1,0:T(2,128)(2,1)} %table_ref.3) | copy-start | bytes 970756
  22.0 0.8 %copy-start.6 = (s32[32,189]{1,0:T(8,128)S(1)}, s32[32,189]{1,0:T(8,128)}, u32[]{:S(2)}) copy-start(s32[32,189]{1,0:T(8,128)} %source_ref.3) | copy-start | bytes 72580
  22.7 0.8 %copy-start.7 = (s32[32,189]{1,0:T(8,128)S(1)}, s32[32,189]{1,0:T(8,128)}, u32[]{:S(2)}) copy-start(s32[32,189]{1,0:T(8,128)} %kind_ref.3) | copy-start | bytes 72580
  27.7 12.1 %copy-start.1 = (s32[2]{0:T(128)S(1)}, s32[2]{0:T(128)}, u32[]{:S(2)}) copy-start(s32[2]{0:T(128)} %pad_add_fusion.place_ref) | copy-start | bytes 28
  27.7 12.1 %copy-start.2 = (bf16[1024,2,128]{2,1,0:T(2,128)(2,1)S(1)}, bf16[1024,2,128]{2,1,0:T(2,128)(2,1)}, u32[]{:S(2)}) copy-start(bf16[1024,2,128]{2,1,0:T(2,128)(2,1)} %forward_ref.1) | copy-start | bytes 1572868
  27.8 12.1 %copy-start.3 = (bf16[1024,2,128]{2,1,0:T(2,128)(2,1)S(1)}, bf16[1024,2,128]{2,1,0:T(2,128)(2,1)}, u32[]{:S(2)}) copy-start(bf16[1024,2,128]{2,1,0:T(2,128)(2,1)} %before_ref.1) | copy-start | bytes 1572868
  27.8 12.1 %copy-start.5 = (bf16[528,256]{1,0:T(8,128)(2,1)S(1)}, bf16[528,256]{1,0:T(8,128)(2,1)}, u32[]{:S(2)}) copy-start(bf16[528,256]{1,0:T(8,128)(2,1)} %get-tuple-element.15.refs_0_) | copy-start | bytes 811012
  27.8 12.1 %copy-start.8 = (f32[16,256]{1,0:T(8,128)S(1)}, f32[16,256]{1,0:T(8,128)}, u32[]{:S(2)}) copy-start(f32[16,256]{1,0:T(8,128)} %get-tuple-element.14.point_ref) | copy-start | bytes 49156
  27.8 14.7 %collective-permute-start.9 = (bf16[528,256]{1,0:T(8,128)(2,1)S(1)}, bf16[528,256]{1,0:T(8,128)(2,1)S(1)}, u32[]{:S(2)}, u32[]{:S(2)}) collective-permute-start(bf16[528,256]{1,0:T(8,128)(2,1)S(1)} %collective-permute-done.1.refs_2_), channel_id=1, source_target_pairs={{0,4},{8,12},{16,20},{24,28},{4,0},{12,8},{20,16},{28,24},{1,5},{9... | collective-permute-start | bytes 811016 | tf_op jit(solution)/shard_map/ppermute | solution.py:357
  29.5 13.0 %collective-permute-start.4 = (bf16[528,256]{1,0:T(8,128)(2,1)S(1)}, bf16[528,256]{1,0:T(8,128)(2,1)S(1)}, u32[]{:S(2)}, u32[]{:S(2)}) collective-permute-start(bf16[528,256]{1,0:T(8,128)(2,1)S(1)} %collective-permute-done.refs_1_), channel_id=1, source_target_pairs={{4,8},{12,16},{20,24},{8,4},{16,12},{24,20},{5,9},{13,17},{21,25},... | collective-permute-start | bytes 811016 | tf_op jit(solution)/shard_map/ppermute | solution.py:357
  31.7 10.8 %collective-permute-start.8 = (bf16[528,256]{1,0:T(8,128)(2,1)S(1)}, bf16[528,256]{1,0:T(8,128)(2,1)S(1)}, u32[]{:S(2)}, u32[]{:S(2)}) collective-permute-start(bf16[528,256]{1,0:T(8,128)(2,1)S(1)} %collective-permute-done.refs_1_), channel_id=1, source_target_pairs={{0,4},{8,12},{16,20},{24,28},{4,0},{12,8},{20,16},{28,24},{1,5},{9... | collective-permute-start | bytes 811016 | tf_op jit(solution)/shard_map/ppermute | solution.py:357
  33.1 9.4 %collective-permute-start.10 = (bf16[528,256]{1,0:T(8,128)(2,1)S(1)}, bf16[528,256]{1,0:T(8,128)(2,1)S(1)}, u32[]{:S(2)}, u32[]{:S(2)}) collective-permute-start(bf16[528,256]{1,0:T(8,128)(2,1)S(1)} %collective-permute-done.2.refs_3_), channel_id=1, source_target_pairs={{0,4},{8,12},{16,20},{24,28},{4,0},{12,8},{20,16},{28,24},{1,5},{9... | collective-permute-start | bytes 811016 | tf_op jit(solution)/shard_map/ppermute | solution.py:357
  33.1 10.6 %collective-permute-start.6 = (bf16[528,256]{1,0:T(8,128)(2,1)S(1)}, bf16[528,256]{1,0:T(8,128)(2,1)S(1)}, u32[]{:S(2)}, u32[]{:S(2)}) collective-permute-start(bf16[528,256]{1,0:T(8,128)(2,1)S(1)} %collective-permute-done.2.refs_3_), channel_id=1, source_target_pairs={{4,8},{12,16},{20,24},{8,4},{16,12},{24,20},{5,9},{13,17},{21,25},... | collective-permute-start | bytes 811016 | tf_op jit(solution)/shard_map/ppermute | solution.py:357
  43.7 16.6 %copy-start.9 = (s32[8]{0:T(128)S(1)}, s32[8]{0:T(128)}, u32[]{:S(2)}) copy-start(s32[8]{0:T(128)} %live_ref.1) | copy-start | bytes 100
  48.3 8.6 %collective-permute-start.12 = (bf16[8,64,256]{2,1,0:T(8,128)(2,1)S(1)}, bf16[8,64,256]{2,1,0:T(8,128)(2,1)S(1)}, u32[]{:S(2)}, u32[]{:S(2)}) collective-permute-start(bf16[8,64,256]{2,1,0:T(8,128)(2,1)S(1)} %get-tuple-element.22), channel_id=1, source_target_pairs={{0,1},{1,0},{2,3},{3,2},{4,5},{5,4},{6,7},{7,6},{8,9},{9,8},{10,11... | collective-permute-start | bytes 786440 | tf_op jit(solution)/shard_map/ppermute | solution.py:353
  49.7 16.8 %collective-permute-start.11 = (bf16[8,64,256]{2,1,0:T(8,128)(2,1)S(1)}, bf16[8,64,256]{2,1,0:T(8,128)(2,1)S(1)}, u32[]{:S(2)}, u32[]{:S(2)}) collective-permute-start(bf16[8,64,256]{2,1,0:T(8,128)(2,1)S(1)} %get-tuple-element.20), channel_id=1, source_target_pairs={{0,1},{1,0},{2,3},{3,2},{4,5},{5,4},{6,7},{7,6},{8,9},{9,8},{10,11... | collective-permute-start | bytes 786440 | tf_op jit(solution)/shard_map/ppermute | solution.py:353
  57.0 15.5 %collective-permute-start.13 = (bf16[8,64,256]{2,1,0:T(8,128)(2,1)S(1)}, bf16[8,64,256]{2,1,0:T(8,128)(2,1)S(1)}, u32[]{:S(2)}, u32[]{:S(2)}) collective-permute-start(bf16[8,64,256]{2,1,0:T(8,128)(2,1)S(1)} %add_convert_fusion), channel_id=1, source_target_pairs={{0,2},{1,3},{2,0},{3,1},{4,6},{5,7},{6,4},{7,5},{8,10},{9,11},{10,... | collective-permute-start | bytes 786440 | tf_op jit(solution)/shard_map/ppermute | solution.py:353

commit v5 on v4

v5 whole, which is shorter than its diff:
```python
import functools
import math

import jax
import jax.numpy as jnp
from jax import lax
from jax.experimental import pallas as pl
from jax.experimental.pallas import tpu as pltpu
from jax.sharding import PartitionSpec as P

RIM = 8
LANES = 128
BF = jnp.bfloat16
F32 = jnp.float32
I32 = jnp.int32
NT = (((1,), (1,)), ((), ()))
TN = (((0,), (0,)), ((), ()))
NN = (((1,), (0,)), ((), ()))
VMEM = pl.BlockSpec(memory_space=pltpu.VMEM)
SMEM = pl.BlockSpec(memory_space=pltpu.SMEM)


def round_up(value, unit):
    return -(-value // unit) * unit


def dot(a, b, dims):
    return lax.dot_general(a, b, dims, preferred_element_type=F32)


def cost(flops, nbytes):
    return pl.CostEstimate(flops=int(flops), bytes_accessed=int(nbytes), transcendentals=0)


def grant(*groups):
    size = 4 << 20
    for group in groups:
        for item in group:
            size += math.prod(item.shape) * jnp.dtype(item.dtype).itemsize
    return pltpu.CompilerParams(vmem_limit_bytes=min(size, 60 * 1024 * 1024))


def count_of(shape, axis):
    return lax.broadcasted_iota(I32, shape, axis)


def as_bf16(mask):
    return mask.astype(F32).astype(BF)


def unrolled(trips, most, step):
    size = next(n for n in range(min(most, trips), 0, -1) if trips % n == 0)

    def block(i, carry):
        for j in range(size):
            step(i * size + j)
        return carry

    lax.fori_loop(0, trips // size, block, 0)


def prepare_kernel(all_dirs, place_ref, live_ref, stencil_ref, weight_ref, box_ref, out_ref):
    boxes, incid, width = box_ref.shape
    points, dirs = stencil_ref.shape
    unk = count_of((incid, width), 1)
    unk = jnp.where(unk < width // 2, unk, unk - width // 2)
    for b in range(boxes):
        kept = jnp.where(unk < live_ref[b], box_ref[b].astype(F32), 0.0)
        out_ref[b * incid : (b + 1) * incid, :] = kept.astype(BF)
    away = stencil_ref[...] - (count_of((points, dirs), 1) + place_ref[0] * dirs)
    away = jnp.where(away > all_dirs // 2, away - all_dirs, away)
    away = jnp.where(away < -(all_dirs // 2), away + all_dirs, away)
    rows = jnp.concatenate([away.astype(F32), weight_ref[...].astype(F32)], axis=0)
    if dirs < width:
        rows = jnp.concatenate([rows, jnp.zeros((2 * points, width - dirs), F32)], axis=1)
    out_ref[boxes * incid :, :] = rows.astype(BF)


def prepare(place, live_counts, stencil, weights, currents, all_dirs):
    boxes, incid, width = currents.shape
    points, dirs = stencil.shape
    out_shape = jax.ShapeDtypeStruct((boxes * incid + 2 * points, width), BF)
    return pl.pallas_call(
        functools.partial(prepare_kernel, all_dirs),
        out_shape=out_shape,
        in_specs=[SMEM, SMEM, VMEM, VMEM, VMEM],
        out_specs=VMEM,
        compiler_params=grant([out_shape, currents]),
        cost_estimate=cost(1 << 20, 1 << 20),
        name="prepare",
    )(place, live_counts, stencil, weights, currents)


def counts_kernel(slots, place_ref, source_ref, kind_ref, counts_ref, lists):
    all_boxes, width = source_ref.shape
    per = all_boxes // slots
    padded, lanes_out = counts_ref.shape
    window = lanes_out // (2 * per)
    own_dir, own_group = place_ref[0], place_ref[1]
    lists[...] = jnp.full(lists.shape, -1, I32)
    for i in range(2):
        first = pl.multiple_of((own_dir ^ i) * per, 8)
        local = source_ref[pl.ds(first, per), :] - (own_group - 1) * all_boxes
        group = (local >= all_boxes).astype(I32) + (local >= 2 * all_boxes).astype(I32)
        inside = local - group * all_boxes
        holder = jnp.zeros_like(inside)
        for j in range(1, slots):
            holder += (inside >= j * per).astype(I32)
        slot = own_dir ^ holder
        side = jnp.where(group == 0, 0, 1)
        around = jnp.where(slot < 2, 2 * slots - 2 + 2 * slot + side, slots - 2 + slot)
        slot = jnp.where(group == 1, slot, around)
        lists[i * per : (i + 1) * per, :width] = slot * per + inside - holder * per
        lists[(2 + i) * per : (3 + i) * per, :width] = kind_ref[pl.ds(first, per), :]
    lanes = lists.shape[1]
    for i in range(2 * per):
        hit_kind = count_of((padded, lanes), 0) == lists[2 * per + i : 2 * per + i + 1, :]
        hit_source = count_of((window, lanes), 0) == lists[i : i + 1, :]
        counts = dot(as_bf16(hit_kind), as_bf16(hit_source), NT)
        counts_ref[:, i * window : (i + 1) * window] = counts.astype(BF)


def count_entries(place, sources, operator_ids, kinds, slots, window):
    all_boxes, width = sources.shape
    boxes = 2 * (all_boxes // slots)
    out_shape = jax.ShapeDtypeStruct((round_up(kinds, LANES), boxes * window), BF)
    scratch = [pltpu.VMEM((2 * boxes, round_up(width, LANES)), I32)]
    return pl.pallas_call(
        functools.partial(counts_kernel, slots),
        out_shape=out_shape,
        in_specs=[SMEM, VMEM, VMEM],
        out_specs=VMEM,
        scratch_shapes=scratch,
        compiler_params=grant(scratch, [out_shape, sources, sources]),
        cost_estimate=cost(1 << 30, 1 << 20),
        name="counts",
    )(place, sources, operator_ids)


def transfer_kernel(counts_ref, table_ref, matrix_ref, table, wide):
    dirs, rows, window = matrix_ref.shape
    boxes = rows // 2
    kinds = table_ref.shape[0]
    fill = jnp.zeros((table.shape[1] - kinds, dirs), BF)
    for c in range(2):
        part = jnp.concatenate([table_ref[:, c, :], fill], axis=0)
        table[c * dirs : (c + 1) * dirs, :] = part.T
    for at in range(0, boxes, 2):
        entries = dot(table[...], counts_ref[:, at * window : (at + 2) * window], NN)
        for i in range(2):
            for c in range(window // LANES):
                part = entries[:, i * window + c * LANES : i * window + (c + 1) * LANES]
                wide[c, pl.ds(at + i, dirs, stride=rows + 1), :] = part[:dirs]
                wide[c, pl.ds(at + i + boxes, dirs, stride=rows + 1), :] = part[dirs:]

    def narrow(k):
        for c in range(window // LANES):
            part = wide[c, pl.ds(k * (rows + 1), rows), :]
            matrix_ref[k, :, c * LANES : (c + 1) * LANES] = part.astype(BF)

    unrolled(dirs, 64, narrow)


def transfer(counts, translators, per, window):
    kinds, _, dirs = translators.shape
    out_shape = jax.ShapeDtypeStruct((dirs, 2 * per, window), BF)
    scratch = [
        pltpu.VMEM((2 * dirs, counts.shape[0]), BF),
        pltpu.VMEM((window // LANES, dirs * (2 * per + 1), LANES), F32),
    ]
    return pl.pallas_call(
        transfer_kernel,
        out_shape=out_shape,
        in_specs=[VMEM, VMEM],
        out_specs=VMEM,
        scratch_shapes=scratch,
        compiler_params=grant(scratch, [out_shape, translators, translators, counts]),
        cost_estimate=cost(1 << 30, 1 << 20),
        name="transfer",
    )(counts, translators)


def rotated(box):
    half = box.shape[1] // 2
    re, im = box[:, :half], box[:, half:]
    return jnp.concatenate(
        [jnp.concatenate([re, -im], axis=1), jnp.concatenate([im, re], axis=1)], axis=0
    )


def radiate(forward, box_refs, incid, out, stride):
    dirs = forward.shape[0]
    at = 0
    for ref in box_refs:
        for row in range(0, ref.shape[0] // incid * incid, 2 * incid):
            both = [rotated(ref[i : i + incid, :]) for i in (row, row + incid)]
            field = dot(forward[...], jnp.concatenate(both, axis=0), NT)
            out[pl.ds(at, dirs, stride=stride), :] = field[:, : 2 * incid]
            out[pl.ds(at + 1, dirs, stride=stride), :] = field[:, 2 * incid :]
            at += 2


def pattern_kernel(slots, count, incid, rim, place_ref, *refs):
    forward_refs, refs = refs[: len(slots)], refs[len(slots) :]
    receive_ref, refs = refs[0], refs[1:]
    box_refs, (pattern_ref, turned_ref, folded_ref, wide, tails) = refs[:count], refs[count:]
    rows, boxes, _ = pattern_ref.shape
    dirs = rows // len(slots)
    for j, ref in enumerate(forward_refs):
        flat = jnp.concatenate([ref[:, 0, :], ref[:, 1, :]], axis=1)
        turned_ref[j * dirs : (j + 1) * dirs, :] = flat
    radiate(turned_ref, box_refs, incid, wide, boxes + 1)

    def narrow(k):
        pattern_ref[k] = wide[pl.ds(k * (boxes + 1), boxes), :].astype(BF)

    unrolled(rows, 32, narrow)

    own_dir = place_ref[0]
    points = tails.shape[1] // 2
    total = receive_ref.shape[0]
    for j, ref in enumerate(box_refs):
        tails[j] = ref[ref.shape[0] - 2 * points :, :].astype(F32)
    lane = count_of((2 * points, LANES), 1)
    source = count_of((tails.shape[2], LANES), 0)
    target = count_of((tails.shape[2], LANES), 1)
    head = as_bf16((target < rim) & (source == target))
    tail = as_bf16((target >= rim) & (target < 2 * rim) & (source == target + dirs - 2 * rim))
    for at, j in enumerate(slots):
        holder = own_dir ^ j
        follows = own_dir ^ lax.rem(holder + 1, count)
        leads = own_dir ^ lax.rem(holder + count - 1, count)
        ends = dot(tails[follows].astype(BF), head, NN) + dot(tails[leads].astype(BF), tail, NN)
        here = tails[j][:, :dirs]
        spot = count_of((points, LANES), 1)
        spot = jnp.where(spot < rim, spot + dirs, spot - 2 * rim)
        spots = [here[:points].astype(I32) + count_of((points, dirs), 1)]
        spots.append(ends[:points].astype(I32) + spot)
        gains = [here[points:], ends[points:]]
        start = holder * dirs
        after = receive_ref[pl.ds(lax.rem(start + dirs, total), rim)]
        before = receive_ref[pl.ds(lax.rem(start + total - rim, total), rim)]
        tables = [receive_ref[pl.ds(start, dirs)], jnp.concatenate([after, before], axis=0)]
        folded = None
        for spot, gain, table in zip(spots, gains, tables):
            extent = spot.shape[1]
            own = count_of((dirs, extent), 0)
            spread = jnp.zeros((dirs, extent), F32)
            for p in range(points):
                spread += jnp.where(own == spot[p : p + 1, :], gain[p : p + 1, :], 0.0)
            flat = jnp.concatenate([table[:, 0, :], table[:, 1, :]], axis=1)
            if flat.shape[0] < extent:
                blank = jnp.zeros((extent - flat.shape[0], flat.shape[1]), BF)
                flat = jnp.concatenate([flat, blank], axis=0)
            part = dot(spread.astype(BF), flat, NN)
            folded = part if folded is None else folded + part
        folded_ref[at * dirs : (at + 1) * dirs, :] = folded.astype(BF)


def own_pattern(place, radiation, receiving, shards, slots, incid, points, dirs):
    count = len(shards)
    boxes = sum(s.shape[0] // incid for s in shards)
    all_dirs, parts, unk = receiving.shape
    rows = len(slots) * dirs
    blocks = [
        pl.BlockSpec((dirs, parts, unk), lambda i, at, j=j: (at[0] ^ j, 0, 0)) for j in slots
    ]
    out_shape = (
        jax.ShapeDtypeStruct((rows, boxes, 2 * incid), BF),
        jax.ShapeDtypeStruct((rows, parts * unk), BF),
        jax.ShapeDtypeStruct((rows, parts * unk), BF),
    )
    scratch = [
        pltpu.VMEM((rows * (boxes + 1), 2 * incid), F32),
        pltpu.VMEM((count, 2 * points, shards[0].shape[1]), F32),
    ]
    return pl.pallas_call(
        functools.partial(pattern_kernel, slots, count, incid, RIM),
        out_shape=out_shape,
        grid_spec=pltpu.PrefetchScalarGridSpec(
            num_scalar_prefetch=1,
            grid=(1,),
            in_specs=blocks + [VMEM] * (1 + count),
            out_specs=(VMEM, VMEM, VMEM),
            scratch_shapes=scratch,
        ),
        compiler_params=grant(scratch, out_shape, shards, [radiation, radiation, receiving]),
        cost_estimate=cost(4 << 30, 4 << 20),
        name="pattern",
    )(place, *[radiation] * len(slots), receiving, *shards)


def field_kernel(slices, live_ref, forward_ref, folded_ref, own_ref, *refs):
    matrix_refs, refs = refs[:slices], refs[slices:]
    box_refs, (out_ref, pair_ref, near, moved) = refs[:-4], refs[-4:]
    rows, own_boxes, width = own_ref.shape
    per, half, _ = out_ref.shape
    boxes = 2 * per
    near_boxes = len(box_refs) * per
    radiate(forward_ref, box_refs, half, near, near_boxes + 1)
    sign = jnp.where(count_of((boxes, width), 1) < half, -1.0, 1.0).astype(F32)
    stride = boxes + 1
    dirs = rows // slices
    for at, matrix_ref in enumerate(matrix_refs):

        def translate(i, at=at, matrix_ref=matrix_ref):
            k = at * dirs + i
            around = near[pl.ds(k * (near_boxes + 1), near_boxes), :].astype(BF)
            fields = jnp.concatenate([own_ref[k], around], axis=0)
            both = dot(matrix_ref[i][:, : own_boxes + near_boxes], fields, NN)
            turned = pltpu.roll(both[boxes:], half, 1)
            moved[pl.ds(k * stride, boxes), :] = both[:boxes] + sign * turned

        unrolled(dirs, 64, translate)

    unk = folded_ref.shape[1] // 2
    lane = count_of((half, unk), 1)
    for i in reversed(range(boxes)):
        field = moved[pl.ds(i, rows, stride=stride), :].astype(BF)
        full = dot(field, folded_ref[...], TN)
        re = full[:half, :unk] - full[half:, unk:]
        im = full[:half, unk:] + full[half:, :unk]
        both = jnp.concatenate([re, im], axis=1)
        if i < per:
            out_ref[i] = both
        else:
            pair_ref[i - per] = both.astype(pair_ref.dtype)


def receive_field(live_counts, forward, folded, own, matrices, near, kind):
    rows, _, width = own.shape
    per = matrices[0].shape[1] // 4
    shape = (per, width // 2, folded.shape[1])
    out_shape = (jax.ShapeDtypeStruct(shape, F32), jax.ShapeDtypeStruct(shape, kind))
    scratch = [
        pltpu.VMEM((rows * (len(near) * per + 1), width), F32),
        pltpu.VMEM((rows * (2 * per + 1), width), F32),
    ]
    return pl.pallas_call(
        functools.partial(field_kernel, len(matrices)),
        out_shape=out_shape,
        in_specs=[SMEM] + [VMEM] * (3 + len(matrices) + len(near)),
        out_specs=(VMEM, VMEM),
        scratch_shapes=scratch,
        compiler_params=grant(scratch, out_shape, [forward, folded, own], matrices, near),
        cost_estimate=cost(4 << 30, 16 << 20),
        name="field",
    )(live_counts, forward, folded, own, *matrices, *near)


def mask_rows(values, live_counts):
    column = jnp.arange(values.shape[-1], dtype=I32) % (values.shape[-1] // 2)
    keep = column[None, None, :] < live_counts[:, None, None]
    return jnp.where(keep, values, jnp.zeros_like(values))


def body(
    currents,
    live_counts,
    radiation,
    sources,
    operator_ids,
    translators,
    stencil,
    stencil_weights,
    receiving,
):
    n_dir, n_grp = lax.axis_size("dir"), lax.axis_size("grp")
    kinds, _, dirs = translators.shape
    per, incid, _ = currents.shape
    points = stencil.shape[1]
    window = round_up((2 * n_dir + 2) * per, LANES)
    place = jnp.stack([lax.axis_index("dir"), lax.axis_index("grp")]).astype(I32)

    def swap(values, bit):
        return lax.ppermute(values, "dir", [(i, i ^ bit) for i in range(n_dir)])

    def gather(values, last):
        slots = {0: values}
        bit = n_dir // 2
        while bit >= last:
            for j in sorted(slots):
                slots[j + bit] = swap(slots[j], bit)
            bit //= 2
        return [slots[j] for j in sorted(slots)]

    def across(values, step_of):
        pairs = []
        for g in range(n_grp):
            for d in range(n_dir):
                to = g + step_of(d)
                if 0 <= to < n_grp:
                    pairs.append((g * n_dir + d, to * n_dir + d))
        return lax.ppermute(values, ("grp", "dir"), pairs)

    shard = prepare(
        place, live_counts, stencil.T, stencil_weights.T, currents, radiation.shape[0]
    )
    shards = gather(shard, 1)
    near = [across(shards[j], lambda d, j=j: 1 if d ^ j > d else -1) for j in range(2, n_dir)]
    near += [across(shards[j], lambda d, step=step: step) for j in range(2) for step in (1, -1)]
    tables = gather(translators, 2)

    counts = count_entries(place, sources, operator_ids, kinds, n_dir, window)
    matrices = [transfer(counts, table, 2 * per, window) for table in tables]
    wide = dirs * (len(near) * per + 1) * LANES * 4
    slices = len(tables)
    size = max(n for n in range(1, slices + 1) if slices % n == 0 and (n == 1 or n * wide <= 24 << 20))
    sums = None
    for first in range(0, slices, size):
        own, forward, folded = own_pattern(
            place,
            radiation,
            receiving,
            shards,
            [2 * j for j in range(first, first + size)],
            incid,
            points,
            dirs,
        )
        part = receive_field(
            live_counts,
            forward,
            folded,
            own,
            matrices[first : first + size],
            near,
            BF if size == slices else F32,
        )
        sums = part if sums is None else [a + b for a, b in zip(sums, part)]
    total = sums[0] + swap(sums[1].astype(BF), 1).astype(F32)
    return mask_rows(total, live_counts)


def solution(mesh):
    placed = (
        P(("grp", "dir"), None, None),
        P(("grp", "dir")),
        P(),
        P("grp", None),
        P("grp", None),
        P(None, None, "dir"),
        P("dir", None),
        P("dir", None),
        P(),
    )
    return jax.shard_map(
        body,
        mesh=mesh,
        in_specs=placed,
        out_specs=P(("grp", "dir"), None, None),
        check_vma=False,
    )
```

time: 74.4 us -> 68.8 us (0.925)
  waiting for transfers between devices: 27.4 us -> 20.5 us
  local copies, waits for them, and re-layouts: 3.17 us -> 4.53 us
  Pallas kernels: 17.4 us -> 18.2 us
    ppermute x6 -> x5, waiting for transfers between devices: 26.2 us -> 20.5 us  [swap(): return lax.ppermute(values, 'dir', [(i, i ^ bit) for i in range(n_dir)])]
    ppermute x6 -> x5, starting transfers between devices: 10.3 us -> 6.66 us  [swap(): return lax.ppermute(values, 'dir', [(i, i ^ bit) for i in range(n_dir)])]
    ppermute x8 -> x6, starting transfers between devices: 13.3 us -> 16.5 us  [across(): return lax.ppermute(values, ('grp', 'dir'), pairs)]
    unnamed x20, local copies, waits for them, and re-layouts: 3.17 us -> 4.53 us
    ppermute x8 -> x6, waiting for transfers between devices: 1.21 us -> 0.02 us  [across(): return lax.ppermute(values, ('grp', 'dir'), pairs)]
    pallas_call x5 -> x6, Pallas kernels: 17.4 us -> 18.2 us  [the longest x1 7.48 us: receive_field(): pl.pallas_call(functools.partial(field_kernel, len(matrices)), out_shape=...]
  transfers between devices with their start and end apart: 14 -> 11, of which waited for: 5 -> 2; matrix products, arithmetic and copies ran while one was open for 0% -> 0% of each run, Pallas kernels for 15% -> 15%
where the time goes in v5:
time: 68.8 us; the launch traced here: 67.7 us
  starting transfers between devices  23.2 us (34%)
  waiting for transfers between devices  20.5 us (30%)
  Pallas kernels  18.2 us (26%)
  local copies, waits for them, and re-layouts  4.53 us (7%)
  other arithmetic  1.01 us (1%)
    ppermute x5, waiting for transfers between devices, swap(): return lax.ppermute(values, 'dir', [(i, i ^ bit) for i in range(n_dir)])  20.5 us
    ppermute x6, starting transfers between devices, across(): return lax.ppermute(values, ('grp', 'dir'), pairs)  16.5 us
    pallas_call x1, Pallas kernels, receive_field(): pl.pallas_call(functools.partial(field_kernel, len(matrices)), out_shape=...  7.48 us
    ppermute x5, starting transfers between devices, swap(): return lax.ppermute(values, 'dir', [(i, i ^ bit) for i in range(n_dir)])  6.66 us
    unnamed x20, local copies, waits for them, and re-layouts  4.53 us
    pallas_call x1, Pallas kernels, own_pattern(): pl.pallas_call(functools.partial(pattern_kernel, slots, count, incid, RIM...  4.35 us
    pallas_call x2, Pallas kernels, transfer(): pl.pallas_call(transfer_kernel, out_shape=out_shape, in_specs=[VMEM, VMEM...  4.18 us
    pallas_call x1, Pallas kernels, count_entries(): pl.pallas_call(functools.partial(counts_kernel, slots), out_shape=out_sha...  1.61 us
  transfers between devices with their start and end apart: 11, of which 2 were waited for; matrix products, arithmetic and copies ran while one was open for 0% of the time, Pallas kernels for 15%

profile of v5, /device:TPU:2, one launch (start us, length us, event | category | flops | bytes accessed | tf_op | source)
XLA Modules:
  0.0 67.7 jit_solution(5080453720718154889)
XLA Ops:
  0.1 0.9 %copy-done.1 = bf16[8,64,256]{2,1,0:T(8,128)(2,1)S(1)} copy-done((bf16[8,64,256]{2,1,0:T(8,128)(2,1)S(1)}, bf16[8,64,256]{2,1,0:T(8,128)(2,1)}, u32[]{:S(2)}) %copy-start.1) | copy-done | bytes 262168
  1.0 0.7 %copy-done.2 = s32[256,8]{0,1:T(8,128)S(1)} copy-done((s32[256,8]{0,1:T(8,128)S(1)}, s32[256,8]{0,1:T(8,128)}, u32[]{:S(2)}) %copy-start.2) | copy-done | bytes 8216
  1.7 0.7 %copy-done.3 = bf16[256,8]{0,1:T(8,128)(2,1)S(1)} copy-done((bf16[256,8]{0,1:T(8,128)(2,1)S(1)}, bf16[256,8]{0,1:T(8,128)(2,1)}, u32[]{:S(2)}) %copy-start.3) | copy-done | bytes 4120
  2.4 0.7 copy-done.4
  3.1 0.6 prepare.1.refs_3_
  3.7 2.7 %collective-permute-start.1 = (bf16[528,256]{1,0:T(8,128)(2,1)S(1)}, bf16[528,256]{1,0:T(8,128)(2,1)S(1)}, u32[]{:S(2)}, u32[]{:S(2)}) collective-permute-start(bf16[528,256]{1,0:T(8,128)(2,1)S(1)} %prepare.1.refs_3_), channel_id=1, source_target_pairs={{0,2},{1,3},{2,0},{3,1},{4,6},{5,7},{6,4},{7,5},{8,10},{9,11},{10,... | collective-permute-start | bytes 811016 | tf_op jit(solution)/shard_map/ppermute | solution.py:376
  6.7 1.6 %collective-permute-start = (bf16[528,256]{1,0:T(8,128)(2,1)S(1)}, bf16[528,256]{1,0:T(8,128)(2,1)S(1)}, u32[]{:S(2)}, u32[]{:S(2)}) collective-permute-start(bf16[528,256]{1,0:T(8,128)(2,1)S(1)} %prepare.1.refs_3_), channel_id=1, source_target_pairs={{0,1},{1,0},{2,3},{3,2},{4,5},{5,4},{6,7},{7,6},{8,9},{9,8},{10,11... | collective-permute-start | bytes 811016 | tf_op jit(solution)/shard_map/ppermute | solution.py:376
  8.2 1.9 %collective-permute-start.7 = (bf16[528,256]{1,0:T(8,128)(2,1)S(1)}, bf16[528,256]{1,0:T(8,128)(2,1)S(1)}, u32[]{:S(2)}, u32[]{:S(2)}) collective-permute-start(bf16[528,256]{1,0:T(8,128)(2,1)S(1)} %prepare.1.refs_3_), channel_id=1, source_target_pairs={{4,0},{5,1},{6,2},{7,3},{8,4},{9,5},{10,6},{11,7},{12,8},{13,9},{1... | collective-permute-start | bytes 811016 | tf_op jit(solution)/shard_map/ppermute | solution.py:394
  10.2 2.4 %collective-permute-start.6 = (bf16[528,256]{1,0:T(8,128)(2,1)S(1)}, bf16[528,256]{1,0:T(8,128)(2,1)S(1)}, u32[]{:S(2)}, u32[]{:S(2)}) collective-permute-start(bf16[528,256]{1,0:T(8,128)(2,1)S(1)} %prepare.1.refs_3_), channel_id=1, source_target_pairs={{0,4},{1,5},{2,6},{3,7},{4,8},{5,9},{6,10},{7,11},{8,12},{9,13},{1... | collective-permute-start | bytes 811016 | tf_op jit(solution)/shard_map/ppermute | solution.py:394
  12.6 14.1 %collective-permute-done.1.refs_5_ = bf16[528,256]{1,0:T(8,128)(2,1)S(1)} collective-permute-done((bf16[528,256]{1,0:T(8,128)(2,1)S(1)}, bf16[528,256]{1,0:T(8,128)(2,1)S(1)}, u32[]{:S(2)}, u32[]{:S(2)}) %collective-permute-start.1) | collective-permute-done | bytes 270368 | tf_op jit(solution)/shard_map/ppermute | solution.py:376
  26.7 0.8 %copy-done.8 = s32[32,189]{1,0:T(8,128)S(1)} copy-done((s32[32,189]{1,0:T(8,128)S(1)}, s32[32,189]{1,0:T(8,128)}, u32[]{:S(2)}) %copy-start.8) | copy-done | bytes 24216
  27.5 0.8 %copy-done.9 = s32[32,189]{1,0:T(8,128)S(1)} copy-done((s32[32,189]{1,0:T(8,128)S(1)}, s32[32,189]{1,0:T(8,128)}, u32[]{:S(2)}) %copy-start.9) | copy-done | bytes 24216
  28.2 1.6 %counts.1.counts_ref = bf16[384,2048]{1,0:T(8,128)(2,1)S(1)} custom-call(s32[2]{0:T(128)S(1)} %pad_add_fusion.place_ref, s32[32,189]{1,0:T(8,128)S(1)} %copy-done.8, s32[32,189]{1,0:T(8,128)S(1)} %copy-done.9), custom_call_target="tpu_custom_call" | custom-call | flops 1073741824 | bytes 1048576 | tf_op jit(solution)/shard_map/counts/pallas_call | solution.py:128
  29.9 2.1 %transfer.2.refs_0_ = bf16[256,32,128]{2,1,0:T(8,128)(2,1)S(1)} custom-call(bf16[384,2048]{1,0:T(8,128)(2,1)S(1)} %counts.1.counts_ref, bf16[316,2,256]{2,1,0:T(2,128)(2,1)S(1)} %copy-done), custom_call_target="tpu_custom_call" | custom-call | flops 1073741824 | bytes 1048576 | tf_op jit(solution)/shard_map/transfer/pallas_call | solution.py:171
  32.0 2.1 %collective-permute-start.4 = (bf16[528,256]{1,0:T(8,128)(2,1)S(1)}, bf16[528,256]{1,0:T(8,128)(2,1)S(1)}, u32[]{:S(2)}, u32[]{:S(2)}) collective-permute-start(bf16[528,256]{1,0:T(8,128)(2,1)S(1)} %collective-permute-done.1.refs_5_), channel_id=1, source_target_pairs={{0,4},{1,5},{4,8},{5,9},{6,2},{7,3},{8,12},{9,13},{10,6},{11,7},{1... | collective-permute-start | bytes 811016 | tf_op jit(solution)/shard_map/ppermute | solution.py:394
  34.1 3.6 %collective-permute-start.9 = (bf16[528,256]{1,0:T(8,128)(2,1)S(1)}, bf16[528,256]{1,0:T(8,128)(2,1)S(1)}, u32[]{:S(2)}, u32[]{:S(2)}) collective-permute-start(bf16[528,256]{1,0:T(8,128)(2,1)S(1)} %collective-permute-done.refs_4_), channel_id=1, source_target_pairs={{4,0},{5,1},{6,2},{7,3},{8,4},{9,5},{10,6},{11,7},{12,8},{13,9},{1... | collective-permute-start | bytes 811016 | tf_op jit(solution)/shard_map/ppermute | solution.py:394
  37.7 2.1 %transfer.3.refs_1_ = bf16[256,32,128]{2,1,0:T(8,128)(2,1)S(1)} custom-call(bf16[384,2048]{1,0:T(8,128)(2,1)S(1)} %counts.1.counts_ref, bf16[316,2,256]{2,1,0:T(2,128)(2,1)S(1)} %collective-permute-done.3.table_ref), custom_call_target="tpu_custom_call" | custom-call | flops 1073741824 | bytes 1048576 | tf_op jit(solution)/shard_map/transfer/pallas_call | solution.py:171
  39.8 1.9 %collective-permute-start.8 = (bf16[528,256]{1,0:T(8,128)(2,1)S(1)}, bf16[528,256]{1,0:T(8,128)(2,1)S(1)}, u32[]{:S(2)}, u32[]{:S(2)}) collective-permute-start(bf16[528,256]{1,0:T(8,128)(2,1)S(1)} %collective-permute-done.refs_4_), channel_id=1, source_target_pairs={{0,4},{1,5},{2,6},{3,7},{4,8},{5,9},{6,10},{7,11},{8,12},{9,13},{1... | collective-permute-start | bytes 811016 | tf_op jit(solution)/shard_map/ppermute | solution.py:394
  41.8 4.6 %collective-permute-start.5 = (bf16[528,256]{1,0:T(8,128)(2,1)S(1)}, bf16[528,256]{1,0:T(8,128)(2,1)S(1)}, u32[]{:S(2)}, u32[]{:S(2)}) collective-permute-start(bf16[528,256]{1,0:T(8,128)(2,1)S(1)} %collective-permute-done.2.refs_6_), channel_id=1, source_target_pairs={{0,4},{1,5},{4,8},{5,9},{6,2},{7,3},{8,12},{9,13},{10,6},{11,7},{1... | collective-permute-start | bytes 811016 | tf_op jit(solution)/shard_map/ppermute | solution.py:394
  46.4 4.4 %pattern.1 = (bf16[512,32,128]{2,1,0:T(8,128)(2,1)S(1)}, bf16[512,256]{1,0:T(8,128)(2,1)S(1)}, bf16[512,256]{1,0:T(8,128)(2,1)S(1)}) custom-call(s32[2]{0:T(128)S(1)} %pad_add_fusion.place_ref, bf16[1024,2,128]{2,1,0:T(2,128)(2,1)S(1)} %copy-done.6, bf16[1024,2,128]{2,1,0:T(2,128)(2,1)S(1)} %copy-done.6, bf16[1024,2,128]{2,1,0:T(2,128)(2,1)S(1)} %copy-done.7, ...), custom_call_target="tpu_custom_call" | custom-call | flops 4294967296 | bytes 4194304 | tf_op jit(solution)/shard_map/pattern/pallas_call | solution.py:277
  50.8 7.5 %field.1 = (f32[8,64,256]{2,1,0:T(8,128)S(1)}, bf16[8,64,256]{2,1,0:T(8,128)(2,1)S(1)}) custom-call(s32[8]{0:T(128)S(1)} %copy-done.5, bf16[512,256]{1,0:T(8,128)(2,1)S(1)} %get-tuple-element.10.forward_ref, bf16[512,256]{1,0:T(8,128)(2,1)S(1)} %get-tuple-element.11.folded_ref, bf16[512,32,128]{2,1,0:T(8,128)(2,1)S(1)} %get-tuple-element.12.own_ref, ...), custom_call_target="tpu_custom_call" | custom-call | flops 4294967296 | bytes 16777216 | tf_op jit(solution)/shard_map/field/pallas_call | solution.py:339
  58.3 2.1 %collective-permute-start.10 = (bf16[8,64,256]{2,1,0:T(8,128)(2,1)S(1)}, bf16[8,64,256]{2,1,0:T(8,128)(2,1)S(1)}, u32[]{:S(2)}, u32[]{:S(2)}) collective-permute-start(bf16[8,64,256]{2,1,0:T(8,128)(2,1)S(1)} %get-tuple-element.14), channel_id=1, source_target_pairs={{0,1},{1,0},{2,3},{3,2},{4,5},{5,4},{6,7},{7,6},{8,9},{9,8},{10,11... | collective-permute-start | bytes 786440 | tf_op jit(solution)/shard_map/ppermute | solution.py:376
  60.4 6.4 %collective-permute-done.10 = bf16[8,64,256]{2,1,0:T(8,128)(2,1)S(1)} collective-permute-done((bf16[8,64,256]{2,1,0:T(8,128)(2,1)S(1)}, bf16[8,64,256]{2,1,0:T(8,128)(2,1)S(1)}, u32[]{:S(2)}, u32[]{:S(2)}) %collective-permute-start.10) | collective-permute-done | bytes 262176 | tf_op jit(solution)/shard_map/ppermute | solution.py:376
  66.8 0.9 %add_select_fusion = f32[8,64,256]{2,1,0:T(8,128)} fusion(f32[8,64,256]{2,1,0:T(8,128)S(1)} %get-tuple-element.13, bf16[8,64,256]{2,1,0:T(8,128)(2,1)S(1)} %collective-permute-done.10, pred[8,256]{1,0:T(8,128)(4,1)S(1)} %broadcast_compare_fusion), kind=kLoop, calls=%fused_computation | loop fusion | flops 393216 | bytes 1312768 | tf_op jit(solution)/shard_map/jit(_where)/select_n | solution.py:354
  (28 shorter events, 0.6 us)
Async XLA Ops:
  0.1 0.9 %copy-start.1 = (bf16[8,64,256]{2,1,0:T(8,128)(2,1)S(1)}, bf16[8,64,256]{2,1,0:T(8,128)(2,1)}, u32[]{:S(2)}) copy-start(bf16[8,64,256]{2,1,0:T(8,128)(2,1)} %box_ref.1) | copy-start | bytes 786436
  1.0 0.7 %copy-start.2 = (s32[256,8]{0,1:T(8,128)S(1)}, s32[256,8]{0,1:T(8,128)}, u32[]{:S(2)}) copy-start(s32[256,8]{0,1:T(8,128)} %param.15) | copy-start | bytes 24580
  1.7 0.7 %copy-start.3 = (bf16[256,8]{0,1:T(8,128)(2,1)S(1)}, bf16[256,8]{0,1:T(8,128)(2,1)}, u32[]{:S(2)}) copy-start(bf16[256,8]{0,1:T(8,128)(2,1)} %param.16) | copy-start | bytes 12292
  2.4 0.7 copy-start.4
  3.7 26.2 %copy-start = (bf16[316,2,256]{2,1,0:T(2,128)(2,1)S(1)}, bf16[316,2,256]{2,1,0:T(2,128)(2,1)}, u32[]{:S(2)}) copy-start(bf16[316,2,256]{2,1,0:T(2,128)(2,1)} %table_ref.1) | copy-start | bytes 970756
  3.7 23.0 %collective-permute-start.1 = (bf16[528,256]{1,0:T(8,128)(2,1)S(1)}, bf16[528,256]{1,0:T(8,128)(2,1)S(1)}, u32[]{:S(2)}, u32[]{:S(2)}) collective-permute-start(bf16[528,256]{1,0:T(8,128)(2,1)S(1)} %prepare.1.refs_3_), channel_id=1, source_target_pairs={{0,2},{1,3},{2,0},{3,1},{4,6},{5,7},{6,4},{7,5},{8,10},{9,11},{10,... | collective-permute-start | bytes 811016 | tf_op jit(solution)/shard_map/ppermute | solution.py:376
  6.3 27.7 %collective-permute-start.3 = (bf16[316,2,256]{2,1,0:T(2,128)(2,1)}, bf16[316,2,256]{2,1,0:T(2,128)(2,1)S(1)}, u32[]{:S(2)}, u32[]{:S(2)}) collective-permute-start(bf16[316,2,256]{2,1,0:T(2,128)(2,1)} %table_ref.1), channel_id=1, source_target_pairs={{0,2},{1,3},{2,0},{3,1},{4,6},{5,7},{6,4},{7,5},{8,10},{9,11},{10,... | collective-permute-start | bytes 970760 | tf_op jit(solution)/shard_map/ppermute | solution.py:376
  6.7 25.3 %collective-permute-start = (bf16[528,256]{1,0:T(8,128)(2,1)S(1)}, bf16[528,256]{1,0:T(8,128)(2,1)S(1)}, u32[]{:S(2)}, u32[]{:S(2)}) collective-permute-start(bf16[528,256]{1,0:T(8,128)(2,1)S(1)} %prepare.1.refs_3_), channel_id=1, source_target_pairs={{0,1},{1,0},{2,3},{3,2},{4,5},{5,4},{6,7},{7,6},{8,9},{9,8},{10,11... | collective-permute-start | bytes 811016 | tf_op jit(solution)/shard_map/ppermute | solution.py:376
  8.2 31.6 %collective-permute-start.7 = (bf16[528,256]{1,0:T(8,128)(2,1)S(1)}, bf16[528,256]{1,0:T(8,128)(2,1)S(1)}, u32[]{:S(2)}, u32[]{:S(2)}) collective-permute-start(bf16[528,256]{1,0:T(8,128)(2,1)S(1)} %prepare.1.refs_3_), channel_id=1, source_target_pairs={{4,0},{5,1},{6,2},{7,3},{8,4},{9,5},{10,6},{11,7},{12,8},{13,9},{1... | collective-permute-start | bytes 811016 | tf_op jit(solution)/shard_map/ppermute | solution.py:394
  10.2 40.6 %collective-permute-start.6 = (bf16[528,256]{1,0:T(8,128)(2,1)S(1)}, bf16[528,256]{1,0:T(8,128)(2,1)S(1)}, u32[]{:S(2)}, u32[]{:S(2)}) collective-permute-start(bf16[528,256]{1,0:T(8,128)(2,1)S(1)} %prepare.1.refs_3_), channel_id=1, source_target_pairs={{0,4},{1,5},{2,6},{3,7},{4,8},{5,9},{6,10},{7,11},{8,12},{9,13},{1... | collective-permute-start | bytes 811016 | tf_op jit(solution)/shard_map/ppermute | solution.py:394
  26.7 15.1 %collective-permute-start.2 = (bf16[528,256]{1,0:T(8,128)(2,1)S(1)}, bf16[528,256]{1,0:T(8,128)(2,1)S(1)}, u32[]{:S(2)}, u32[]{:S(2)}) collective-permute-start(bf16[528,256]{1,0:T(8,128)(2,1)S(1)} %collective-permute-done.1.refs_5_), channel_id=1, source_target_pairs={{0,1},{1,0},{2,3},{3,2},{4,5},{5,4},{6,7},{7,6},{8,9},{9,8},{10,11... | collective-permute-start | bytes 811016 | tf_op jit(solution)/shard_map/ppermute | solution.py:376
  26.7 0.8 %copy-start.8 = (s32[32,189]{1,0:T(8,128)S(1)}, s32[32,189]{1,0:T(8,128)}, u32[]{:S(2)}) copy-start(s32[32,189]{1,0:T(8,128)} %source_ref.1) | copy-start | bytes 72580
  27.5 0.8 %copy-start.9 = (s32[32,189]{1,0:T(8,128)S(1)}, s32[32,189]{1,0:T(8,128)}, u32[]{:S(2)}) copy-start(s32[32,189]{1,0:T(8,128)} %kind_ref.1) | copy-start | bytes 72580
  32.0 14.4 %copy-start.6 = (bf16[1024,2,128]{2,1,0:T(2,128)(2,1)S(1)}, bf16[1024,2,128]{2,1,0:T(2,128)(2,1)}, u32[]{:S(2)}) copy-start(bf16[1024,2,128]{2,1,0:T(2,128)(2,1)} %refs_1_.1) | copy-start | bytes 1572868
  32.0 14.4 %copy-start.7 = (bf16[1024,2,128]{2,1,0:T(2,128)(2,1)S(1)}, bf16[1024,2,128]{2,1,0:T(2,128)(2,1)}, u32[]{:S(2)}) copy-start(bf16[1024,2,128]{2,1,0:T(2,128)(2,1)} %refs_2_.1) | copy-start | bytes 1572868
  32.0 18.8 %collective-permute-start.4 = (bf16[528,256]{1,0:T(8,128)(2,1)S(1)}, bf16[528,256]{1,0:T(8,128)(2,1)S(1)}, u32[]{:S(2)}, u32[]{:S(2)}) collective-permute-start(bf16[528,256]{1,0:T(8,128)(2,1)S(1)} %collective-permute-done.1.refs_5_), channel_id=1, source_target_pairs={{0,4},{1,5},{4,8},{5,9},{6,2},{7,3},{8,12},{9,13},{10,6},{11,7},{1... | collective-permute-start | bytes 811016 | tf_op jit(solution)/shard_map/ppermute | solution.py:394
  34.1 16.7 %collective-permute-start.9 = (bf16[528,256]{1,0:T(8,128)(2,1)S(1)}, bf16[528,256]{1,0:T(8,128)(2,1)S(1)}, u32[]{:S(2)}, u32[]{:S(2)}) collective-permute-start(bf16[528,256]{1,0:T(8,128)(2,1)S(1)} %collective-permute-done.refs_4_), channel_id=1, source_target_pairs={{4,0},{5,1},{6,2},{7,3},{8,4},{9,5},{10,6},{11,7},{12,8},{13,9},{1... | collective-permute-start | bytes 811016 | tf_op jit(solution)/shard_map/ppermute | solution.py:394
  39.8 11.0 %copy-start.5 = (s32[8]{0:T(128)S(1)}, s32[8]{0:T(128)}, u32[]{:S(2)}) copy-start(s32[8]{0:T(128)} %live_ref.3) | copy-start | bytes 100
  39.8 10.9 %collective-permute-start.8 = (bf16[528,256]{1,0:T(8,128)(2,1)S(1)}, bf16[528,256]{1,0:T(8,128)(2,1)S(1)}, u32[]{:S(2)}, u32[]{:S(2)}) collective-permute-start(bf16[528,256]{1,0:T(8,128)(2,1)S(1)} %collective-permute-done.refs_4_), channel_id=1, source_target_pairs={{0,4},{1,5},{2,6},{3,7},{4,8},{5,9},{6,10},{7,11},{8,12},{9,13},{1... | collective-permute-start | bytes 811016 | tf_op jit(solution)/shard_map/ppermute | solution.py:394
  41.8 9.0 %collective-permute-start.5 = (bf16[528,256]{1,0:T(8,128)(2,1)S(1)}, bf16[528,256]{1,0:T(8,128)(2,1)S(1)}, u32[]{:S(2)}, u32[]{:S(2)}) collective-permute-start(bf16[528,256]{1,0:T(8,128)(2,1)S(1)} %collective-permute-done.2.refs_6_), channel_id=1, source_target_pairs={{0,4},{1,5},{4,8},{5,9},{6,2},{7,3},{8,12},{9,13},{10,6},{11,7},{1... | collective-permute-start | bytes 811016 | tf_op jit(solution)/shard_map/ppermute | solution.py:394
  58.3 8.6 %collective-permute-start.10 = (bf16[8,64,256]{2,1,0:T(8,128)(2,1)S(1)}, bf16[8,64,256]{2,1,0:T(8,128)(2,1)S(1)}, u32[]{:S(2)}, u32[]{:S(2)}) collective-permute-start(bf16[8,64,256]{2,1,0:T(8,128)(2,1)S(1)} %get-tuple-element.14), channel_id=1, source_target_pairs={{0,1},{1,0},{2,3},{3,2},{4,5},{5,4},{6,7},{7,6},{8,9},{9,8},{10,11... | collective-permute-start | bytes 786440 | tf_op jit(solution)/shard_map/ppermute | solution.py:376

commit v6 on v5

v6 whole, which is shorter than its diff:
```python
import functools
import math

import jax
import jax.numpy as jnp
from jax import lax
from jax.experimental import pallas as pl
from jax.experimental.pallas import tpu as pltpu
from jax.sharding import PartitionSpec as P


RIM = 8
LANES = 128
BF = jnp.bfloat16
F32 = jnp.float32
I32 = jnp.int32
NT = (((1,), (1,)), ((), ()))
TN = (((0,), (0,)), ((), ()))
NN = (((1,), (0,)), ((), ()))
VMEM = pl.BlockSpec(memory_space=pltpu.VMEM)
SMEM = pl.BlockSpec(memory_space=pltpu.SMEM)


def round_up(value, unit):
    return -(-value // unit) * unit


def half_of(kinds):
    return (kinds + 1) // 2


def table_rows(kinds):
    return round_up(2 * round_up(half_of(kinds), 16), LANES)


def dot(a, b, dims):
    return lax.dot_general(a, b, dims, preferred_element_type=F32)


def cost(flops, nbytes):
    return pl.CostEstimate(flops=int(flops), bytes_accessed=int(nbytes), transcendentals=0)


def grant(*groups):
    size = 4 << 20
    for group in groups:
        for item in group:
            size += math.prod(item.shape) * jnp.dtype(item.dtype).itemsize
    return pltpu.CompilerParams(vmem_limit_bytes=min(size, 60 * 1024 * 1024))


def count_of(shape, axis):
    return lax.broadcasted_iota(I32, shape, axis)


def as_bf16(mask):
    return mask.astype(F32).astype(BF)


def unrolled(trips, most, step):
    size = next(n for n in range(min(most, trips), 0, -1) if trips % n == 0)

    def block(i, carry):
        for j in range(size):
            step(i * size + j)
        return carry

    lax.fori_loop(0, trips // size, block, 0)


def prepare_kernel(all_dirs, live_ref, stencil_ref, weight_ref, box_ref, table_ref, out_ref, half_ref, sem):
    boxes, incid, width = box_ref.shape
    points, dirs = stencil_ref.shape
    half = half_ref.shape[0]
    first = lax.rem(lax.axis_index("grp"), 2) * (table_ref.shape[0] - half)
    fetch = pltpu.make_async_copy(table_ref.at[pl.ds(first, half)], half_ref, sem)
    fetch.start()
    unk = count_of((incid, width), 1)
    unk = jnp.where(unk < width // 2, unk, unk - width // 2)
    for b in range(boxes):
        kept = jnp.where(unk < live_ref[b], box_ref[b].astype(F32), 0.0)
        out_ref[b * incid : (b + 1) * incid, :] = kept.astype(BF)
    away = stencil_ref[...] - (count_of((points, dirs), 1) + lax.axis_index("dir") * dirs)
    away = jnp.where(away > all_dirs // 2, away - all_dirs, away)
    away = jnp.where(away < -(all_dirs // 2), away + all_dirs, away)
    rows = jnp.concatenate([away.astype(F32), weight_ref[...].astype(F32)], axis=0)
    if dirs < width:
        rows = jnp.concatenate([rows, jnp.zeros((2 * points, width - dirs), F32)], axis=1)
    out_ref[boxes * incid :, :] = rows.astype(BF)
    fetch.wait()


def prepare(live_counts, stencil, weights, currents, translators, all_dirs):
    boxes, incid, width = currents.shape
    points, dirs = stencil.shape
    kinds, parts, _ = translators.shape
    return pl.pallas_call(
        functools.partial(prepare_kernel, all_dirs),
        out_shape=(
            jax.ShapeDtypeStruct((boxes * incid + 2 * points, width), BF),
            jax.ShapeDtypeStruct((half_of(kinds), parts, dirs), BF),
        ),
        in_specs=[SMEM, VMEM, VMEM, VMEM, pl.BlockSpec(memory_space=pl.ANY)],
        out_specs=(VMEM, VMEM),
        scratch_shapes=[pltpu.SemaphoreType.DMA],
        cost_estimate=cost(1 << 20, 1 << 20),
        name="prepare",
    )(live_counts, stencil, weights, currents, translators)


def count_entries(slots, kinds, window, place_ref, source_ref, kind_ref, counts_ref, lists):
    all_boxes, width = source_ref.shape
    per = all_boxes // slots
    own_dir, own_group = place_ref[0], place_ref[1]
    half = half_of(kinds)
    lists[...] = jnp.full(lists.shape, -1, I32)
    for i in range(2):
        first = pl.multiple_of((own_dir ^ i) * per, 8)
        local = source_ref[pl.ds(first, per), :] - (own_group - 1) * all_boxes
        group = (local >= all_boxes).astype(I32) + (local >= 2 * all_boxes).astype(I32)
        inside = local - group * all_boxes
        holder = jnp.zeros_like(inside)
        for j in range(1, slots):
            holder += (inside >= j * per).astype(I32)
        slot = own_dir ^ holder
        side = jnp.where(group == jnp.where(own_group % 2 == 0, 2, 0), 1, 0)
        around = jnp.where(slot < 2, slots + 2 * slot + side, slots + 2 + slot)
        slot = jnp.where(group == 1, slot, around)
        lists[i * per : (i + 1) * per, :width] = slot * per + inside - holder * per
        kind = kind_ref[pl.ds(first, per), :]
        upper = kind - (kinds - half) + round_up(half, 16)
        kind = jnp.where(kind < half, kind, upper)
        lists[(2 + i) * per : (3 + i) * per, :width] = kind
    lanes = lists.shape[1]
    used = 2 * round_up(half, 16)
    if used < counts_ref.shape[0]:
        rest = (counts_ref.shape[0] - used, counts_ref.shape[1])
        counts_ref[used:, :] = jnp.zeros(rest, BF)
    for i in range(2 * per):
        hit_kind = count_of((used, lanes), 0) == lists[2 * per + i : 2 * per + i + 1, :]
        hit_source = count_of((window, lanes), 0) == lists[i : i + 1, :]
        counts = dot(as_bf16(hit_kind), as_bf16(hit_source), NT)
        counts_ref[:used, i * window : (i + 1) * window] = counts.astype(BF)


def fill_matrix(low, high, counts_ref, matrix_ref, table, wide):
    dirs, rows, window = matrix_ref.shape
    boxes = rows // 2
    half = low.shape[0]
    gap = round_up(half, 16) - half
    for c in range(2):
        fill = jnp.zeros((table.shape[1] - 2 * half - gap, dirs), BF)
        blank = jnp.zeros((gap, dirs), BF)
        part = jnp.concatenate([low[:, c, :], blank, high[:, c, :], fill], axis=0)
        table[c * dirs : (c + 1) * dirs, :] = part.T
    for at in range(0, boxes, 2):
        entries = dot(table[...], counts_ref[:, at * window : (at + 2) * window], NN)
        for i in range(2):
            for c in range(window // LANES):
                part = entries[:, i * window + c * LANES : i * window + (c + 1) * LANES]
                wide[c, pl.ds(at + i, dirs, stride=rows + 1), :] = part[:dirs]
                wide[c, pl.ds(at + i + boxes, dirs, stride=rows + 1), :] = part[dirs:]

    def narrow(k):
        for c in range(window // LANES):
            part = wide[c, pl.ds(k * (rows + 1), rows), :]
            matrix_ref[k, :, c * LANES : (c + 1) * LANES] = part.astype(BF)

    unrolled(dirs, 64, narrow)


def first_kernel(slots, place_ref, source_hbm, kind_hbm, table_hbm, counts_ref, matrix_ref, *scratch):
    source_ref, kind_ref, table_ref, lists, table, wide, sems = scratch
    window = matrix_ref.shape[2]
    kinds = table_ref.shape[0]
    copies = [
        pltpu.make_async_copy(source_hbm, source_ref, sems.at[0]),
        pltpu.make_async_copy(kind_hbm, kind_ref, sems.at[1]),
        pltpu.make_async_copy(table_hbm, table_ref, sems.at[2]),
    ]
    for copy in copies:
        copy.start()
    copies[0].wait()
    copies[1].wait()
    count_entries(slots, kinds, window, place_ref, source_ref, kind_ref, counts_ref, lists)
    copies[2].wait()
    half = half_of(kinds)
    low, high = table_ref.at[pl.ds(0, half)], table_ref.at[pl.ds(kinds - half, half)]
    fill_matrix(low, high, counts_ref, matrix_ref, table, wide)


def first_transfer(place, sources, operator_ids, translators, slots, window):
    all_boxes, width = sources.shape
    boxes = 2 * (all_boxes // slots)
    kinds, _, dirs = translators.shape
    out_shape = (
        jax.ShapeDtypeStruct((table_rows(kinds), boxes * window), BF),
        jax.ShapeDtypeStruct((dirs, 2 * boxes, window), BF),
    )
    scratch = [
        pltpu.VMEM(sources.shape, I32),
        pltpu.VMEM(sources.shape, I32),
        pltpu.VMEM(translators.shape, BF),
        pltpu.VMEM((2 * boxes, round_up(width, LANES)), I32),
        pltpu.VMEM((2 * dirs, table_rows(kinds)), BF),
        pltpu.VMEM((window // LANES, dirs * (2 * boxes + 1), LANES), F32),
    ]
    return pl.pallas_call(
        functools.partial(first_kernel, slots),
        out_shape=out_shape,
        in_specs=[SMEM] + [pl.BlockSpec(memory_space=pltpu.HBM)] * 3,
        out_specs=(VMEM, VMEM),
        scratch_shapes=scratch + [pltpu.SemaphoreType.DMA((3,))],
        compiler_params=grant(scratch, out_shape),
        cost_estimate=cost(1 << 30, 1 << 20),
        name="first",
    )(place, sources, operator_ids, translators)


def transfer_kernel(place_ref, counts_ref, mine_ref, other_ref, matrix_ref, low, high, table, wide):
    upper = place_ref[1] % 2 == 1

    @pl.when(upper)
    def _():
        low[...], high[...] = other_ref[...], mine_ref[...]

    @pl.when(jnp.logical_not(upper))
    def _():
        low[...], high[...] = mine_ref[...], other_ref[...]

    fill_matrix(low, high, counts_ref, matrix_ref, table, wide)


def transfer(place, counts, mine, other, boxes, window):
    _, _, dirs = mine.shape
    out_shape = jax.ShapeDtypeStruct((dirs, 2 * boxes, window), BF)
    scratch = [
        pltpu.VMEM(mine.shape, BF),
        pltpu.VMEM(mine.shape, BF),
        pltpu.VMEM((2 * dirs, counts.shape[0]), BF),
        pltpu.VMEM((window // LANES, dirs * (2 * boxes + 1), LANES), F32),
    ]
    return pl.pallas_call(
        transfer_kernel,
        out_shape=out_shape,
        in_specs=[SMEM] + [VMEM] * 3,
        out_specs=VMEM,
        scratch_shapes=scratch,
        compiler_params=grant(scratch, [out_shape, counts, mine, other]),
        cost_estimate=cost(1 << 30, 1 << 20),
        name="transfer",
    )(place, counts, mine, other)


def rotated(box):
    half = box.shape[1] // 2
    re, im = box[:, :half], box[:, half:]
    return jnp.concatenate(
        [jnp.concatenate([re, -im], axis=1), jnp.concatenate([im, re], axis=1)], axis=0
    )


def radiate(forward, box_refs, incid, out, stride):
    dirs = forward.shape[0]
    at = 0
    for ref in box_refs:
        for row in range(0, ref.shape[0] // incid * incid, 2 * incid):
            both = [rotated(ref[i : i + incid, :]) for i in (row, row + incid)]
            field = dot(forward[...], jnp.concatenate(both, axis=0), NT)
            out[pl.ds(at, dirs, stride=stride), :] = field[:, : 2 * incid]
            out[pl.ds(at + 1, dirs, stride=stride), :] = field[:, 2 * incid :]
            at += 2


def early_kernel(parts, count, incid, *refs):
    forward_refs, refs = refs[1 : 1 + parts], refs[1 + parts :]
    box_refs, (pattern_ref, turned_ref, wide) = refs[:count], refs[count:]
    rows, boxes, _ = pattern_ref.shape
    dirs = rows // parts
    for j, ref in enumerate(forward_refs):
        flat = jnp.concatenate([ref[:, 0, :], ref[:, 1, :]], axis=1)
        turned_ref[j * dirs : (j + 1) * dirs, :] = flat
    radiate(turned_ref, box_refs, incid, wide, boxes + 1)

    def narrow(k):
        pattern_ref[k] = wide[pl.ds(k * (boxes + 1), boxes), :].astype(BF)

    unrolled(rows, 32, narrow)


def early_pattern(place, radiation, shards, slots, incid, dirs):
    boxes = sum(s.shape[0] // incid for s in shards)
    _, parts, unk = radiation.shape
    rows = len(slots) * dirs
    blocks = [
        pl.BlockSpec((dirs, parts, unk), lambda i, at, j=j: (at[0] ^ j, 0, 0)) for j in slots
    ]
    out_shape = (
        jax.ShapeDtypeStruct((rows, boxes, 2 * incid), BF),
        jax.ShapeDtypeStruct((rows, parts * unk), BF),
    )
    scratch = [pltpu.VMEM((rows * (boxes + 1), 2 * incid), F32)]
    return pl.pallas_call(
        functools.partial(early_kernel, len(slots), len(shards), incid),
        out_shape=out_shape,
        grid_spec=pltpu.PrefetchScalarGridSpec(
            num_scalar_prefetch=1,
            grid=(1,),
            in_specs=blocks + [VMEM] * len(shards),
            out_specs=(VMEM, VMEM),
            scratch_shapes=scratch,
        ),
        compiler_params=grant(scratch, out_shape, shards, [radiation]),
        cost_estimate=cost(4 << 30, 4 << 20),
        name="early",
    )(place, *[radiation] * len(slots), *shards)


def pattern_kernel(slots, count, incid, rim, place_ref, turned_ref, receive_ref, *refs):
    box_refs, (pattern_ref, folded_ref, wide, tails) = refs[:count], refs[count:]
    rows, boxes, _ = pattern_ref.shape
    dirs = rows // len(slots)
    radiate(turned_ref, box_refs, incid, wide, boxes + 1)

    def narrow(k):
        pattern_ref[k] = wide[pl.ds(k * (boxes + 1), boxes), :].astype(BF)

    unrolled(rows, 32, narrow)

    own_dir = place_ref[0]
    points = tails.shape[1] // 2
    total = receive_ref.shape[0]
    for j, ref in enumerate(box_refs):
        tails[j] = ref[ref.shape[0] - 2 * points :, :].astype(F32)
    lane = count_of((2 * points, LANES), 1)
    source = count_of((tails.shape[2], LANES), 0)
    target = count_of((tails.shape[2], LANES), 1)
    head = as_bf16((target < rim) & (source == target))
    tail = as_bf16((target >= rim) & (target < 2 * rim) & (source == target + dirs - 2 * rim))
    for at, j in enumerate(slots):
        holder = own_dir ^ j
        follows = own_dir ^ lax.rem(holder + 1, count)
        leads = own_dir ^ lax.rem(holder + count - 1, count)
        ends = dot(tails[follows].astype(BF), head, NN) + dot(tails[leads].astype(BF), tail, NN)
        here = tails[j][:, :dirs]
        spot = count_of((points, LANES), 1)
        spot = jnp.where(spot < rim, spot + dirs, spot - 2 * rim)
        spots = [here[:points].astype(I32) + count_of((points, dirs), 1)]
        spots.append(ends[:points].astype(I32) + spot)
        gains = [here[points:], ends[points:]]
        start = holder * dirs
        after = receive_ref[pl.ds(lax.rem(start + dirs, total), rim)]
        before = receive_ref[pl.ds(lax.rem(start + total - rim, total), rim)]
        tables = [receive_ref[pl.ds(start, dirs)], jnp.concatenate([after, before], axis=0)]
        folded = None
        for spot, gain, table in zip(spots, gains, tables):
            extent = spot.shape[1]
            own = count_of((dirs, extent), 0)
            spread = jnp.zeros((dirs, extent), F32)
            for p in range(points):
                spread += jnp.where(own == spot[p : p + 1, :], gain[p : p + 1, :], 0.0)
            flat = jnp.concatenate([table[:, 0, :], table[:, 1, :]], axis=1)
            if flat.shape[0] < extent:
                blank = jnp.zeros((extent - flat.shape[0], flat.shape[1]), BF)
                flat = jnp.concatenate([flat, blank], axis=0)
            part = dot(spread.astype(BF), flat, NN)
            folded = part if folded is None else folded + part
        folded_ref[at * dirs : (at + 1) * dirs, :] = folded.astype(BF)


def own_pattern(place, forward, receiving, shards, slots, incid, points):
    count = len(shards)
    boxes = sum(s.shape[0] // incid for s in shards)
    rows, width = forward.shape
    out_shape = (
        jax.ShapeDtypeStruct((rows, boxes, 2 * incid), BF),
        jax.ShapeDtypeStruct((rows, width), BF),
    )
    scratch = [
        pltpu.VMEM((rows * (boxes + 1), 2 * incid), F32),
        pltpu.VMEM((count, 2 * points, shards[0].shape[1]), F32),
    ]
    return pl.pallas_call(
        functools.partial(pattern_kernel, slots, count, incid, RIM),
        out_shape=out_shape,
        in_specs=[SMEM] + [VMEM] * (2 + count),
        out_specs=(VMEM, VMEM),
        scratch_shapes=scratch,
        compiler_params=grant(scratch, out_shape, shards, [forward, receiving]),
        cost_estimate=cost(4 << 30, 4 << 20),
        name="pattern",
    )(place, forward, receiving, *shards)


def receive(moved, folded, first, out_ref, stride):
    rows, half, unk = folded.shape[0], moved.shape[1] // 2, folded.shape[1] // 2
    count = out_ref.shape[0]
    step = 4 if count % 4 == 0 else 1
    for begin in range(0, count, step):
        fields = [
            moved[pl.ds(first + begin + i, rows, stride=stride), :].astype(BF) for i in range(step)
        ]
        every = dot(jnp.concatenate(fields, axis=1), folded[...], TN)
        for i in range(step):
            full = every[2 * half * i : 2 * half * (i + 1)]
            re = full[:half, :unk] - full[half:, unk:]
            im = full[:half, unk:] + full[half:, :unk]
            out_ref[begin + i] = jnp.concatenate([re, im], axis=1).astype(out_ref.dtype)


def field_kernel(slices, forward_ref, folded_ref, own_ref, early_ref, *refs):
    matrix_refs, refs = refs[:slices], refs[slices:]
    box_refs, (pair_ref, moved, near) = refs[:-3], refs[-3:]
    rows, own_boxes, width = own_ref.shape
    per, half, _ = pair_ref.shape
    boxes = 2 * per
    near_boxes = len(box_refs) * per
    radiate(forward_ref, box_refs, half, near, near_boxes + 1)
    sign = jnp.where(count_of((boxes, width), 1) < half, -1.0, 1.0).astype(F32)
    stride = boxes + 1
    dirs = rows // slices
    window = own_boxes + early_ref.shape[1] + near_boxes
    for at, matrix_ref in enumerate(matrix_refs):

        def translate(i, at=at, matrix_ref=matrix_ref):
            k = at * dirs + i
            around = near[pl.ds(k * (near_boxes + 1), near_boxes), :].astype(BF)
            fields = jnp.concatenate([own_ref[k], early_ref[k], around], axis=0)
            both = dot(matrix_ref[i][:, :window], fields, NN)
            turned = pltpu.roll(both[boxes:], half, 1)
            moved[pl.ds(k * stride, boxes), :] = both[:boxes] + sign * turned

        unrolled(dirs, 64, translate)

    receive(moved, folded_ref, per, pair_ref, stride)


def translate_field(forward, folded, own, early, matrices, near, kind):
    rows, _, width = own.shape
    per = matrices[0].shape[1] // 4
    shape = (per, width // 2, folded.shape[1])
    out_shape = (
        jax.ShapeDtypeStruct(shape, kind),
        jax.ShapeDtypeStruct((rows * (2 * per + 1), width), F32),
    )
    scratch = [pltpu.VMEM((rows * (len(near) * per + 1), width), F32)]
    return pl.pallas_call(
        functools.partial(field_kernel, len(matrices)),
        out_shape=out_shape,
        in_specs=[VMEM] * (4 + len(matrices) + len(near)),
        out_specs=(VMEM, VMEM),
        scratch_shapes=scratch,
        compiler_params=grant(scratch, out_shape, [forward, folded, own, early], matrices, near),
        cost_estimate=cost(4 << 30, 16 << 20),
        name="field",
    )(forward, folded, own, early, *matrices, *near)


def finish_kernel(folded_ref, moved_ref, out_ref):
    receive(moved_ref, folded_ref, 0, out_ref, 2 * out_ref.shape[0] + 1)


def finish(folded, moved, shape):
    out_shape = jax.ShapeDtypeStruct(shape, F32)
    return pl.pallas_call(
        finish_kernel,
        out_shape=out_shape,
        in_specs=[VMEM, VMEM],
        out_specs=VMEM,
        compiler_params=grant([out_shape, folded, moved]),
        cost_estimate=cost(1 << 28, 1 << 20),
        name="finish",
    )(folded, moved)


def mask_rows(values, live_counts):
    column = jnp.arange(values.shape[-1], dtype=I32) % (values.shape[-1] // 2)
    keep = column[None, None, :] < live_counts[:, None, None]
    return jnp.where(keep, values, jnp.zeros_like(values))


def body(
    currents,
    live_counts,
    radiation,
    sources,
    operator_ids,
    translators,
    stencil,
    stencil_weights,
    receiving,
):
    n_dir, n_grp = lax.axis_size("dir"), lax.axis_size("grp")
    _, _, dirs = translators.shape
    per, incid, _ = currents.shape
    points = stencil.shape[1]
    window = round_up((2 * n_dir + 2) * per, LANES)
    place = jnp.stack([lax.axis_index("dir"), lax.axis_index("grp")]).astype(I32)

    def swap(values, bit):
        return lax.ppermute(values, "dir", [(i, i ^ bit) for i in range(n_dir)])

    def gather(values, last):
        slots = {0: values}
        bit = n_dir // 2
        while bit >= last:
            for j in sorted(slots):
                slots[j + bit] = swap(slots[j], bit)
            bit //= 2
        return [slots[j] for j in sorted(slots)]

    def across(values, step_of):
        pairs = []
        for g in range(n_grp):
            for d in range(n_dir):
                to = g + step_of(d, g)
                if 0 <= to < n_grp:
                    pairs.append((g * n_dir + d, to * n_dir + d))
        return lax.ppermute(values, ("grp", "dir"), pairs)

    shard, part = prepare(
        live_counts, stencil.T, stencil_weights.T, currents, translators, radiation.shape[0]
    )
    shards = gather(shard, 1)
    near = [across(shards[j], lambda d, g, j=j: 1 if d ^ j > d else -1) for j in range(2, n_dir)]
    next_to = []
    for j in range(2):
        next_to.append(across(shards[j], lambda d, g: 1 if g % 2 else -1))
        next_to.append(across(shards[j], lambda d, g: -1 if g % 2 else 1))
    counts, matrix = first_transfer(
        place, sources, operator_ids, translators, n_dir, window
    )
    matrices = [matrix]
    for j, mine in enumerate(gather(part, 2)[1:], 1):
        other = across(mine, lambda d, g: -1 if g % 2 else 1)
        matrices.append(transfer(place, counts, mine, other, 2 * per, window))
    bulk = dirs * ((n_dir + 4) * per + 1) * LANES * 4
    slices = len(matrices)
    size = max(n for n in range(1, slices + 1) if slices % n == 0 and (n == 1 or n * bulk <= 24 << 20))
    sums = None
    for first in range(0, slices, size):
        slots = [2 * j for j in range(first, first + size)]
        early, forward = early_pattern(place, radiation, next_to, slots, incid, dirs)
        own, folded = own_pattern(place, forward, receiving, shards, slots, incid, points)
        kind = BF if size == slices else F32
        pair, moved = translate_field(
            forward, folded, own, early, matrices[first : first + size], near, kind
        )
        product = [finish(folded, moved, pair.shape), pair]
        sums = product if sums is None else [a + b for a, b in zip(sums, product)]
    total = sums[0] + swap(sums[1].astype(BF), 1).astype(F32)
    return mask_rows(total, live_counts)


def solution(mesh):
    placed = (
        P(("grp", "dir"), None, None),
        P(("grp", "dir")),
        P(),
        P("grp", None),
        P("grp", None),
        P(None, None, "dir"),
        P("dir", None),
        P("dir", None),
        P(),
    )
    return jax.shard_map(
        body,
        mesh=mesh,
        in_specs=placed,
        out_specs=P(("grp", "dir"), None, None),
        check_vma=False,
    )
```

time: 68.8 us -> 64.1 us (0.932)
  the two profiles are of different devices: /device:TPU:2 before, /device:TPU:0 now
where the time goes in v6:
time: 64.1 us; the launch traced here: 63.7 us
  Pallas kernels  21.9 us (34%)
  waiting for transfers between devices  19.6 us (31%)
  starting transfers between devices  18.5 us (29%)
  local copies, waits for them, and re-layouts  2.51 us (4%)
  other arithmetic  1.02 us (2%)
    ppermute x5, waiting for transfers between devices, swap(): return lax.ppermute(values, 'dir', [(i, i ^ bit) for i in range(n_dir)])  19.6 us
    ppermute x7, starting transfers between devices, across(): return lax.ppermute(values, ('grp', 'dir'), pairs)  10.3 us
    ppermute x5, starting transfers between devices, swap(): return lax.ppermute(values, 'dir', [(i, i ^ bit) for i in range(n_dir)])  8.18 us
    pallas_call x1, Pallas kernels, translate_field(): pl.pallas_call(functools.partial(field_kernel, len(matrices)), out_shape=...  5.54 us
    pallas_call x1, Pallas kernels, own_pattern(): pl.pallas_call(functools.partial(pattern_kernel, slots, count, incid, RIM...  3.94 us
    pallas_call x1, Pallas kernels, first_transfer(): pl.pallas_call(functools.partial(first_kernel, slots), out_shape=out_shap...  3.8 us
    pallas_call x1, Pallas kernels, prepare(): pl.pallas_call(functools.partial(prepare_kernel, all_dirs), out_shape=(ja...  2.72 us
    pallas_call x1, Pallas kernels, early_pattern(): pl.pallas_call(functools.partial(early_kernel, len(slots), len(shards), i...  2.71 us
  transfers between devices with their start and end apart: 12, of which 4 were waited for; matrix products, arithmetic and copies ran while one was open for 0% of the time, Pallas kernels for 21%

profile of v6, /device:TPU:0, one launch (start us, length us, event | category | flops | bytes accessed | tf_op | source)
XLA Modules:
  0.0 63.7 jit_solution(8210962344906677505)
XLA Ops:
  0.0 2.7 %prepare.1 = (bf16[528,256]{1,0:T(8,128)(2,1)}, bf16[158,2,256]{2,1,0:T(2,128)(2,1)}) custom-call(s32[8]{0:T(128)} %live_ref.1, s32[8,256]{1,0:T(8,128)} %bitcast.4, bf16[8,256]{1,0:T(8,128)(2,1)} %bitcast.5, bf16[8,64,256]{2,1,0:T(8,128)(2,1)} %box_ref.1, bf16[316,2,256]{2,1,0:T(2,128)(2,1)} %table_hbm.1), custom_call_target="tpu_custom_call" | custom-call | flops 1048576 | bytes 1048576 | tf_op jit(solution)/shard_map/prepare/pallas_call | solution.py:97
  2.7 4.1 %collective-permute-start.7 = (bf16[158,2,256]{2,1,0:T(2,128)(2,1)}, bf16[158,2,256]{2,1,0:T(2,128)(2,1)S(1)}, u32[]{:S(2)}, u32[]{:S(2)}) collective-permute-start(bf16[158,2,256]{2,1,0:T(2,128)(2,1)} %get-tuple-element.22), channel_id=1, source_target_pairs={{0,2},{1,3},{2,0},{3,1},{4,6},{5,7},{6,4},{7,5},{8,10},{9,11},{10,... | collective-permute-start | bytes 485384 | tf_op jit(solution)/shard_map/ppermute | solution.py:501
  6.9 1.6 %collective-permute-start.2 = (bf16[528,256]{1,0:T(8,128)(2,1)}, bf16[528,256]{1,0:T(8,128)(2,1)S(1)}, u32[]{:S(2)}, u32[]{:S(2)}) collective-permute-start(bf16[528,256]{1,0:T(8,128)(2,1)} %get-tuple-element.15.refs_0_), channel_id=1, source_target_pairs={{0,1},{1,0},{2,3},{3,2},{4,5},{5,4},{6,7},{7,6},{8,9},{9,8},{10,11... | collective-permute-start | bytes 811016 | tf_op jit(solution)/shard_map/ppermute | solution.py:501
  8.8 6.9 %collective-permute-done.7.mine_ref = bf16[158,2,256]{2,1,0:T(2,128)(2,1)S(1)} collective-permute-done((bf16[158,2,256]{2,1,0:T(2,128)(2,1)}, bf16[158,2,256]{2,1,0:T(2,128)(2,1)S(1)}, u32[]{:S(2)}, u32[]{:S(2)}) %collective-permute-start.7) | collective-permute-done | bytes 161824 | tf_op jit(solution)/shard_map/ppermute | solution.py:501
  15.7 0.7 %collective-permute-start = (bf16[528,256]{1,0:T(8,128)(2,1)}, bf16[528,256]{1,0:T(8,128)(2,1)S(1)}, u32[]{:S(2)}, u32[]{:S(2)}) collective-permute-start(bf16[528,256]{1,0:T(8,128)(2,1)} %get-tuple-element.15.refs_0_), channel_id=1, source_target_pairs={{4,8},{5,9},{6,10},{7,11},{8,4},{9,5},{10,6},{11,7},{12,16},{13,17... | collective-permute-start | bytes 811016 | tf_op jit(solution)/shard_map/ppermute | solution.py:519
  16.3 3.2 %collective-permute-start.1 = (bf16[528,256]{1,0:T(8,128)(2,1)}, bf16[528,256]{1,0:T(8,128)(2,1)S(1)}, u32[]{:S(2)}, u32[]{:S(2)}) collective-permute-start(bf16[528,256]{1,0:T(8,128)(2,1)} %get-tuple-element.15.refs_0_), channel_id=1, source_target_pairs={{0,4},{1,5},{2,6},{3,7},{4,0},{5,1},{6,2},{7,3},{8,12},{9,13},{10,... | collective-permute-start | bytes 811016 | tf_op jit(solution)/shard_map/ppermute | solution.py:519
  19.5 1.3 %collective-permute-done.2.refs_1_ = bf16[528,256]{1,0:T(8,128)(2,1)S(1)} collective-permute-done((bf16[528,256]{1,0:T(8,128)(2,1)}, bf16[528,256]{1,0:T(8,128)(2,1)S(1)}, u32[]{:S(2)}, u32[]{:S(2)}) %collective-permute-start.2) | collective-permute-done | bytes 270368 | tf_op jit(solution)/shard_map/ppermute | solution.py:501
  20.8 0.7 %collective-permute-start.3 = (bf16[528,256]{1,0:T(8,128)(2,1)S(1)}, bf16[528,256]{1,0:T(8,128)(2,1)S(1)}, u32[]{:S(2)}, u32[]{:S(2)}) collective-permute-start(bf16[528,256]{1,0:T(8,128)(2,1)S(1)} %collective-permute-done.2.refs_1_), channel_id=1, source_target_pairs={{4,8},{5,9},{6,10},{7,11},{8,4},{9,5},{10,6},{11,7},{12,16},{13,17... | collective-permute-start | bytes 811016 | tf_op jit(solution)/shard_map/ppermute | solution.py:519
  21.5 4.8 %collective-permute-done.5.refs_2_ = bf16[528,256]{1,0:T(8,128)(2,1)S(1)} collective-permute-done((bf16[528,256]{1,0:T(8,128)(2,1)}, bf16[528,256]{1,0:T(8,128)(2,1)S(1)}, u32[]{:S(2)}, u32[]{:S(2)}) %collective-permute-start.5) | collective-permute-done | bytes 270368 | tf_op jit(solution)/shard_map/ppermute | solution.py:501
  26.3 0.8 %collective-permute-start.6 = (bf16[528,256]{1,0:T(8,128)(2,1)S(1)}, bf16[528,256]{1,0:T(8,128)(2,1)S(1)}, u32[]{:S(2)}, u32[]{:S(2)}) collective-permute-start(bf16[528,256]{1,0:T(8,128)(2,1)S(1)} %collective-permute-done.5.refs_2_), channel_id=1, source_target_pairs={{0,1},{1,0},{2,3},{3,2},{4,5},{5,4},{6,7},{7,6},{8,9},{9,8},{10,11... | collective-permute-start | bytes 811016 | tf_op jit(solution)/shard_map/ppermute | solution.py:501
  27.3 1.0 %copy-done = bf16[316,2,256]{2,1,0:T(2,128)(2,1)S(1)} copy-done((bf16[316,2,256]{2,1,0:T(2,128)(2,1)S(1)}, bf16[316,2,256]{2,1,0:T(2,128)(2,1)}, u32[]{:S(2)}) %copy-start) | copy-done | bytes 323608
  28.2 0.8 %copy-done.4 = s32[32,189]{1,0:T(8,128)S(1)} copy-done((s32[32,189]{1,0:T(8,128)S(1)}, s32[32,189]{1,0:T(8,128)}, u32[]{:S(2)}) %copy-start.4) | copy-done | bytes 24216
  29.0 0.8 %copy-done.5 = s32[32,189]{1,0:T(8,128)S(1)} copy-done((s32[32,189]{1,0:T(8,128)S(1)}, s32[32,189]{1,0:T(8,128)}, u32[]{:S(2)}) %copy-start.5) | copy-done | bytes 24216
  29.7 3.8 %first.1 = (bf16[384,2048]{1,0:T(8,128)(2,1)S(1)}, bf16[256,32,128]{2,1,0:T(8,128)(2,1)S(1)}) custom-call(s32[2]{0:T(128)S(1)} %pad_add_fusion.refs_0_.place_ref, s32[32,189]{1,0:T(8,128)S(1)} %copy-done.4, s32[32,189]{1,0:T(8,128)S(1)} %copy-done.5, bf16[316,2,256]{2,1,0:T(2,128)(2,1)S(1)} %copy-done), custom_call_target="tpu_custom_call" | custom-call | flops 1073741824 | bytes 1048576 | tf_op jit(solution)/shard_map/first/pallas_call | solution.py:208
  33.6 2.7 %transfer.1.refs_1_ = bf16[256,32,128]{2,1,0:T(8,128)(2,1)S(1)} custom-call(s32[2]{0:T(128)S(1)} %pad_add_fusion.refs_0_.place_ref, bf16[384,2048]{1,0:T(8,128)(2,1)S(1)} %get-tuple-element.21.counts_ref, bf16[158,2,256]{2,1,0:T(2,128)(2,1)S(1)} %collective-permute-done.7.mine_ref, bf16[158,2,256]{2,1,0:T(2,128)(2,1)S(1)} %collective-permute-done.8.other_ref), custom_call_target="tpu_custom_call" | custom-call | flops 1073741824 | bytes 1048576 | tf_op jit(solution)/shard_map/transfer/pallas_call | solution.py:243
  36.3 2.3 %collective-permute-start.9 = (bf16[528,256]{1,0:T(8,128)(2,1)S(1)}, bf16[528,256]{1,0:T(8,128)(2,1)S(1)}, u32[]{:S(2)}, u32[]{:S(2)}) collective-permute-start(bf16[528,256]{1,0:T(8,128)(2,1)S(1)} %collective-permute-done.5.refs_2_), channel_id=1, source_target_pairs={{0,4},{1,5},{4,8},{5,9},{6,2},{7,3},{8,12},{9,13},{10,6},{11,7},{1... | collective-permute-start | bytes 811016 | tf_op jit(solution)/shard_map/ppermute | solution.py:519
  38.5 3.5 %collective-permute-start.10 = (bf16[528,256]{1,0:T(8,128)(2,1)S(1)}, bf16[528,256]{1,0:T(8,128)(2,1)S(1)}, u32[]{:S(2)}, u32[]{:S(2)}) collective-permute-start(bf16[528,256]{1,0:T(8,128)(2,1)S(1)} %collective-permute-done.6.refs_3_), channel_id=1, source_target_pairs={{0,4},{1,5},{4,8},{5,9},{6,2},{7,3},{8,12},{9,13},{10,6},{11,7},{1... | collective-permute-start | bytes 811016 | tf_op jit(solution)/shard_map/ppermute | solution.py:519
  42.1 2.7 %early.1 = (bf16[512,32,128]{2,1,0:T(8,128)(2,1)S(1)}, bf16[512,256]{1,0:T(8,128)(2,1)S(1)}) custom-call(s32[2]{0:T(128)S(1)} %pad_add_fusion.refs_0_.place_ref, bf16[1024,2,128]{2,1,0:T(2,128)(2,1)S(1)} %copy-done.1, bf16[1024,2,128]{2,1,0:T(2,128)(2,1)S(1)} %copy-done.1, bf16[528,256]{1,0:T(8,128)(2,1)S(1)} %collective-permute-done.refs_3_, ...), custom_call_target="tpu_custom_call" | custom-call | flops 4294967296 | bytes 4194304 | tf_op jit(solution)/shard_map/early/pallas_call | solution.py:303
  44.8 3.9 %pattern.1 = (bf16[512,32,128]{2,1,0:T(8,128)(2,1)S(1)}, bf16[512,256]{1,0:T(8,128)(2,1)S(1)}) custom-call(s32[2]{0:T(128)S(1)} %pad_add_fusion.refs_0_.place_ref, bf16[512,256]{1,0:T(8,128)(2,1)S(1)} %get-tuple-element.16.turned_ref.forward_ref, bf16[1024,2,128]{2,1,0:T(2,128)(2,1)S(1)} %copy-done.2, bf16[528,256]{1,0:T(8,128)(2,1)S(1)} %copy-done.3, ...), custom_call_target="tpu_custom_call" | custom-call | flops 4294967296 | bytes 4194304 | tf_op jit(solution)/shard_map/pattern/pallas_call | solution.py:383
  48.8 5.5 %field.1 = (bf16[8,64,256]{2,1,0:T(8,128)(2,1)S(1)}, f32[8704,128]{1,0:T(8,128)S(1)}) custom-call(bf16[512,256]{1,0:T(8,128)(2,1)S(1)} %get-tuple-element.16.turned_ref.forward_ref, bf16[512,256]{1,0:T(8,128)(2,1)S(1)} %get-tuple-element.17.folded_ref, bf16[512,32,128]{2,1,0:T(8,128)(2,1)S(1)} %get-tuple-element.18.own_ref, ...), custom_call_target="tpu_custom_call" | custom-call | flops 4294967296 | bytes 16777216 | tf_op jit(solution)/shard_map/field/pallas_call | solution.py:447
  54.3 1.3 %collective-permute-start.11 = (bf16[8,64,256]{2,1,0:T(8,128)(2,1)S(1)}, bf16[8,64,256]{2,1,0:T(8,128)(2,1)S(1)}, u32[]{:S(2)}, u32[]{:S(2)}) collective-permute-start(bf16[8,64,256]{2,1,0:T(8,128)(2,1)S(1)} %get-tuple-element.24), channel_id=1, source_target_pairs={{0,1},{1,0},{2,3},{3,2},{4,5},{5,4},{6,7},{7,6},{8,9},{9,8},{10,11... | collective-permute-start | bytes 786440 | tf_op jit(solution)/shard_map/ppermute | solution.py:501
  55.7 0.5 finish.1
  56.2 6.6 %collective-permute-done.11 = bf16[8,64,256]{2,1,0:T(8,128)(2,1)S(1)} collective-permute-done((bf16[8,64,256]{2,1,0:T(8,128)(2,1)S(1)}, bf16[8,64,256]{2,1,0:T(8,128)(2,1)S(1)}, u32[]{:S(2)}, u32[]{:S(2)}) %collective-permute-start.11) | collective-permute-done | bytes 262176 | tf_op jit(solution)/shard_map/ppermute | solution.py:501
  62.8 0.9 %add_select_fusion = f32[8,64,256]{2,1,0:T(8,128)} fusion(f32[8,64,256]{2,1,0:T(8,128)S(1)} %finish.1, bf16[8,64,256]{2,1,0:T(8,128)(2,1)S(1)} %collective-permute-done.11, pred[8,256]{1,0:T(8,128)(4,1)S(1)} %broadcast_compare_fusion), kind=kLoop, calls=%fused_computation | loop fusion | flops 393216 | bytes 1312768 | tf_op jit(solution)/shard_map/jit(_where)/select_n | solution.py:479
  (25 shorter events, 0.5 us)
Async XLA Ops:
  0.0 42.1 %copy-start.1 = (bf16[1024,2,128]{2,1,0:T(2,128)(2,1)S(1)}, bf16[1024,2,128]{2,1,0:T(2,128)(2,1)}, u32[]{:S(2)}) copy-start(bf16[1024,2,128]{2,1,0:T(2,128)(2,1)} %refs_2_.1) | copy-start | bytes 1572868
  2.7 12.9 %collective-permute-start.7 = (bf16[158,2,256]{2,1,0:T(2,128)(2,1)}, bf16[158,2,256]{2,1,0:T(2,128)(2,1)S(1)}, u32[]{:S(2)}, u32[]{:S(2)}) collective-permute-start(bf16[158,2,256]{2,1,0:T(2,128)(2,1)} %get-tuple-element.22), channel_id=1, source_target_pairs={{0,2},{1,3},{2,0},{3,1},{4,6},{5,7},{6,4},{7,5},{8,10},{9,11},{10,... | collective-permute-start | bytes 485384 | tf_op jit(solution)/shard_map/ppermute | solution.py:501
  6.9 13.9 %collective-permute-start.2 = (bf16[528,256]{1,0:T(8,128)(2,1)}, bf16[528,256]{1,0:T(8,128)(2,1)S(1)}, u32[]{:S(2)}, u32[]{:S(2)}) collective-permute-start(bf16[528,256]{1,0:T(8,128)(2,1)} %get-tuple-element.15.refs_0_), channel_id=1, source_target_pairs={{0,1},{1,0},{2,3},{3,2},{4,5},{5,4},{6,7},{7,6},{8,9},{9,8},{10,11... | collective-permute-start | bytes 811016 | tf_op jit(solution)/shard_map/ppermute | solution.py:501
  8.4 17.9 %collective-permute-start.5 = (bf16[528,256]{1,0:T(8,128)(2,1)}, bf16[528,256]{1,0:T(8,128)(2,1)S(1)}, u32[]{:S(2)}, u32[]{:S(2)}) collective-permute-start(bf16[528,256]{1,0:T(8,128)(2,1)} %get-tuple-element.15.refs_0_), channel_id=1, source_target_pairs={{0,2},{1,3},{2,0},{3,1},{4,6},{5,7},{6,4},{7,5},{8,10},{9,11},{10,... | collective-permute-start | bytes 811016 | tf_op jit(solution)/shard_map/ppermute | solution.py:501
  15.6 10.7 %collective-permute-start.8 = (bf16[158,2,256]{2,1,0:T(2,128)(2,1)S(1)}, bf16[158,2,256]{2,1,0:T(2,128)(2,1)S(1)}, u32[]{:S(2)}, u32[]{:S(2)}) collective-permute-start(bf16[158,2,256]{2,1,0:T(2,128)(2,1)S(1)} %collective-permute-done.7.mine_ref), channel_id=1, source_target_pairs={{0,4},{1,5},{2,6},{3,7},{4,0},{5,1},{6,2},{7,3},{8,12},{9,13},{10,... | collective-permute-start | bytes 485384 | tf_op jit(solution)/shard_map/ppermute | solution.py:519
  15.7 20.6 %collective-permute-start = (bf16[528,256]{1,0:T(8,128)(2,1)}, bf16[528,256]{1,0:T(8,128)(2,1)S(1)}, u32[]{:S(2)}, u32[]{:S(2)}) collective-permute-start(bf16[528,256]{1,0:T(8,128)(2,1)} %get-tuple-element.15.refs_0_), channel_id=1, source_target_pairs={{4,8},{5,9},{6,10},{7,11},{8,4},{9,5},{10,6},{11,7},{12,16},{13,17... | collective-permute-start | bytes 811016 | tf_op jit(solution)/shard_map/ppermute | solution.py:519
  16.3 25.7 %collective-permute-start.1 = (bf16[528,256]{1,0:T(8,128)(2,1)}, bf16[528,256]{1,0:T(8,128)(2,1)S(1)}, u32[]{:S(2)}, u32[]{:S(2)}) collective-permute-start(bf16[528,256]{1,0:T(8,128)(2,1)} %get-tuple-element.15.refs_0_), channel_id=1, source_target_pairs={{0,4},{1,5},{2,6},{3,7},{4,0},{5,1},{6,2},{7,3},{8,12},{9,13},{10,... | collective-permute-start | bytes 811016 | tf_op jit(solution)/shard_map/ppermute | solution.py:519
  20.8 21.2 %collective-permute-start.3 = (bf16[528,256]{1,0:T(8,128)(2,1)S(1)}, bf16[528,256]{1,0:T(8,128)(2,1)S(1)}, u32[]{:S(2)}, u32[]{:S(2)}) collective-permute-start(bf16[528,256]{1,0:T(8,128)(2,1)S(1)} %collective-permute-done.2.refs_1_), channel_id=1, source_target_pairs={{4,8},{5,9},{6,10},{7,11},{8,4},{9,5},{10,6},{11,7},{12,16},{13,17... | collective-permute-start | bytes 811016 | tf_op jit(solution)/shard_map/ppermute | solution.py:519
  26.3 15.7 %collective-permute-start.4 = (bf16[528,256]{1,0:T(8,128)(2,1)S(1)}, bf16[528,256]{1,0:T(8,128)(2,1)S(1)}, u32[]{:S(2)}, u32[]{:S(2)}) collective-permute-start(bf16[528,256]{1,0:T(8,128)(2,1)S(1)} %collective-permute-done.2.refs_1_), channel_id=1, source_target_pairs={{0,4},{1,5},{2,6},{3,7},{4,0},{5,1},{6,2},{7,3},{8,12},{9,13},{10,... | collective-permute-start | bytes 811016 | tf_op jit(solution)/shard_map/ppermute | solution.py:519
  26.3 12.2 %collective-permute-start.6 = (bf16[528,256]{1,0:T(8,128)(2,1)S(1)}, bf16[528,256]{1,0:T(8,128)(2,1)S(1)}, u32[]{:S(2)}, u32[]{:S(2)}) collective-permute-start(bf16[528,256]{1,0:T(8,128)(2,1)S(1)} %collective-permute-done.5.refs_2_), channel_id=1, source_target_pairs={{0,1},{1,0},{2,3},{3,2},{4,5},{5,4},{6,7},{7,6},{8,9},{9,8},{10,11... | collective-permute-start | bytes 811016 | tf_op jit(solution)/shard_map/ppermute | solution.py:501
  27.3 1.0 %copy-start = (bf16[316,2,256]{2,1,0:T(2,128)(2,1)S(1)}, bf16[316,2,256]{2,1,0:T(2,128)(2,1)}, u32[]{:S(2)}) copy-start(bf16[316,2,256]{2,1,0:T(2,128)(2,1)} %table_hbm.1) | copy-start | bytes 970756
  28.2 0.8 %copy-start.4 = (s32[32,189]{1,0:T(8,128)S(1)}, s32[32,189]{1,0:T(8,128)}, u32[]{:S(2)}) copy-start(s32[32,189]{1,0:T(8,128)} %source_hbm.1) | copy-start | bytes 72580
  29.0 0.8 %copy-start.5 = (s32[32,189]{1,0:T(8,128)S(1)}, s32[32,189]{1,0:T(8,128)}, u32[]{:S(2)}) copy-start(s32[32,189]{1,0:T(8,128)} %kind_hbm.1) | copy-start | bytes 72580
  36.2 8.6 %copy-start.2 = (bf16[1024,2,128]{2,1,0:T(2,128)(2,1)S(1)}, bf16[1024,2,128]{2,1,0:T(2,128)(2,1)}, u32[]{:S(2)}) copy-start(bf16[1024,2,128]{2,1,0:T(2,128)(2,1)} %receive_ref.1) | copy-start | bytes 1572868
  36.2 8.6 %copy-start.3 = (bf16[528,256]{1,0:T(8,128)(2,1)S(1)}, bf16[528,256]{1,0:T(8,128)(2,1)}, u32[]{:S(2)}) copy-start(bf16[528,256]{1,0:T(8,128)(2,1)} %get-tuple-element.15.refs_0_) | copy-start | bytes 811012
  36.3 12.5 %collective-permute-start.9 = (bf16[528,256]{1,0:T(8,128)(2,1)S(1)}, bf16[528,256]{1,0:T(8,128)(2,1)S(1)}, u32[]{:S(2)}, u32[]{:S(2)}) collective-permute-start(bf16[528,256]{1,0:T(8,128)(2,1)S(1)} %collective-permute-done.5.refs_2_), channel_id=1, source_target_pairs={{0,4},{1,5},{4,8},{5,9},{6,2},{7,3},{8,12},{9,13},{10,6},{11,7},{1... | collective-permute-start | bytes 811016 | tf_op jit(solution)/shard_map/ppermute | solution.py:519
  38.5 10.2 %collective-permute-start.10 = (bf16[528,256]{1,0:T(8,128)(2,1)S(1)}, bf16[528,256]{1,0:T(8,128)(2,1)S(1)}, u32[]{:S(2)}, u32[]{:S(2)}) collective-permute-start(bf16[528,256]{1,0:T(8,128)(2,1)S(1)} %collective-permute-done.6.refs_3_), channel_id=1, source_target_pairs={{0,4},{1,5},{4,8},{5,9},{6,2},{7,3},{8,12},{9,13},{10,6},{11,7},{1... | collective-permute-start | bytes 811016 | tf_op jit(solution)/shard_map/ppermute | solution.py:519
  48.8 6.9 %copy-start.6 = (s32[8]{0:T(128)S(1)}, s32[8]{0:T(128)}, u32[]{:S(2)}) copy-start(s32[8]{0:T(128)} %live_ref.1) | copy-start | bytes 100
  54.3 8.5 %collective-permute-start.11 = (bf16[8,64,256]{2,1,0:T(8,128)(2,1)S(1)}, bf16[8,64,256]{2,1,0:T(8,128)(2,1)S(1)}, u32[]{:S(2)}, u32[]{:S(2)}) collective-permute-start(bf16[8,64,256]{2,1,0:T(8,128)(2,1)S(1)} %get-tuple-element.24), channel_id=1, source_target_pairs={{0,1},{1,0},{2,3},{3,2},{4,5},{5,4},{6,7},{7,6},{8,9},{9,8},{10,11... | collective-permute-start | bytes 786440 | tf_op jit(solution)/shard_map/ppermute | solution.py:501

commit v7 on v6

--- a/solution.py
+++ b/solution.py
@@ -145,7 +145,7 @@
 
 def fill_matrix(low, high, counts_ref, matrix_ref, table, wide):
     dirs, rows, window = matrix_ref.shape
-    boxes = rows // 2
+    boxes, per = rows // 2, rows // 4
     half = low.shape[0]
     gap = round_up(half, 16) - half
     for c in range(2):
@@ -158,8 +158,9 @@
         for i in range(2):
             for c in range(window // LANES):
                 part = entries[:, i * window + c * LANES : i * window + (c + 1) * LANES]
-                wide[c, pl.ds(at + i, dirs, stride=rows + 1), :] = part[:dirs]
-                wide[c, pl.ds(at + i + boxes, dirs, stride=rows + 1), :] = part[dirs:]
+                spot = at + i + (at + i) // per * per
+                wide[c, pl.ds(spot, dirs, stride=rows + 1), :] = part[:dirs]
+                wide[c, pl.ds(spot + per, dirs, stride=rows + 1), :] = part[dirs:]
 
     def narrow(k):
         for c in range(window // LANES):
@@ -408,31 +409,39 @@
             out_ref[begin + i] = jnp.concatenate([re, im], axis=1).astype(out_ref.dtype)
 
 
+def translate(part, matrix_refs, own_ref, early_ref, near, moved):
+    rows, own_boxes, width = own_ref.shape
+    dirs, lines, _ = matrix_refs[0].shape
+    per, half = lines // 4, width // 2
+    near_boxes = near.shape[0] // rows - 1
+    window = own_boxes + early_ref.shape[1] + near_boxes
+    sign = jnp.where(count_of((per, width), 1) < half, -1.0, 1.0).astype(F32)
+    for at, matrix_ref in enumerate(matrix_refs):
+
+        def two(i, at=at, matrix_ref=matrix_ref):
+            fields, weights = [], []
+            for j in (2 * i, 2 * i + 1):
+                k = at * dirs + j
+                around = near[pl.ds(k * (near_boxes + 1), near_boxes), :].astype(BF)
+                fields.append(jnp.concatenate([own_ref[k], early_ref[k], around], axis=0))
+                weights.append(matrix_ref[j][2 * per * part : 2 * per * (part + 1), :window])
+            both = dot(jnp.concatenate(weights, axis=0), jnp.concatenate(fields, axis=1), NN)
+            for j in range(2):
+                each = both[2 * per * j : 2 * per * (j + 1), width * j : width * (j + 1)]
+                turned = pltpu.roll(each[per:], half, 1)
+                begin = (at * dirs + 2 * i + j) * (per + 1)
+                moved[pl.ds(begin, per), :] = each[:per] + sign * turned
+
+        unrolled(dirs // 2, 32, two)
+
+
 def field_kernel(slices, forward_ref, folded_ref, own_ref, early_ref, *refs):
     matrix_refs, refs = refs[:slices], refs[slices:]
-    box_refs, (pair_ref, moved, near) = refs[:-3], refs[-3:]
-    rows, own_boxes, width = own_ref.shape
+    box_refs, (pair_ref, near, moved) = refs[:-3], refs[-3:]
     per, half, _ = pair_ref.shape
-    boxes = 2 * per
-    near_boxes = len(box_refs) * per
-    radiate(forward_ref, box_refs, half, near, near_boxes + 1)
-    sign = jnp.where(count_of((boxes, width), 1) < half, -1.0, 1.0).astype(F32)
-    stride = boxes + 1
-    dirs = rows // slices
-    window = own_boxes + early_ref.shape[1] + near_boxes
-    for at, matrix_ref in enumerate(matrix_refs):
-
-        def translate(i, at=at, matrix_ref=matrix_ref):
-            k = at * dirs + i
-            around = near[pl.ds(k * (near_boxes + 1), near_boxes), :].astype(BF)
-            fields = jnp.concatenate([own_ref[k], early_ref[k], around], axis=0)
-            both = dot(matrix_ref[i][:, :window], fields, NN)
-            turned = pltpu.roll(both[boxes:], half, 1)
-            moved[pl.ds(k * stride, boxes), :] = both[:boxes] + sign * turned
-
-        unrolled(dirs, 64, translate)
-
-    receive(moved, folded_ref, per, pair_ref, stride)
+    radiate(forward_ref, box_refs, half, near, len(box_refs) * per + 1)
+    translate(1, matrix_refs, own_ref, early_ref, near, moved)
+    receive(moved, folded_ref, 0, pair_ref, per + 1)
 
 
 def translate_field(forward, folded, own, early, matrices, near, kind):
@@ -441,9 +450,9 @@
     shape = (per, width // 2, folded.shape[1])
     out_shape = (
         jax.ShapeDtypeStruct(shape, kind),
-        jax.ShapeDtypeStruct((rows * (2 * per + 1), width), F32),
-    )
-    scratch = [pltpu.VMEM((rows * (len(near) * per + 1), width), F32)]
+        jax.ShapeDtypeStruct((rows * (len(near) * per + 1), width), F32),
+    )
+    scratch = [pltpu.VMEM((rows * (per + 1), width), F32)]
     return pl.pallas_call(
         functools.partial(field_kernel, len(matrices)),
         out_shape=out_shape,
@@ -456,21 +465,26 @@
     )(forward, folded, own, early, *matrices, *near)
 
 
-def finish_kernel(folded_ref, moved_ref, out_ref):
-    receive(moved_ref, folded_ref, 0, out_ref, 2 * out_ref.shape[0] + 1)
-
-
-def finish(folded, moved, shape):
+def finish_kernel(slices, folded_ref, own_ref, early_ref, near_ref, *refs):
+    matrix_refs, (out_ref, moved) = refs[:slices], refs[slices:]
+    translate(0, matrix_refs, own_ref, early_ref, near_ref, moved)
+    receive(moved, folded_ref, 0, out_ref, out_ref.shape[0] + 1)
+
+
+def finish(folded, own, early, around, matrices, shape):
     out_shape = jax.ShapeDtypeStruct(shape, F32)
-    return pl.pallas_call(
-        finish_kernel,
+    rows, _, width = own.shape
+    scratch = [pltpu.VMEM((rows * (shape[0] + 1), width), F32)]
+    return pl.pallas_call(
+        functools.partial(finish_kernel, len(matrices)),
         out_shape=out_shape,
-        in_specs=[VMEM, VMEM],
+        in_specs=[VMEM] * (4 + len(matrices)),
         out_specs=VMEM,
-        compiler_params=grant([out_shape, folded, moved]),
-        cost_estimate=cost(1 << 28, 1 << 20),
+        scratch_shapes=scratch,
+        compiler_params=grant(scratch, [out_shape, folded, own, early, around], matrices),
+        cost_estimate=cost(2 << 30, 8 << 20),
         name="finish",
-    )(folded, moved)
+    )(folded, own, early, around, *matrices)
 
 
 def mask_rows(values, live_counts):
@@ -536,17 +550,20 @@
         matrices.append(transfer(place, counts, mine, other, 2 * per, window))
     bulk = dirs * ((n_dir + 4) * per + 1) * LANES * 4
     slices = len(matrices)
-    size = max(n for n in range(1, slices + 1) if slices % n == 0 and (n == 1 or n * bulk <= 24 << 20))
+    size = max(n for n in range(1, slices + 1) if slices % n == 0 and (n == 1 or n * bulk <= 20 << 20))
     sums = None
     for first in range(0, slices, size):
         slots = [2 * j for j in range(first, first + size)]
         early, forward = early_pattern(place, radiation, next_to, slots, incid, dirs)
         own, folded = own_pattern(place, forward, receiving, shards, slots, incid, points)
         kind = BF if size == slices else F32
-        pair, moved = translate_field(
+        pair, around = translate_field(
             forward, folded, own, early, matrices[first : first + size], near, kind
         )
-        product = [finish(folded, moved, pair.shape), pair]
+        mine = finish(
+            folded, own, early, around, matrices[first : first + size], pair.shape
+        )
+        product = [mine, pair]
         sums = product if sums is None else [a + b for a, b in zip(sums, product)]
     total = sums[0] + swap(sums[1].astype(BF), 1).astype(F32)
     return mask_rows(total, live_counts)

time: 64.1 us -> 62.7 us (0.978)
  waiting for transfers between devices: 19.6 us -> 16.5 us
  Pallas kernels: 21.9 us -> 23.7 us
    ppermute x5, waiting for transfers between devices: 19.6 us -> 16.4 us  [swap(): return lax.ppermute(values, 'dir', [(i, i ^ bit) for i in range(n_dir)])]
    pallas_call x1, Pallas kernels: 0.48 us -> 3.56 us  [finish(): pl.pallas_call(functools.partial(finish_kernel, len(matrices)), out_shape...]
    pallas_call x1, Pallas kernels: 5.54 us -> 4.31 us  [translate_field(): pl.pallas_call(functools.partial(field_kernel, len(matrices)), out_shape=...]
  transfers between devices with their start and end apart: 12 -> 12, of which waited for: 4 -> 4; matrix products, arithmetic and copies ran while one was open for 0% -> 0% of each run, Pallas kernels for 21% -> 27%
where the time goes in v7:
time: 62.7 us; the launch traced here: 62.3 us
  Pallas kernels  23.7 us (38%)
  starting transfers between devices  18.5 us (30%)
  waiting for transfers between devices  16.5 us (26%)
  local copies, waits for them, and re-layouts  2.51 us (4%)
  other arithmetic  1.01 us (2%)
    ppermute x5, waiting for transfers between devices, swap(): return lax.ppermute(values, 'dir', [(i, i ^ bit) for i in range(n_dir)])  16.4 us
    ppermute x7, starting transfers between devices, across(): return lax.ppermute(values, ('grp', 'dir'), pairs)  10.3 us
    ppermute x5, starting transfers between devices, swap(): return lax.ppermute(values, 'dir', [(i, i ^ bit) for i in range(n_dir)])  8.19 us
    pallas_call x1, Pallas kernels, translate_field(): pl.pallas_call(functools.partial(field_kernel, len(matrices)), out_shape=...  4.31 us
    pallas_call x1, Pallas kernels, own_pattern(): pl.pallas_call(functools.partial(pattern_kernel, slots, count, incid, RIM...  3.93 us
    pallas_call x1, Pallas kernels, first_transfer(): pl.pallas_call(functools.partial(first_kernel, slots), out_shape=out_shap...  3.79 us
    pallas_call x1, Pallas kernels, finish(): pl.pallas_call(functools.partial(finish_kernel, len(matrices)), out_shape...  3.56 us
    pallas_call x1, Pallas kernels, prepare(): pl.pallas_call(functools.partial(prepare_kernel, all_dirs), out_shape=(ja...  2.72 us
  transfers between devices with their start and end apart: 12, of which 4 were waited for; matrix products, arithmetic and copies ran while one was open for 0% of the time, Pallas kernels for 27%

profile of v7, /device:TPU:0, one launch (start us, length us, event | category | flops | bytes accessed | tf_op | source)
XLA Modules:
  0.0 62.3 jit_solution(10374910509353642324)
XLA Ops:
  0.0 2.7 %prepare.1 = (bf16[528,256]{1,0:T(8,128)(2,1)}, bf16[158,2,256]{2,1,0:T(2,128)(2,1)}) custom-call(s32[8]{0:T(128)} %live_ref.1, s32[8,256]{1,0:T(8,128)} %bitcast.4, bf16[8,256]{1,0:T(8,128)(2,1)} %bitcast.5, bf16[8,64,256]{2,1,0:T(8,128)(2,1)} %box_ref.1, bf16[316,2,256]{2,1,0:T(2,128)(2,1)} %table_hbm.1), custom_call_target="tpu_custom_call" | custom-call | flops 1048576 | bytes 1048576 | tf_op jit(solution)/shard_map/prepare/pallas_call | solution.py:97
  2.7 4.1 %collective-permute-start.7 = (bf16[158,2,256]{2,1,0:T(2,128)(2,1)}, bf16[158,2,256]{2,1,0:T(2,128)(2,1)S(1)}, u32[]{:S(2)}, u32[]{:S(2)}) collective-permute-start(bf16[158,2,256]{2,1,0:T(2,128)(2,1)} %get-tuple-element.22), channel_id=1, source_target_pairs={{0,2},{1,3},{2,0},{3,1},{4,6},{5,7},{6,4},{7,5},{8,10},{9,11},{10,... | collective-permute-start | bytes 485384 | tf_op jit(solution)/shard_map/ppermute | solution.py:515
  6.9 1.6 %collective-permute-start.2 = (bf16[528,256]{1,0:T(8,128)(2,1)}, bf16[528,256]{1,0:T(8,128)(2,1)S(1)}, u32[]{:S(2)}, u32[]{:S(2)}) collective-permute-start(bf16[528,256]{1,0:T(8,128)(2,1)} %get-tuple-element.15.refs_0_), channel_id=1, source_target_pairs={{0,1},{1,0},{2,3},{3,2},{4,5},{5,4},{6,7},{7,6},{8,9},{9,8},{10,11... | collective-permute-start | bytes 811016 | tf_op jit(solution)/shard_map/ppermute | solution.py:515
  8.8 6.9 %collective-permute-done.7.mine_ref = bf16[158,2,256]{2,1,0:T(2,128)(2,1)S(1)} collective-permute-done((bf16[158,2,256]{2,1,0:T(2,128)(2,1)}, bf16[158,2,256]{2,1,0:T(2,128)(2,1)S(1)}, u32[]{:S(2)}, u32[]{:S(2)}) %collective-permute-start.7) | collective-permute-done | bytes 161824 | tf_op jit(solution)/shard_map/ppermute | solution.py:515
  15.7 0.7 %collective-permute-start = (bf16[528,256]{1,0:T(8,128)(2,1)}, bf16[528,256]{1,0:T(8,128)(2,1)S(1)}, u32[]{:S(2)}, u32[]{:S(2)}) collective-permute-start(bf16[528,256]{1,0:T(8,128)(2,1)} %get-tuple-element.15.refs_0_), channel_id=1, source_target_pairs={{4,8},{5,9},{6,10},{7,11},{8,4},{9,5},{10,6},{11,7},{12,16},{13,17... | collective-permute-start | bytes 811016 | tf_op jit(solution)/shard_map/ppermute | solution.py:533
  16.3 3.2 %collective-permute-start.1 = (bf16[528,256]{1,0:T(8,128)(2,1)}, bf16[528,256]{1,0:T(8,128)(2,1)S(1)}, u32[]{:S(2)}, u32[]{:S(2)}) collective-permute-start(bf16[528,256]{1,0:T(8,128)(2,1)} %get-tuple-element.15.refs_0_), channel_id=1, source_target_pairs={{0,4},{1,5},{2,6},{3,7},{4,0},{5,1},{6,2},{7,3},{8,12},{9,13},{10,... | collective-permute-start | bytes 811016 | tf_op jit(solution)/shard_map/ppermute | solution.py:533
  19.6 1.2 %collective-permute-done.2.refs_1_ = bf16[528,256]{1,0:T(8,128)(2,1)S(1)} collective-permute-done((bf16[528,256]{1,0:T(8,128)(2,1)}, bf16[528,256]{1,0:T(8,128)(2,1)S(1)}, u32[]{:S(2)}, u32[]{:S(2)}) %collective-permute-start.2) | collective-permute-done | bytes 270368 | tf_op jit(solution)/shard_map/ppermute | solution.py:515
  20.8 0.7 %collective-permute-start.3 = (bf16[528,256]{1,0:T(8,128)(2,1)S(1)}, bf16[528,256]{1,0:T(8,128)(2,1)S(1)}, u32[]{:S(2)}, u32[]{:S(2)}) collective-permute-start(bf16[528,256]{1,0:T(8,128)(2,1)S(1)} %collective-permute-done.2.refs_1_), channel_id=1, source_target_pairs={{4,8},{5,9},{6,10},{7,11},{8,4},{9,5},{10,6},{11,7},{12,16},{13,17... | collective-permute-start | bytes 811016 | tf_op jit(solution)/shard_map/ppermute | solution.py:533
  21.5 4.8 %collective-permute-done.5.refs_2_ = bf16[528,256]{1,0:T(8,128)(2,1)S(1)} collective-permute-done((bf16[528,256]{1,0:T(8,128)(2,1)}, bf16[528,256]{1,0:T(8,128)(2,1)S(1)}, u32[]{:S(2)}, u32[]{:S(2)}) %collective-permute-start.5) | collective-permute-done | bytes 270368 | tf_op jit(solution)/shard_map/ppermute | solution.py:515
  26.3 0.8 %collective-permute-start.6 = (bf16[528,256]{1,0:T(8,128)(2,1)S(1)}, bf16[528,256]{1,0:T(8,128)(2,1)S(1)}, u32[]{:S(2)}, u32[]{:S(2)}) collective-permute-start(bf16[528,256]{1,0:T(8,128)(2,1)S(1)} %collective-permute-done.5.refs_2_), channel_id=1, source_target_pairs={{0,1},{1,0},{2,3},{3,2},{4,5},{5,4},{6,7},{7,6},{8,9},{9,8},{10,11... | collective-permute-start | bytes 811016 | tf_op jit(solution)/shard_map/ppermute | solution.py:515
  27.2 1.0 %copy-done = bf16[316,2,256]{2,1,0:T(2,128)(2,1)S(1)} copy-done((bf16[316,2,256]{2,1,0:T(2,128)(2,1)S(1)}, bf16[316,2,256]{2,1,0:T(2,128)(2,1)}, u32[]{:S(2)}) %copy-start) | copy-done | bytes 323608
  28.2 0.8 %copy-done.4 = s32[32,189]{1,0:T(8,128)S(1)} copy-done((s32[32,189]{1,0:T(8,128)S(1)}, s32[32,189]{1,0:T(8,128)}, u32[]{:S(2)}) %copy-start.4) | copy-done | bytes 24216
  28.9 0.8 %copy-done.5 = s32[32,189]{1,0:T(8,128)S(1)} copy-done((s32[32,189]{1,0:T(8,128)S(1)}, s32[32,189]{1,0:T(8,128)}, u32[]{:S(2)}) %copy-start.5) | copy-done | bytes 24216
  29.7 3.8 %first.1 = (bf16[384,2048]{1,0:T(8,128)(2,1)S(1)}, bf16[256,32,128]{2,1,0:T(8,128)(2,1)S(1)}) custom-call(s32[2]{0:T(128)S(1)} %pad_add_fusion.refs_0_.place_ref, s32[32,189]{1,0:T(8,128)S(1)} %copy-done.4, s32[32,189]{1,0:T(8,128)S(1)} %copy-done.5, bf16[316,2,256]{2,1,0:T(2,128)(2,1)S(1)} %copy-done), custom_call_target="tpu_custom_call" | custom-call | flops 1073741824 | bytes 1048576 | tf_op jit(solution)/shard_map/first/pallas_call | solution.py:209
  33.5 2.7 %transfer.1.refs_1_ = bf16[256,32,128]{2,1,0:T(8,128)(2,1)S(1)} custom-call(s32[2]{0:T(128)S(1)} %pad_add_fusion.refs_0_.place_ref, bf16[384,2048]{1,0:T(8,128)(2,1)S(1)} %get-tuple-element.21.counts_ref, bf16[158,2,256]{2,1,0:T(2,128)(2,1)S(1)} %collective-permute-done.7.mine_ref, bf16[158,2,256]{2,1,0:T(2,128)(2,1)S(1)} %collective-permute-done.8.other_ref), custom_call_target="tpu_custom_call" | custom-call | flops 1073741824 | bytes 1048576 | tf_op jit(solution)/shard_map/transfer/pallas_call | solution.py:244
  36.2 2.3 %collective-permute-start.9 = (bf16[528,256]{1,0:T(8,128)(2,1)S(1)}, bf16[528,256]{1,0:T(8,128)(2,1)S(1)}, u32[]{:S(2)}, u32[]{:S(2)}) collective-permute-start(bf16[528,256]{1,0:T(8,128)(2,1)S(1)} %collective-permute-done.5.refs_2_), channel_id=1, source_target_pairs={{0,4},{1,5},{4,8},{5,9},{6,2},{7,3},{8,12},{9,13},{10,6},{11,7},{1... | collective-permute-start | bytes 811016 | tf_op jit(solution)/shard_map/ppermute | solution.py:533
  38.5 3.5 %collective-permute-start.10 = (bf16[528,256]{1,0:T(8,128)(2,1)S(1)}, bf16[528,256]{1,0:T(8,128)(2,1)S(1)}, u32[]{:S(2)}, u32[]{:S(2)}) collective-permute-start(bf16[528,256]{1,0:T(8,128)(2,1)S(1)} %collective-permute-done.6.refs_3_), channel_id=1, source_target_pairs={{0,4},{1,5},{4,8},{5,9},{6,2},{7,3},{8,12},{9,13},{10,6},{11,7},{1... | collective-permute-start | bytes 811016 | tf_op jit(solution)/shard_map/ppermute | solution.py:533
  42.0 2.7 %early.1 = (bf16[512,32,128]{2,1,0:T(8,128)(2,1)S(1)}, bf16[512,256]{1,0:T(8,128)(2,1)S(1)}) custom-call(s32[2]{0:T(128)S(1)} %pad_add_fusion.refs_0_.place_ref, bf16[1024,2,128]{2,1,0:T(2,128)(2,1)S(1)} %copy-done.1, bf16[1024,2,128]{2,1,0:T(2,128)(2,1)S(1)} %copy-done.1, bf16[528,256]{1,0:T(8,128)(2,1)S(1)} %collective-permute-done.refs_3_, ...), custom_call_target="tpu_custom_call" | custom-call | flops 4294967296 | bytes 4194304 | tf_op jit(solution)/shard_map/early/pallas_call | solution.py:304
  44.7 3.9 %pattern.1 = (bf16[512,32,128]{2,1,0:T(8,128)(2,1)S(1)}, bf16[512,256]{1,0:T(8,128)(2,1)S(1)}) custom-call(s32[2]{0:T(128)S(1)} %pad_add_fusion.refs_0_.place_ref, bf16[512,256]{1,0:T(8,128)(2,1)S(1)} %get-tuple-element.16.turned_ref.forward_ref, bf16[1024,2,128]{2,1,0:T(2,128)(2,1)S(1)} %copy-done.2, bf16[528,256]{1,0:T(8,128)(2,1)S(1)} %copy-done.3, ...), custom_call_target="tpu_custom_call" | custom-call | flops 4294967296 | bytes 4194304 | tf_op jit(solution)/shard_map/pattern/pallas_call | solution.py:384
  48.7 4.3 %field.1 = (bf16[8,64,256]{2,1,0:T(8,128)(2,1)S(1)}, f32[8704,128]{1,0:T(8,128)S(1)}) custom-call(bf16[512,256]{1,0:T(8,128)(2,1)S(1)} %get-tuple-element.16.turned_ref.forward_ref, bf16[512,256]{1,0:T(8,128)(2,1)S(1)} %get-tuple-element.17.folded_ref, bf16[512,32,128]{2,1,0:T(8,128)(2,1)S(1)} %get-tuple-element.18.own_ref, ...), custom_call_target="tpu_custom_call" | custom-call | flops 4294967296 | bytes 16777216 | tf_op jit(solution)/shard_map/field/pallas_call | solution.py:456
  53.0 1.3 %collective-permute-start.11 = (bf16[8,64,256]{2,1,0:T(8,128)(2,1)S(1)}, bf16[8,64,256]{2,1,0:T(8,128)(2,1)S(1)}, u32[]{:S(2)}, u32[]{:S(2)}) collective-permute-start(bf16[8,64,256]{2,1,0:T(8,128)(2,1)S(1)} %get-tuple-element.24), channel_id=1, source_target_pairs={{0,1},{1,0},{2,3},{3,2},{4,5},{5,4},{6,7},{7,6},{8,9},{9,8},{10,11... | collective-permute-start | bytes 786440 | tf_op jit(solution)/shard_map/ppermute | solution.py:515
  54.4 3.6 %finish.1 = f32[8,64,256]{2,1,0:T(8,128)S(1)} custom-call(bf16[512,256]{1,0:T(8,128)(2,1)S(1)} %get-tuple-element.17.folded_ref, bf16[512,32,128]{2,1,0:T(8,128)(2,1)S(1)} %get-tuple-element.18.own_ref, bf16[512,32,128]{2,1,0:T(8,128)(2,1)S(1)} %get-tuple-element.19.early_ref, f32[8704,128]{1,0:T(8,128)S(1)} %get-tuple-element.23.near_ref, ...), custom_call_target="tpu_custom_call" | custom-call | flops 2147483648 | bytes 8388608 | tf_op jit(solution)/shard_map/finish/pallas_call | solution.py:478
  58.0 3.5 %collective-permute-done.11 = bf16[8,64,256]{2,1,0:T(8,128)(2,1)S(1)} collective-permute-done((bf16[8,64,256]{2,1,0:T(8,128)(2,1)S(1)}, bf16[8,64,256]{2,1,0:T(8,128)(2,1)S(1)}, u32[]{:S(2)}, u32[]{:S(2)}) %collective-permute-start.11) | collective-permute-done | bytes 262176 | tf_op jit(solution)/shard_map/ppermute | solution.py:515
  61.5 0.9 %add_select_fusion = f32[8,64,256]{2,1,0:T(8,128)} fusion(f32[8,64,256]{2,1,0:T(8,128)S(1)} %finish.1, bf16[8,64,256]{2,1,0:T(8,128)(2,1)S(1)} %collective-permute-done.11, pred[8,256]{1,0:T(8,128)(4,1)S(1)} %broadcast_compare_fusion), kind=kLoop, calls=%fused_computation | loop fusion | flops 393216 | bytes 1312768 | tf_op jit(solution)/shard_map/jit(_where)/select_n | solution.py:493
  (25 shorter events, 0.5 us)
Async XLA Ops:
  0.0 42.0 %copy-start.1 = (bf16[1024,2,128]{2,1,0:T(2,128)(2,1)S(1)}, bf16[1024,2,128]{2,1,0:T(2,128)(2,1)}, u32[]{:S(2)}) copy-start(bf16[1024,2,128]{2,1,0:T(2,128)(2,1)} %refs_2_.1) | copy-start | bytes 1572868
  2.7 12.9 %collective-permute-start.7 = (bf16[158,2,256]{2,1,0:T(2,128)(2,1)}, bf16[158,2,256]{2,1,0:T(2,128)(2,1)S(1)}, u32[]{:S(2)}, u32[]{:S(2)}) collective-permute-start(bf16[158,2,256]{2,1,0:T(2,128)(2,1)} %get-tuple-element.22), channel_id=1, source_target_pairs={{0,2},{1,3},{2,0},{3,1},{4,6},{5,7},{6,4},{7,5},{8,10},{9,11},{10,... | collective-permute-start | bytes 485384 | tf_op jit(solution)/shard_map/ppermute | solution.py:515
  6.9 13.9 %collective-permute-start.2 = (bf16[528,256]{1,0:T(8,128)(2,1)}, bf16[528,256]{1,0:T(8,128)(2,1)S(1)}, u32[]{:S(2)}, u32[]{:S(2)}) collective-permute-start(bf16[528,256]{1,0:T(8,128)(2,1)} %get-tuple-element.15.refs_0_), channel_id=1, source_target_pairs={{0,1},{1,0},{2,3},{3,2},{4,5},{5,4},{6,7},{7,6},{8,9},{9,8},{10,11... | collective-permute-start | bytes 811016 | tf_op jit(solution)/shard_map/ppermute | solution.py:515
  8.4 17.9 %collective-permute-start.5 = (bf16[528,256]{1,0:T(8,128)(2,1)}, bf16[528,256]{1,0:T(8,128)(2,1)S(1)}, u32[]{:S(2)}, u32[]{:S(2)}) collective-permute-start(bf16[528,256]{1,0:T(8,128)(2,1)} %get-tuple-element.15.refs_0_), channel_id=1, source_target_pairs={{0,2},{1,3},{2,0},{3,1},{4,6},{5,7},{6,4},{7,5},{8,10},{9,11},{10,... | collective-permute-start | bytes 811016 | tf_op jit(solution)/shard_map/ppermute | solution.py:515
  15.6 10.7 %collective-permute-start.8 = (bf16[158,2,256]{2,1,0:T(2,128)(2,1)S(1)}, bf16[158,2,256]{2,1,0:T(2,128)(2,1)S(1)}, u32[]{:S(2)}, u32[]{:S(2)}) collective-permute-start(bf16[158,2,256]{2,1,0:T(2,128)(2,1)S(1)} %collective-permute-done.7.mine_ref), channel_id=1, source_target_pairs={{0,4},{1,5},{2,6},{3,7},{4,0},{5,1},{6,2},{7,3},{8,12},{9,13},{10,... | collective-permute-start | bytes 485384 | tf_op jit(solution)/shard_map/ppermute | solution.py:533
  15.7 20.5 %collective-permute-start = (bf16[528,256]{1,0:T(8,128)(2,1)}, bf16[528,256]{1,0:T(8,128)(2,1)S(1)}, u32[]{:S(2)}, u32[]{:S(2)}) collective-permute-start(bf16[528,256]{1,0:T(8,128)(2,1)} %get-tuple-element.15.refs_0_), channel_id=1, source_target_pairs={{4,8},{5,9},{6,10},{7,11},{8,4},{9,5},{10,6},{11,7},{12,16},{13,17... | collective-permute-start | bytes 811016 | tf_op jit(solution)/shard_map/ppermute | solution.py:533
  16.3 25.6 %collective-permute-start.1 = (bf16[528,256]{1,0:T(8,128)(2,1)}, bf16[528,256]{1,0:T(8,128)(2,1)S(1)}, u32[]{:S(2)}, u32[]{:S(2)}) collective-permute-start(bf16[528,256]{1,0:T(8,128)(2,1)} %get-tuple-element.15.refs_0_), channel_id=1, source_target_pairs={{0,4},{1,5},{2,6},{3,7},{4,0},{5,1},{6,2},{7,3},{8,12},{9,13},{10,... | collective-permute-start | bytes 811016 | tf_op jit(solution)/shard_map/ppermute | solution.py:533
  20.8 21.1 %collective-permute-start.3 = (bf16[528,256]{1,0:T(8,128)(2,1)S(1)}, bf16[528,256]{1,0:T(8,128)(2,1)S(1)}, u32[]{:S(2)}, u32[]{:S(2)}) collective-permute-start(bf16[528,256]{1,0:T(8,128)(2,1)S(1)} %collective-permute-done.2.refs_1_), channel_id=1, source_target_pairs={{4,8},{5,9},{6,10},{7,11},{8,4},{9,5},{10,6},{11,7},{12,16},{13,17... | collective-permute-start | bytes 811016 | tf_op jit(solution)/shard_map/ppermute | solution.py:533
  26.3 15.6 %collective-permute-start.4 = (bf16[528,256]{1,0:T(8,128)(2,1)S(1)}, bf16[528,256]{1,0:T(8,128)(2,1)S(1)}, u32[]{:S(2)}, u32[]{:S(2)}) collective-permute-start(bf16[528,256]{1,0:T(8,128)(2,1)S(1)} %collective-permute-done.2.refs_1_), channel_id=1, source_target_pairs={{0,4},{1,5},{2,6},{3,7},{4,0},{5,1},{6,2},{7,3},{8,12},{9,13},{10,... | collective-permute-start | bytes 811016 | tf_op jit(solution)/shard_map/ppermute | solution.py:533
  26.3 12.1 %collective-permute-start.6 = (bf16[528,256]{1,0:T(8,128)(2,1)S(1)}, bf16[528,256]{1,0:T(8,128)(2,1)S(1)}, u32[]{:S(2)}, u32[]{:S(2)}) collective-permute-start(bf16[528,256]{1,0:T(8,128)(2,1)S(1)} %collective-permute-done.5.refs_2_), channel_id=1, source_target_pairs={{0,1},{1,0},{2,3},{3,2},{4,5},{5,4},{6,7},{7,6},{8,9},{9,8},{10,11... | collective-permute-start | bytes 811016 | tf_op jit(solution)/shard_map/ppermute | solution.py:515
  27.2 1.0 %copy-start = (bf16[316,2,256]{2,1,0:T(2,128)(2,1)S(1)}, bf16[316,2,256]{2,1,0:T(2,128)(2,1)}, u32[]{:S(2)}) copy-start(bf16[316,2,256]{2,1,0:T(2,128)(2,1)} %table_hbm.1) | copy-start | bytes 970756
  28.2 0.8 %copy-start.4 = (s32[32,189]{1,0:T(8,128)S(1)}, s32[32,189]{1,0:T(8,128)}, u32[]{:S(2)}) copy-start(s32[32,189]{1,0:T(8,128)} %source_hbm.1) | copy-start | bytes 72580
  28.9 0.8 %copy-start.5 = (s32[32,189]{1,0:T(8,128)S(1)}, s32[32,189]{1,0:T(8,128)}, u32[]{:S(2)}) copy-start(s32[32,189]{1,0:T(8,128)} %kind_hbm.1) | copy-start | bytes 72580
  36.1 8.6 %copy-start.2 = (bf16[1024,2,128]{2,1,0:T(2,128)(2,1)S(1)}, bf16[1024,2,128]{2,1,0:T(2,128)(2,1)}, u32[]{:S(2)}) copy-start(bf16[1024,2,128]{2,1,0:T(2,128)(2,1)} %receive_ref.1) | copy-start | bytes 1572868
  36.1 8.6 %copy-start.3 = (bf16[528,256]{1,0:T(8,128)(2,1)S(1)}, bf16[528,256]{1,0:T(8,128)(2,1)}, u32[]{:S(2)}) copy-start(bf16[528,256]{1,0:T(8,128)(2,1)} %get-tuple-element.15.refs_0_) | copy-start | bytes 811012
  36.2 12.5 %collective-permute-start.9 = (bf16[528,256]{1,0:T(8,128)(2,1)S(1)}, bf16[528,256]{1,0:T(8,128)(2,1)S(1)}, u32[]{:S(2)}, u32[]{:S(2)}) collective-permute-start(bf16[528,256]{1,0:T(8,128)(2,1)S(1)} %collective-permute-done.5.refs_2_), channel_id=1, source_target_pairs={{0,4},{1,5},{4,8},{5,9},{6,2},{7,3},{8,12},{9,13},{10,6},{11,7},{1... | collective-permute-start | bytes 811016 | tf_op jit(solution)/shard_map/ppermute | solution.py:533
  38.5 10.2 %collective-permute-start.10 = (bf16[528,256]{1,0:T(8,128)(2,1)S(1)}, bf16[528,256]{1,0:T(8,128)(2,1)S(1)}, u32[]{:S(2)}, u32[]{:S(2)}) collective-permute-start(bf16[528,256]{1,0:T(8,128)(2,1)S(1)} %collective-permute-done.6.refs_3_), channel_id=1, source_target_pairs={{0,4},{1,5},{4,8},{5,9},{6,2},{7,3},{8,12},{9,13},{10,6},{11,7},{1... | collective-permute-start | bytes 811016 | tf_op jit(solution)/shard_map/ppermute | solution.py:533
  48.7 5.6 %copy-start.6 = (s32[8]{0:T(128)S(1)}, s32[8]{0:T(128)}, u32[]{:S(2)}) copy-start(s32[8]{0:T(128)} %live_ref.1) | copy-start | bytes 100
  53.0 8.5 %collective-permute-start.11 = (bf16[8,64,256]{2,1,0:T(8,128)(2,1)S(1)}, bf16[8,64,256]{2,1,0:T(8,128)(2,1)S(1)}, u32[]{:S(2)}, u32[]{:S(2)}) collective-permute-start(bf16[8,64,256]{2,1,0:T(8,128)(2,1)S(1)} %get-tuple-element.24), channel_id=1, source_target_pairs={{0,1},{1,0},{2,3},{3,2},{4,5},{5,4},{6,7},{7,6},{8,9},{9,8},{10,11... | collective-permute-start | bytes 786440 | tf_op jit(solution)/shard_map/ppermute | solution.py:515

commit v8 on v7

--- a/solution.py
+++ b/solution.py
@@ -25,6 +25,10 @@
     return -(-value // unit) * unit
 
 
+def padded_rows(rows, boxes):
+    return rows * (boxes + 1) + round_up(boxes + 1, 8)
+
+
 def half_of(kinds):
     return (kinds + 1) // 2
 
@@ -68,13 +72,9 @@
     lax.fori_loop(0, trips // size, block, 0)
 
 
-def prepare_kernel(all_dirs, live_ref, stencil_ref, weight_ref, box_ref, table_ref, out_ref, half_ref, sem):
+def prepare_kernel(all_dirs, live_ref, stencil_ref, weight_ref, box_ref, out_ref):
     boxes, incid, width = box_ref.shape
     points, dirs = stencil_ref.shape
-    half = half_ref.shape[0]
-    first = lax.rem(lax.axis_index("grp"), 2) * (table_ref.shape[0] - half)
-    fetch = pltpu.make_async_copy(table_ref.at[pl.ds(first, half)], half_ref, sem)
-    fetch.start()
     unk = count_of((incid, width), 1)
     unk = jnp.where(unk < width // 2, unk, unk - width // 2)
     for b in range(boxes):
@@ -87,25 +87,19 @@
     if dirs < width:
         rows = jnp.concatenate([rows, jnp.zeros((2 * points, width - dirs), F32)], axis=1)
     out_ref[boxes * incid :, :] = rows.astype(BF)
-    fetch.wait()
-
-
-def prepare(live_counts, stencil, weights, currents, translators, all_dirs):
+
+
+def prepare(live_counts, stencil, weights, currents, all_dirs):
     boxes, incid, width = currents.shape
-    points, dirs = stencil.shape
-    kinds, parts, _ = translators.shape
+    points, _ = stencil.shape
     return pl.pallas_call(
         functools.partial(prepare_kernel, all_dirs),
-        out_shape=(
-            jax.ShapeDtypeStruct((boxes * incid + 2 * points, width), BF),
-            jax.ShapeDtypeStruct((half_of(kinds), parts, dirs), BF),
-        ),
-        in_specs=[SMEM, VMEM, VMEM, VMEM, pl.BlockSpec(memory_space=pl.ANY)],
-        out_specs=(VMEM, VMEM),
-        scratch_shapes=[pltpu.SemaphoreType.DMA],
+        out_shape=jax.ShapeDtypeStruct((boxes * incid + 2 * points, width), BF),
+        in_specs=[SMEM, VMEM, VMEM, VMEM],
+        out_specs=VMEM,
         cost_estimate=cost(1 << 20, 1 << 20),
         name="prepare",
-    )(live_counts, stencil, weights, currents, translators)
+    )(live_counts, stencil, weights, currents)
 
 
 def count_entries(slots, kinds, window, place_ref, source_ref, kind_ref, counts_ref, lists):
@@ -170,7 +164,9 @@
     unrolled(dirs, 64, narrow)
 
 
-def first_kernel(slots, place_ref, source_hbm, kind_hbm, table_hbm, counts_ref, matrix_ref, *scratch):
+def first_kernel(
+    slots, place_ref, source_hbm, kind_hbm, table_hbm, counts_ref, matrix_ref, half_ref, *scratch
+):
     source_ref, kind_ref, table_ref, lists, table, wide, sems = scratch
     window = matrix_ref.shape[2]
     kinds = table_ref.shape[0]
@@ -186,6 +182,7 @@
     count_entries(slots, kinds, window, place_ref, source_ref, kind_ref, counts_ref, lists)
     copies[2].wait()
     half = half_of(kinds)
+    half_ref[...] = table_ref[pl.ds(lax.rem(place_ref[1], 2) * (kinds - half), half)]
     low, high = table_ref.at[pl.ds(0, half)], table_ref.at[pl.ds(kinds - half, half)]
     fill_matrix(low, high, counts_ref, matrix_ref, table, wide)
 
@@ -197,6 +194,7 @@
     out_shape = (
         jax.ShapeDtypeStruct((table_rows(kinds), boxes * window), BF),
         jax.ShapeDtypeStruct((dirs, 2 * boxes, window), BF),
+        jax.ShapeDtypeStruct((half_of(kinds), 2, dirs), BF),
     )
     scratch = [
         pltpu.VMEM(sources.shape, I32),
@@ -204,13 +202,13 @@
         pltpu.VMEM(translators.shape, BF),
         pltpu.VMEM((2 * boxes, round_up(width, LANES)), I32),
         pltpu.VMEM((2 * dirs, table_rows(kinds)), BF),
-        pltpu.VMEM((window // LANES, dirs * (2 * boxes + 1), LANES), F32),
+        pltpu.VMEM((window // LANES, padded_rows(dirs, 2 * boxes), LANES), F32),
     ]
     return pl.pallas_call(
         functools.partial(first_kernel, slots),
         out_shape=out_shape,
         in_specs=[SMEM] + [pl.BlockSpec(memory_space=pltpu.HBM)] * 3,
-        out_specs=(VMEM, VMEM),
+        out_specs=(VMEM, VMEM, VMEM),
         scratch_shapes=scratch + [pltpu.SemaphoreType.DMA((3,))],
         compiler_params=grant(scratch, out_shape),
         cost_estimate=cost(1 << 30, 1 << 20),
@@ -239,7 +237,7 @@
         pltpu.VMEM(mine.shape, BF),
         pltpu.VMEM(mine.shape, BF),
         pltpu.VMEM((2 * dirs, counts.shape[0]), BF),
-        pltpu.VMEM((window // LANES, dirs * (2 * boxes + 1), LANES), F32),
+        pltpu.VMEM((window // LANES, padded_rows(dirs, 2 * boxes), LANES), F32),
     ]
     return pl.pallas_call(
         transfer_kernel,
@@ -300,7 +298,7 @@
         jax.ShapeDtypeStruct((rows, boxes, 2 * incid), BF),
         jax.ShapeDtypeStruct((rows, parts * unk), BF),
     )
-    scratch = [pltpu.VMEM((rows * (boxes + 1), 2 * incid), F32)]
+    scratch = [pltpu.VMEM((padded_rows(rows, boxes), 2 * incid), F32)]
     return pl.pallas_call(
         functools.partial(early_kernel, len(slots), len(shards), incid),
         out_shape=out_shape,
@@ -378,7 +376,7 @@
         jax.ShapeDtypeStruct((rows, width), BF),
     )
     scratch = [
-        pltpu.VMEM((rows * (boxes + 1), 2 * incid), F32),
+        pltpu.VMEM((padded_rows(rows, boxes), 2 * incid), F32),
         pltpu.VMEM((count, 2 * points, shards[0].shape[1]), F32),
     ]
     return pl.pallas_call(
@@ -450,9 +448,9 @@
     shape = (per, width // 2, folded.shape[1])
     out_shape = (
         jax.ShapeDtypeStruct(shape, kind),
-        jax.ShapeDtypeStruct((rows * (len(near) * per + 1), width), F32),
-    )
-    scratch = [pltpu.VMEM((rows * (per + 1), width), F32)]
+        jax.ShapeDtypeStruct((padded_rows(rows, len(near) * per), width), F32),
+    )
+    scratch = [pltpu.VMEM((padded_rows(rows, per), width), F32)]
     return pl.pallas_call(
         functools.partial(field_kernel, len(matrices)),
         out_shape=out_shape,
@@ -474,7 +472,7 @@
 def finish(folded, own, early, around, matrices, shape):
     out_shape = jax.ShapeDtypeStruct(shape, F32)
     rows, _, width = own.shape
-    scratch = [pltpu.VMEM((rows * (shape[0] + 1), width), F32)]
+    scratch = [pltpu.VMEM((padded_rows(rows, shape[0]), width), F32)]
     return pl.pallas_call(
         functools.partial(finish_kernel, len(matrices)),
         out_shape=out_shape,
@@ -532,8 +530,8 @@
                     pairs.append((g * n_dir + d, to * n_dir + d))
         return lax.ppermute(values, ("grp", "dir"), pairs)
 
-    shard, part = prepare(
-        live_counts, stencil.T, stencil_weights.T, currents, translators, radiation.shape[0]
+    shard = prepare(
+        live_counts, stencil.T, stencil_weights.T, currents, radiation.shape[0]
     )
     shards = gather(shard, 1)
     near = [across(shards[j], lambda d, g, j=j: 1 if d ^ j > d else -1) for j in range(2, n_dir)]
@@ -541,9 +539,7 @@
     for j in range(2):
         next_to.append(across(shards[j], lambda d, g: 1 if g % 2 else -1))
         next_to.append(across(shards[j], lambda d, g: -1 if g % 2 else 1))
-    counts, matrix = first_transfer(
-        place, sources, operator_ids, translators, n_dir, window
-    )
+    counts, matrix, part = first_transfer(place, sources, operator_ids, translators, n_dir, window)
     matrices = [matrix]
     for j, mine in enumerate(gather(part, 2)[1:], 1):
         other = across(mine, lambda d, g: -1 if g % 2 else 1)

time: 62.7 us -> 65.7 us (1.048)
  starting transfers between devices: 18.5 us -> 21.3 us
  local copies, waits for them, and re-layouts: 2.51 us -> 5.07 us
  waiting for transfers between devices: 16.5 us -> 15 us
  Pallas kernels: 23.7 us -> 22.8 us
    ppermute x7, starting transfers between devices: 10.3 us -> 13.2 us  [across(): return lax.ppermute(values, ('grp', 'dir'), pairs)]
    unnamed x14 -> x18, local copies, waits for them, and re-layouts: 2.51 us -> 5.07 us
    ppermute x5, waiting for transfers between devices: 16.4 us -> 15 us  [swap(): return lax.ppermute(values, 'dir', [(i, i ^ bit) for i in range(n_dir)])]
    pallas_call x1, Pallas kernels: 2.72 us -> 1.75 us  [prepare(): pl.pallas_call(functools.partial(prepare_kernel, all_dirs), out_shape=jax...]
  transfers between devices with their start and end apart: 12 -> 12, of which waited for: 4 -> 3; matrix products, arithmetic and copies ran while one was open for 0% -> 0% of each run, Pallas kernels for 27% -> 22%
where the time goes in v8:
time: 65.7 us; the launch traced here: 65.3 us
  Pallas kernels  22.8 us (35%)
  starting transfers between devices  21.3 us (32%)
  waiting for transfers between devices  15 us (23%)
  local copies, waits for them, and re-layouts  5.07 us (8%)
  other arithmetic  1.01 us (2%)
    ppermute x5, waiting for transfers between devices, swap(): return lax.ppermute(values, 'dir', [(i, i ^ bit) for i in range(n_dir)])  15 us
    ppermute x7, starting transfers between devices, across(): return lax.ppermute(values, ('grp', 'dir'), pairs)  13.2 us
    ppermute x5, starting transfers between devices, swap(): return lax.ppermute(values, 'dir', [(i, i ^ bit) for i in range(n_dir)])  8.12 us
    unnamed x18, local copies, waits for them, and re-layouts  5.07 us
    pallas_call x1, Pallas kernels, translate_field(): pl.pallas_call(functools.partial(field_kernel, len(matrices)), out_shape=...  4.33 us
    pallas_call x1, Pallas kernels, own_pattern(): pl.pallas_call(functools.partial(pattern_kernel, slots, count, incid, RIM...  3.93 us
    pallas_call x1, Pallas kernels, first_transfer(): pl.pallas_call(functools.partial(first_kernel, slots), out_shape=out_shap...  3.8 us
    pallas_call x1, Pallas kernels, finish(): pl.pallas_call(functools.partial(finish_kernel, len(matrices)), out_shape...  3.58 us
  transfers between devices with their start and end apart: 12, of which 3 were waited for; matrix products, arithmetic and copies ran while one was open for 0% of the time, Pallas kernels for 22%

profile of v8, /device:TPU:0, one launch (start us, length us, event | category | flops | bytes accessed | tf_op | source)
XLA Modules:
  0.0 65.3 jit_solution(12317437258857656875)
XLA Ops:
  0.1 1.0 %copy-done.5 = bf16[316,2,256]{2,1,0:T(2,128)(2,1)S(1)} copy-done((bf16[316,2,256]{2,1,0:T(2,128)(2,1)S(1)}, bf16[316,2,256]{2,1,0:T(2,128)(2,1)}, u32[]{:S(2)}) %copy-start.5) | copy-done | bytes 323608
  1.1 0.8 %copy-done.6 = s32[32,189]{1,0:T(8,128)S(1)} copy-done((s32[32,189]{1,0:T(8,128)S(1)}, s32[32,189]{1,0:T(8,128)}, u32[]{:S(2)}) %copy-start.6) | copy-done | bytes 24216
  1.8 0.8 %copy-done.7 = s32[32,189]{1,0:T(8,128)S(1)} copy-done((s32[32,189]{1,0:T(8,128)S(1)}, s32[32,189]{1,0:T(8,128)}, u32[]{:S(2)}) %copy-start.7) | copy-done | bytes 24216
  2.6 3.8 %first.1 = (bf16[384,2048]{1,0:T(8,128)(2,1)S(1)}, bf16[256,32,128]{2,1,0:T(8,128)(2,1)S(1)}, bf16[158,2,256]{2,1,0:T(2,128)(2,1)S(1)}) custom-call(s32[2]{0:T(128)S(1)} %pad_add_fusion.refs_0_.place_ref, s32[32,189]{1,0:T(8,128)S(1)} %copy-done.6, s32[32,189]{1,0:T(8,128)S(1)} %copy-done.7, bf16[316,2,256]{2,1,0:T(2,128)(2,1)S(1)} %copy-done.5), custom_call_target="tpu_custom_call" | custom-call | flops 1073741824 | bytes 1048576 | tf_op jit(solution)/shard_map/first/pallas_call | solution.py:207
  6.4 1.1 %copy-done = bf16[384,2048]{1,0:T(8,128)(2,1)} copy-done((bf16[384,2048]{1,0:T(8,128)(2,1)}, bf16[384,2048]{1,0:T(8,128)(2,1)S(1)}, u32[]{:S(2)}) %copy-start) | copy-done | bytes 1572888
  7.5 4.1 %collective-permute-start.7 = (bf16[158,2,256]{2,1,0:T(2,128)(2,1)S(1)}, bf16[158,2,256]{2,1,0:T(2,128)(2,1)S(1)}, u32[]{:S(2)}, u32[]{:S(2)}) collective-permute-start(bf16[158,2,256]{2,1,0:T(2,128)(2,1)S(1)} %get-tuple-element.20), channel_id=1, source_target_pairs={{0,2},{1,3},{2,0},{3,1},{4,6},{5,7},{6,4},{7,5},{8,10},{9,11},{10,... | collective-permute-start | bytes 485384 | tf_op jit(solution)/shard_map/ppermute | solution.py:513
  11.6 1.7 %prepare.1.refs_0_ = bf16[528,256]{1,0:T(8,128)(2,1)} custom-call(s32[8]{0:T(128)} %live_ref.1, s32[8,256]{1,0:T(8,128)} %bitcast.4, bf16[8,256]{1,0:T(8,128)(2,1)} %bitcast.5, bf16[8,64,256]{2,1,0:T(8,128)(2,1)} %box_ref.1), custom_call_target="tpu_custom_call" | custom-call | flops 1048576 | bytes 1048576 | tf_op jit(solution)/shard_map/prepare/pallas_call | solution.py:95
  13.4 1.9 %collective-permute-start.2 = (bf16[528,256]{1,0:T(8,128)(2,1)}, bf16[528,256]{1,0:T(8,128)(2,1)S(1)}, u32[]{:S(2)}, u32[]{:S(2)}) collective-permute-start(bf16[528,256]{1,0:T(8,128)(2,1)} %prepare.1.refs_0_), channel_id=1, source_target_pairs={{0,1},{1,0},{2,3},{3,2},{4,5},{5,4},{6,7},{7,6},{8,9},{9,8},{10,11... | collective-permute-start | bytes 811016 | tf_op jit(solution)/shard_map/ppermute | solution.py:513
  15.3 10.6 %collective-permute-done.7.mine_ref = bf16[158,2,256]{2,1,0:T(2,128)(2,1)S(1)} collective-permute-done((bf16[158,2,256]{2,1,0:T(2,128)(2,1)S(1)}, bf16[158,2,256]{2,1,0:T(2,128)(2,1)S(1)}, u32[]{:S(2)}, u32[]{:S(2)}) %collective-permute-start.7) | collective-permute-done | bytes 161824 | tf_op jit(solution)/shard_map/ppermute | solution.py:513
  26.5 3.2 %collective-permute-start.1 = (bf16[528,256]{1,0:T(8,128)(2,1)}, bf16[528,256]{1,0:T(8,128)(2,1)S(1)}, u32[]{:S(2)}, u32[]{:S(2)}) collective-permute-start(bf16[528,256]{1,0:T(8,128)(2,1)} %prepare.1.refs_0_), channel_id=1, source_target_pairs={{0,4},{1,5},{2,6},{3,7},{4,0},{5,1},{6,2},{7,3},{8,12},{9,13},{10,... | collective-permute-start | bytes 811016 | tf_op jit(solution)/shard_map/ppermute | solution.py:531
  29.7 1.1 %collective-permute-done.5.refs_2_ = bf16[528,256]{1,0:T(8,128)(2,1)S(1)} collective-permute-done((bf16[528,256]{1,0:T(8,128)(2,1)}, bf16[528,256]{1,0:T(8,128)(2,1)S(1)}, u32[]{:S(2)}, u32[]{:S(2)}) %collective-permute-start.5) | collective-permute-done | bytes 270368 | tf_op jit(solution)/shard_map/ppermute | solution.py:513
  30.8 0.8 %collective-permute-start.6 = (bf16[528,256]{1,0:T(8,128)(2,1)S(1)}, bf16[528,256]{1,0:T(8,128)(2,1)S(1)}, u32[]{:S(2)}, u32[]{:S(2)}) collective-permute-start(bf16[528,256]{1,0:T(8,128)(2,1)S(1)} %collective-permute-done.5.refs_2_), channel_id=1, source_target_pairs={{0,1},{1,0},{2,3},{3,2},{4,5},{5,4},{6,7},{7,6},{8,9},{9,8},{10,11... | collective-permute-start | bytes 811016 | tf_op jit(solution)/shard_map/ppermute | solution.py:513
  32.3 2.9 %collective-permute-start.4 = (bf16[528,256]{1,0:T(8,128)(2,1)S(1)}, bf16[528,256]{1,0:T(8,128)(2,1)S(1)}, u32[]{:S(2)}, u32[]{:S(2)}) collective-permute-start(bf16[528,256]{1,0:T(8,128)(2,1)S(1)} %collective-permute-done.2.refs_1_), channel_id=1, source_target_pairs={{0,4},{1,5},{2,6},{3,7},{4,0},{5,1},{6,2},{7,3},{8,12},{9,13},{10,... | collective-permute-start | bytes 811016 | tf_op jit(solution)/shard_map/ppermute | solution.py:531
  35.2 1.4 %copy-done.1 = bf16[384,2048]{1,0:T(8,128)(2,1)S(1)} copy-done((bf16[384,2048]{1,0:T(8,128)(2,1)S(1)}, bf16[384,2048]{1,0:T(8,128)(2,1)}, u32[]{:S(2)}) %copy-start.1) | copy-done | bytes 1572888
  36.6 2.7 %transfer.1.refs_1_ = bf16[256,32,128]{2,1,0:T(8,128)(2,1)S(1)} custom-call(s32[2]{0:T(128)S(1)} %pad_add_fusion.refs_0_.place_ref, bf16[384,2048]{1,0:T(8,128)(2,1)S(1)} %copy-done.1, bf16[158,2,256]{2,1,0:T(2,128)(2,1)S(1)} %collective-permute-done.7.mine_ref, bf16[158,2,256]{2,1,0:T(2,128)(2,1)S(1)} %collective-permute-done.8.other_ref), custom_call_target="tpu_custom_call" | custom-call | flops 1073741824 | bytes 1048576 | tf_op jit(solution)/shard_map/transfer/pallas_call | solution.py:242
  39.3 2.1 %collective-permute-start.9 = (bf16[528,256]{1,0:T(8,128)(2,1)S(1)}, bf16[528,256]{1,0:T(8,128)(2,1)S(1)}, u32[]{:S(2)}, u32[]{:S(2)}) collective-permute-start(bf16[528,256]{1,0:T(8,128)(2,1)S(1)} %collective-permute-done.5.refs_2_), channel_id=1, source_target_pairs={{0,4},{1,5},{4,8},{5,9},{6,2},{7,3},{8,12},{9,13},{10,6},{11,7},{1... | collective-permute-start | bytes 811016 | tf_op jit(solution)/shard_map/ppermute | solution.py:531
  41.4 3.7 %collective-permute-start.10 = (bf16[528,256]{1,0:T(8,128)(2,1)S(1)}, bf16[528,256]{1,0:T(8,128)(2,1)S(1)}, u32[]{:S(2)}, u32[]{:S(2)}) collective-permute-start(bf16[528,256]{1,0:T(8,128)(2,1)S(1)} %collective-permute-done.6.refs_3_), channel_id=1, source_target_pairs={{0,4},{1,5},{4,8},{5,9},{6,2},{7,3},{8,12},{9,13},{10,6},{11,7},{1... | collective-permute-start | bytes 811016 | tf_op jit(solution)/shard_map/ppermute | solution.py:531
  45.2 2.7 %early.1 = (bf16[512,32,128]{2,1,0:T(8,128)(2,1)S(1)}, bf16[512,256]{1,0:T(8,128)(2,1)S(1)}) custom-call(s32[2]{0:T(128)S(1)} %pad_add_fusion.refs_0_.place_ref, bf16[1024,2,128]{2,1,0:T(2,128)(2,1)S(1)} %copy-done.3, bf16[1024,2,128]{2,1,0:T(2,128)(2,1)S(1)} %copy-done.3, bf16[528,256]{1,0:T(8,128)(2,1)S(1)} %collective-permute-done.refs_3_, ...), custom_call_target="tpu_custom_call" | custom-call | flops 4294967296 | bytes 4194304 | tf_op jit(solution)/shard_map/early/pallas_call | solution.py:302
  47.9 3.9 %pattern.1 = (bf16[512,32,128]{2,1,0:T(8,128)(2,1)S(1)}, bf16[512,256]{1,0:T(8,128)(2,1)S(1)}) custom-call(s32[2]{0:T(128)S(1)} %pad_add_fusion.refs_0_.place_ref, bf16[512,256]{1,0:T(8,128)(2,1)S(1)} %get-tuple-element.14.turned_ref.forward_ref, bf16[1024,2,128]{2,1,0:T(2,128)(2,1)S(1)} %copy-done.4, bf16[528,256]{1,0:T(8,128)(2,1)S(1)} %copy-done.2, ...), custom_call_target="tpu_custom_call" | custom-call | flops 4294967296 | bytes 4194304 | tf_op jit(solution)/shard_map/pattern/pallas_call | solution.py:382
  51.9 4.3 %field.1 = (bf16[8,64,256]{2,1,0:T(8,128)(2,1)S(1)}, f32[8728,128]{1,0:T(8,128)S(1)}) custom-call(bf16[512,256]{1,0:T(8,128)(2,1)S(1)} %get-tuple-element.14.turned_ref.forward_ref, bf16[512,256]{1,0:T(8,128)(2,1)S(1)} %get-tuple-element.15.folded_ref, bf16[512,32,128]{2,1,0:T(8,128)(2,1)S(1)} %get-tuple-element.16.own_ref, ...), custom_call_target="tpu_custom_call" | custom-call | flops 4294967296 | bytes 16777216 | tf_op jit(solution)/shard_map/field/pallas_call | solution.py:454
  56.2 1.3 %collective-permute-start.11 = (bf16[8,64,256]{2,1,0:T(8,128)(2,1)S(1)}, bf16[8,64,256]{2,1,0:T(8,128)(2,1)S(1)}, u32[]{:S(2)}, u32[]{:S(2)}) collective-permute-start(bf16[8,64,256]{2,1,0:T(8,128)(2,1)S(1)} %get-tuple-element.22), channel_id=1, source_target_pairs={{0,1},{1,0},{2,3},{3,2},{4,5},{5,4},{6,7},{7,6},{8,9},{9,8},{10,11... | collective-permute-start | bytes 786440 | tf_op jit(solution)/shard_map/ppermute | solution.py:513
  57.6 3.6 %finish.1 = f32[8,64,256]{2,1,0:T(8,128)S(1)} custom-call(bf16[512,256]{1,0:T(8,128)(2,1)S(1)} %get-tuple-element.15.folded_ref, bf16[512,32,128]{2,1,0:T(8,128)(2,1)S(1)} %get-tuple-element.16.own_ref, bf16[512,32,128]{2,1,0:T(8,128)(2,1)S(1)} %get-tuple-element.17.early_ref, f32[8728,128]{1,0:T(8,128)S(1)} %get-tuple-element.21.near_ref, ...), custom_call_target="tpu_custom_call" | custom-call | flops 2147483648 | bytes 8388608 | tf_op jit(solution)/shard_map/finish/pallas_call | solution.py:476
  61.2 3.3 %collective-permute-done.11 = bf16[8,64,256]{2,1,0:T(8,128)(2,1)S(1)} collective-permute-done((bf16[8,64,256]{2,1,0:T(8,128)(2,1)S(1)}, bf16[8,64,256]{2,1,0:T(8,128)(2,1)S(1)}, u32[]{:S(2)}, u32[]{:S(2)}) %collective-permute-start.11) | collective-permute-done | bytes 262176 | tf_op jit(solution)/shard_map/ppermute | solution.py:513
  64.5 0.9 %add_select_fusion = f32[8,64,256]{2,1,0:T(8,128)} fusion(f32[8,64,256]{2,1,0:T(8,128)S(1)} %finish.1, bf16[8,64,256]{2,1,0:T(8,128)(2,1)S(1)} %collective-permute-done.11, pred[8,256]{1,0:T(8,128)(4,1)S(1)} %broadcast_compare_fusion), kind=kLoop, calls=%fused_computation | loop fusion | flops 393216 | bytes 1312768 | tf_op jit(solution)/shard_map/jit(_where)/select_n | solution.py:491
  (29 shorter events, 1.6 us)
Async XLA Ops:
  0.1 1.0 %copy-start.5 = (bf16[316,2,256]{2,1,0:T(2,128)(2,1)S(1)}, bf16[316,2,256]{2,1,0:T(2,128)(2,1)}, u32[]{:S(2)}) copy-start(bf16[316,2,256]{2,1,0:T(2,128)(2,1)} %table_hbm.1) | copy-start | bytes 970756
  1.0 0.8 %copy-start.6 = (s32[32,189]{1,0:T(8,128)S(1)}, s32[32,189]{1,0:T(8,128)}, u32[]{:S(2)}) copy-start(s32[32,189]{1,0:T(8,128)} %source_hbm.1) | copy-start | bytes 72580
  1.8 0.8 %copy-start.7 = (s32[32,189]{1,0:T(8,128)S(1)}, s32[32,189]{1,0:T(8,128)}, u32[]{:S(2)}) copy-start(s32[32,189]{1,0:T(8,128)} %kind_hbm.1) | copy-start | bytes 72580
  2.6 42.6 %copy-start.3 = (bf16[1024,2,128]{2,1,0:T(2,128)(2,1)S(1)}, bf16[1024,2,128]{2,1,0:T(2,128)(2,1)}, u32[]{:S(2)}) copy-start(bf16[1024,2,128]{2,1,0:T(2,128)(2,1)} %refs_2_.1) | copy-start | bytes 1572868
  6.4 1.2 %copy-start = (bf16[384,2048]{1,0:T(8,128)(2,1)}, bf16[384,2048]{1,0:T(8,128)(2,1)S(1)}, u32[]{:S(2)}) copy-start(bf16[384,2048]{1,0:T(8,128)(2,1)S(1)} %get-tuple-element.19.counts_ref) | copy-start | bytes 4718596
  7.5 18.3 %collective-permute-start.7 = (bf16[158,2,256]{2,1,0:T(2,128)(2,1)S(1)}, bf16[158,2,256]{2,1,0:T(2,128)(2,1)S(1)}, u32[]{:S(2)}, u32[]{:S(2)}) collective-permute-start(bf16[158,2,256]{2,1,0:T(2,128)(2,1)S(1)} %get-tuple-element.20), channel_id=1, source_target_pairs={{0,2},{1,3},{2,0},{3,1},{4,6},{5,7},{6,4},{7,5},{8,10},{9,11},{10,... | collective-permute-start | bytes 485384 | tf_op jit(solution)/shard_map/ppermute | solution.py:513
  13.3 17.5 %collective-permute-start.5 = (bf16[528,256]{1,0:T(8,128)(2,1)}, bf16[528,256]{1,0:T(8,128)(2,1)S(1)}, u32[]{:S(2)}, u32[]{:S(2)}) collective-permute-start(bf16[528,256]{1,0:T(8,128)(2,1)} %prepare.1.refs_0_), channel_id=1, source_target_pairs={{0,2},{1,3},{2,0},{3,1},{4,6},{5,7},{6,4},{7,5},{8,10},{9,11},{10,... | collective-permute-start | bytes 811016 | tf_op jit(solution)/shard_map/ppermute | solution.py:513
  13.4 18.3 %collective-permute-start.2 = (bf16[528,256]{1,0:T(8,128)(2,1)}, bf16[528,256]{1,0:T(8,128)(2,1)S(1)}, u32[]{:S(2)}, u32[]{:S(2)}) collective-permute-start(bf16[528,256]{1,0:T(8,128)(2,1)} %prepare.1.refs_0_), channel_id=1, source_target_pairs={{0,1},{1,0},{2,3},{3,2},{4,5},{5,4},{6,7},{7,6},{8,9},{9,8},{10,11... | collective-permute-start | bytes 811016 | tf_op jit(solution)/shard_map/ppermute | solution.py:513
  25.9 6.4 %collective-permute-start.8 = (bf16[158,2,256]{2,1,0:T(2,128)(2,1)S(1)}, bf16[158,2,256]{2,1,0:T(2,128)(2,1)S(1)}, u32[]{:S(2)}, u32[]{:S(2)}) collective-permute-start(bf16[158,2,256]{2,1,0:T(2,128)(2,1)S(1)} %collective-permute-done.7.mine_ref), channel_id=1, source_target_pairs={{0,4},{1,5},{2,6},{3,7},{4,0},{5,1},{6,2},{7,3},{8,12},{9,13},{10,... | collective-permute-start | bytes 485384 | tf_op jit(solution)/shard_map/ppermute | solution.py:531
  25.9 13.5 %collective-permute-start = (bf16[528,256]{1,0:T(8,128)(2,1)}, bf16[528,256]{1,0:T(8,128)(2,1)S(1)}, u32[]{:S(2)}, u32[]{:S(2)}) collective-permute-start(bf16[528,256]{1,0:T(8,128)(2,1)} %prepare.1.refs_0_), channel_id=1, source_target_pairs={{4,8},{5,9},{6,10},{7,11},{8,4},{9,5},{10,6},{11,7},{12,16},{13,17... | collective-permute-start | bytes 811016 | tf_op jit(solution)/shard_map/ppermute | solution.py:531
  26.5 18.6 %collective-permute-start.1 = (bf16[528,256]{1,0:T(8,128)(2,1)}, bf16[528,256]{1,0:T(8,128)(2,1)S(1)}, u32[]{:S(2)}, u32[]{:S(2)}) collective-permute-start(bf16[528,256]{1,0:T(8,128)(2,1)} %prepare.1.refs_0_), channel_id=1, source_target_pairs={{0,4},{1,5},{2,6},{3,7},{4,0},{5,1},{6,2},{7,3},{8,12},{9,13},{10,... | collective-permute-start | bytes 811016 | tf_op jit(solution)/shard_map/ppermute | solution.py:531
  30.8 10.6 %collective-permute-start.6 = (bf16[528,256]{1,0:T(8,128)(2,1)S(1)}, bf16[528,256]{1,0:T(8,128)(2,1)S(1)}, u32[]{:S(2)}, u32[]{:S(2)}) collective-permute-start(bf16[528,256]{1,0:T(8,128)(2,1)S(1)} %collective-permute-done.5.refs_2_), channel_id=1, source_target_pairs={{0,1},{1,0},{2,3},{3,2},{4,5},{5,4},{6,7},{7,6},{8,9},{9,8},{10,11... | collective-permute-start | bytes 811016 | tf_op jit(solution)/shard_map/ppermute | solution.py:513
  31.6 13.5 %collective-permute-start.3 = (bf16[528,256]{1,0:T(8,128)(2,1)S(1)}, bf16[528,256]{1,0:T(8,128)(2,1)S(1)}, u32[]{:S(2)}, u32[]{:S(2)}) collective-permute-start(bf16[528,256]{1,0:T(8,128)(2,1)S(1)} %collective-permute-done.2.refs_1_), channel_id=1, source_target_pairs={{4,8},{5,9},{6,10},{7,11},{8,4},{9,5},{10,6},{11,7},{12,16},{13,17... | collective-permute-start | bytes 811016 | tf_op jit(solution)/shard_map/ppermute | solution.py:531
  32.3 12.8 %collective-permute-start.4 = (bf16[528,256]{1,0:T(8,128)(2,1)S(1)}, bf16[528,256]{1,0:T(8,128)(2,1)S(1)}, u32[]{:S(2)}, u32[]{:S(2)}) collective-permute-start(bf16[528,256]{1,0:T(8,128)(2,1)S(1)} %collective-permute-done.2.refs_1_), channel_id=1, source_target_pairs={{0,4},{1,5},{2,6},{3,7},{4,0},{5,1},{6,2},{7,3},{8,12},{9,13},{10,... | collective-permute-start | bytes 811016 | tf_op jit(solution)/shard_map/ppermute | solution.py:531
  35.2 1.4 %copy-start.1 = (bf16[384,2048]{1,0:T(8,128)(2,1)S(1)}, bf16[384,2048]{1,0:T(8,128)(2,1)}, u32[]{:S(2)}) copy-start(bf16[384,2048]{1,0:T(8,128)(2,1)} %copy-done) | copy-start | bytes 4718596
  39.3 8.6 %copy-start.2 = (bf16[528,256]{1,0:T(8,128)(2,1)S(1)}, bf16[528,256]{1,0:T(8,128)(2,1)}, u32[]{:S(2)}) copy-start(bf16[528,256]{1,0:T(8,128)(2,1)} %prepare.1.refs_0_) | copy-start | bytes 811012
  39.3 8.6 %copy-start.4 = (bf16[1024,2,128]{2,1,0:T(2,128)(2,1)S(1)}, bf16[1024,2,128]{2,1,0:T(2,128)(2,1)}, u32[]{:S(2)}) copy-start(bf16[1024,2,128]{2,1,0:T(2,128)(2,1)} %receive_ref.1) | copy-start | bytes 1572868
  39.3 12.5 %collective-permute-start.9 = (bf16[528,256]{1,0:T(8,128)(2,1)S(1)}, bf16[528,256]{1,0:T(8,128)(2,1)S(1)}, u32[]{:S(2)}, u32[]{:S(2)}) collective-permute-start(bf16[528,256]{1,0:T(8,128)(2,1)S(1)} %collective-permute-done.5.refs_2_), channel_id=1, source_target_pairs={{0,4},{1,5},{4,8},{5,9},{6,2},{7,3},{8,12},{9,13},{10,6},{11,7},{1... | collective-permute-start | bytes 811016 | tf_op jit(solution)/shard_map/ppermute | solution.py:531
  41.4 10.4 %collective-permute-start.10 = (bf16[528,256]{1,0:T(8,128)(2,1)S(1)}, bf16[528,256]{1,0:T(8,128)(2,1)S(1)}, u32[]{:S(2)}, u32[]{:S(2)}) collective-permute-start(bf16[528,256]{1,0:T(8,128)(2,1)S(1)} %collective-permute-done.6.refs_3_), channel_id=1, source_target_pairs={{0,4},{1,5},{4,8},{5,9},{6,2},{7,3},{8,12},{9,13},{10,6},{11,7},{1... | collective-permute-start | bytes 811016 | tf_op jit(solution)/shard_map/ppermute | solution.py:531
  51.8 5.7 %copy-start.8 = (s32[8]{0:T(128)S(1)}, s32[8]{0:T(128)}, u32[]{:S(2)}) copy-start(s32[8]{0:T(128)} %live_ref.1) | copy-start | bytes 100
  56.2 8.3 %collective-permute-start.11 = (bf16[8,64,256]{2,1,0:T(8,128)(2,1)S(1)}, bf16[8,64,256]{2,1,0:T(8,128)(2,1)S(1)}, u32[]{:S(2)}, u32[]{:S(2)}) collective-permute-start(bf16[8,64,256]{2,1,0:T(8,128)(2,1)S(1)} %get-tuple-element.22), channel_id=1, source_target_pairs={{0,1},{1,0},{2,3},{3,2},{4,5},{5,4},{6,7},{7,6},{8,9},{9,8},{10,11... | collective-permute-start | bytes 786440 | tf_op jit(solution)/shard_map/ppermute | solution.py:513
